TPU v7x, 32 devices: a whole 2x2x4 slice. The times are simulated.
32 devices in a mesh: group: 8 (over z, x), space: 4 (over y, core).
Axes of the slice: x: 2, y: 2, z: 4, core: 2. Of those that a mesh axis runs over, the one named last changes fastest.
Arguments:
- latent: bfloat16 [16384, 128], P(('group', 'space')), may hold values from -6 to 6
- owner_ids: int32 [16384, 1], P(('group', 'space')), may hold values from 0 to 7; in each aligned block of 512 rows (0 to 511, 512 to 1023, ...) at most 160 rows name the same one
- tile_recv: int32 [2048], P(('group', 'space')), may hold values from 0 to 3
- tile_send: int32 [2048], P(('group', 'space')), may hold values from 0 to 15
- kernels: bfloat16 [2048, 128, 128], P(('group', 'space')), may hold values from -0.125 to 0.125
- w_msg: bfloat16 [128, 128], replicated, may hold values from -0.5 to 0.5
- w_node: bfloat16 [256, 128], replicated, may hold values from -0.375 to 0.375
- upstream: bfloat16 [40960, 128], P(('group', 'space')), may hold values from -6 to 6
Outputs:
- updated: bfloat16 [40960, 128], P(('group', 'space'))
- latent_grad: bfloat16 [16384, 128], P(('group', 'space'))
- grad_msg: float32 [128, 128], replicated
- grad_node: float32 [256, 128], replicated
Inputs may be any that keep to these rules, and one draw needn't show every extreme that they name: `owner_ids`: in the particles of one device no owner is named more than 160 times; in some devices one owner is named exactly 160 times.
All inputs are finite; a program needn't handle non-finite values.
Results may differ from a plain program's by a relative error of at most 0.022.
Values may be sent and summed in bfloat16 or wider, within the bound.
No kernel may reach another device: no remote copies, remote signals or barrier semaphores. Data moves between devices by JAX's collectives and lax.ppermute only.
A program may use at most 64 MiB of HBM per device.

v0:
```python
import jax
import jax.numpy as jnp
from jax import lax
from jax.sharding import PartitionSpec as P


def silu_slope(value):
    sigmoid_val = jax.nn.sigmoid(value)
    return sigmoid_val * (1.0 + value * (1.0 - sigmoid_val))


def contract_rows(left, right):
    return lax.dot_general(
        left, right, (((0,), (0,)), ((), ())), preferred_element_type=jnp.float32
    )


def times_transposed(left, right):
    return lax.dot_general(
        left, right, (((1,), (1,)), ((), ())), preferred_element_type=jnp.float32
    )


def with_zeros(rows):
    return jnp.concatenate([rows.astype(jnp.float32), jnp.zeros(rows.shape, jnp.float32)], axis=1)


def body(latent, owner_ids, tile_recv, tile_send, kernels, w_msg, w_node, upstream):
    node_count, width = latent.shape
    tile_rows = kernels.shape[1]
    groups = lax.axis_size("group")
    slot_count = upstream.shape[0]
    capacity = slot_count // groups
    preact = jnp.dot(latent, w_msg, preferred_element_type=jnp.float32)
    message = jax.nn.silu(preact).astype(jnp.bfloat16)
    ghost_table = lax.all_gather(message, "space", axis=0, tiled=True)
    table_blocks = ghost_table.reshape(-1, tile_rows, width)
    senders = table_blocks[tile_send]
    products = jnp.einsum("tij,tjh->tih", kernels, senders, preferred_element_type=jnp.float32)
    summed = (
        jnp.zeros((node_count // tile_rows, tile_rows, width), jnp.float32)
        .at[tile_recv]
        .add(products)
    )
    aggregate = summed.reshape(node_count, width).astype(jnp.bfloat16)
    owner_col = owner_ids[:, 0]
    onehot = (owner_col[:, None] == jnp.arange(groups, dtype=jnp.int32)[None, :]).astype(jnp.int32)
    slot_rank = jnp.sum((jnp.cumsum(onehot, axis=0) - onehot) * onehot, axis=1)
    slot_index = owner_col * capacity + slot_rank
    joined = jnp.concatenate([latent, aggregate], axis=1)
    mixed = jnp.dot(joined, w_node, preferred_element_type=jnp.float32)
    new_rows = (latent.astype(jnp.float32) + jax.nn.silu(mixed)).astype(jnp.bfloat16)
    outgoing = jnp.zeros((slot_count, width), jnp.bfloat16).at[slot_index].set(new_rows)
    updated = lax.all_to_all(
        outgoing.reshape(groups, capacity, width), "group", split_axis=0, concat_axis=0, tiled=True
    )
    updated = updated.reshape(slot_count, width)
    returned = lax.all_to_all(
        upstream.reshape(groups, capacity, width), "group", split_axis=0, concat_axis=0, tiled=True
    )
    incoming = returned.reshape(slot_count, width)[slot_index]
    slope = (incoming.astype(jnp.float32) * silu_slope(mixed)).astype(jnp.bfloat16)
    grad_node = contract_rows(joined, slope)
    row_grad = (times_transposed(slope, w_node) + with_zeros(incoming)).astype(jnp.bfloat16)
    direct = row_grad[:, :width]
    agg_blocks = row_grad[:, width:].reshape(-1, tile_rows, width)[tile_recv]
    spread = jnp.einsum("tij,tih->tjh", kernels, agg_blocks, preferred_element_type=jnp.float32)
    table_grad = jnp.zeros(table_blocks.shape, jnp.float32).at[tile_send].add(spread)
    message_grad = lax.psum_scatter(
        table_grad.reshape(-1, width).astype(jnp.bfloat16), "space", scatter_dimension=0, tiled=True
    ).astype(jnp.float32)
    preact_grad = (message_grad * silu_slope(preact)).astype(jnp.bfloat16)
    grad_msg = contract_rows(latent, preact_grad)
    latent_grad = (times_transposed(preact_grad, w_msg) + direct.astype(jnp.float32)).astype(
        jnp.bfloat16
    )
    grad_msg, grad_node = lax.psum((grad_msg, grad_node), ("group", "space"))
    return (updated, latent_grad, grad_msg, grad_node)


def solution(mesh):
    return jax.shard_map(
        body,
        mesh=mesh,
        in_specs=(
            P(("group", "space"), None),
            P(("group", "space"), None),
            P(("group", "space")),
            P(("group", "space")),
            P(("group", "space"), None, None),
            P(),
            P(),
            P(("group", "space"), None),
        ),
        out_specs=(P(("group", "space"), None), P(("group", "space"), None), P(), P()),
        check_vma=False,
    )
```

profile of v0, /device:TPU:0, one launch (start us, length us, event | category | flops | bytes accessed | tf_op | source)
XLA Modules:
  0.0 234.9 jit_solution(10526379765851607014)
XLA Ops:
  7.2 7.4 %all-to-all-start.1 = ((bf16[8,160,128]{2,1,0:T(8,128)(2,1)}), bf16[8,160,128]{2,1,0:T(8,128)(2,1)S(1)}, u32[]{:S(2)}, u32[]{:S(2)}) async-start(bf16[8,160,128]{2,1,0:T(8,128)(2,1)} %bitcast.46), calls=%async_computation.1 | async-start | bytes 655360 | tf_op jit(solution)/shard_map/all_to_all | solution.py:58
  14.7 1.8 multiply_convert_fusion.2
  16.4 7.2 %all_gather.3 = bf16[2048,128]{1,0:T(8,128)(2,1)S(1)} all-gather(bf16[512,128]{1,0:T(8,128)(2,1)S(1)} %get-tuple-element.14), channel_id=1, replica_groups=mesh['group'=8,'space'=4] {'space'}, dimensions={0}, use_global_device_ids=true | all-gather | bytes 655360 | tf_op jit(solution)/shard_map/all_gather | solution.py:36
  23.7 1.1 reduce-window.6
  24.8 0.2 slice_reduce_fusion
  25.1 2.2 gather_fusion
  27.2 5.1 %convolution_bitcast_fusion.1 = f32[64,128,128]{1,2,0:T(8,128)} fusion(bf16[64,128,128]{2,1,0:T(8,128)(2,1)} %gather_fusion, bf16[64,128,128]{2,1,0:T(8,128)(2,1)S(1)} %copy-done), kind=kOutput, calls=%fused_computation.7 | convolution fusion | flops 268435456 | bytes 8388608 | tf_op jit(solution)/shard_map/tij,tjh->tih/dot_general | solution.py:39
  32.4 0.1 fusion.7
  32.5 5.6 %copy.16 = f32[64,128,128]{2,1,0:T(8,128)} copy(f32[64,128,128]{1,2,0:T(8,128)} %convolution_bitcast_fusion.1) | data formatting | bytes 8388608 | tf_op jit(solution)/shard_map/tij,tjh->tih/dot_general | solution.py:39
  38.1 8.8 %scatter_fusion = f32[4,128,128]{2,1,0:T(8,128)S(1)} fusion(f32[4,128,128]{2,1,0:T(8,128)S(1)} %broadcast_in_dim.22, s32[64]{0:T(128)S(1)} %compare_select_fusion.2, f32[64,128,128]{2,1,0:T(8,128)} %copy.16), kind=kCustom, calls=%fused_computation.3 | custom fusion | flops 1048576 | bytes 12583168 | tf_op jit(solution)/shard_map/scatter-add | solution.py:43
  47.0 0.2 fusion.3
  47.2 0.4 copy-done.3
  47.6 1.3 gather_fusion.1
  49.0 0.3 fusion
  49.3 2.1 gather_fusion.2
  51.4 4.4 %convolution_bitcast_fusion = f32[64,128,128]{1,2,0:T(8,128)} fusion(bf16[64,128,128]{2,1,0:T(8,128)(2,1)} %gather_fusion.2, bf16[64,128,128]{2,1,0:T(8,128)(2,1)S(1)} %copy-done), kind=kOutput, calls=%fused_computation.6 | convolution fusion | flops 268435456 | bytes 8388608 | tf_op jit(solution)/shard_map/tij,tih->tjh/dot_general | solution.py:67
  55.8 5.6 %copy.18 = f32[64,128,128]{2,1,0:T(8,128)} copy(f32[64,128,128]{1,2,0:T(8,128)} %convolution_bitcast_fusion) | data formatting | bytes 8388608 | tf_op jit(solution)/shard_map/tij,tih->tjh/dot_general | solution.py:67
  61.4 0.1 broadcast_in_dim.25
  61.5 8.8 %scatter_fusion.1 = f32[16,128,128]{2,1,0:T(8,128)S(1)} fusion(f32[16,128,128]{2,1,0:T(8,128)S(1)} %broadcast_in_dim.25, s32[64]{0:T(128)S(1)} %compare_select_fusion.1, f32[64,128,128]{2,1,0:T(8,128)} %copy.18), kind=kCustom, calls=%fused_computation.5 | custom fusion | flops 1048576 | bytes 12583168 | tf_op jit(solution)/shard_map/scatter-add | solution.py:68
  70.3 0.9 convert_element_type.60
  71.2 0.0 all-reduce.4.cloned.1.call-start
  71.3 1.9 scatter_custom_fusion.1
  73.2 17.2 %all_to_all.10 = bf16[8,160,128]{2,1,0:T(8,128)(2,1)S(1)} all-to-all(bf16[8,160,128]{2,1,0:T(8,128)(2,1)S(1)} %bitcast.43), channel_id=1, replica_groups=mesh['group'=8,'space'=4] {'group'}, dimensions={0} | all-to-all | bytes 655360 | tf_op jit(solution)/shard_map/all_to_all | solution.py:54
  90.4 1.9 fusion.2
  92.3 1.5 reduce-scatter.2.cloned.1.call-done
  93.8 1.0 multiply_convert_fusion
  94.8 0.9 convolution_bitcast_fusion.2
  95.7 1.7 fusion.1
  97.4 126.8 %all-reduce.4.cloned.1.call-done = (f32[128,128]{0,1:T(8,128)}, f32[256,128]{1,0:T(8,128)}) async-done(((f32[128,128]{0,1:T(8,128)}, f32[256,128]{1,0:T(8,128)}), (f32[128,128]{0,1:T(8,128)}, f32[256,128]{1,0:T(8,128)})) %all-reduce.4.cloned.1.call-update) | async-done | bytes 196624 | tf_op jit(solution)/shard_map/psum | solution.py:77
  224.2 1.6 copy.19
  225.8 0.7 copy.27
  226.5 1.6 copy.28
  (38 shorter events, 0.3 us)
Async XLA Ops:
  7.2 20.1 %copy-start = (bf16[64,128,128]{2,1,0:T(8,128)(2,1)S(1)}, bf16[64,128,128]{2,1,0:T(8,128)(2,1)}, u32[]{:S(2)}) copy-start(bf16[64,128,128]{2,1,0:T(8,128)(2,1)} %param.12) | copy-start | bytes 6291460
  7.2 16.4 %copy-start.9 = (s32[64]{0:T(128)S(1)}, s32[64]{0:T(128)}, u32[]{:S(2)}) copy-start(s32[64]{0:T(128)} %param.11) | copy-start | bytes 772
  7.2 16.4 %copy-start.10 = (s32[64]{0:T(128)S(1)}, s32[64]{0:T(128)}, u32[]{:S(2)}) copy-start(s32[64]{0:T(128)} %param.10) | copy-start | bytes 772
  7.2 16.5 %copy-start.8 = (s32[512,1]{0,1:T(1,128)S(1)}, s32[512,1]{0,1:T(1,128)}, u32[]{:S(2)}) copy-start(s32[512,1]{0,1:T(1,128)} %param.9) | copy-start | bytes 6148
  7.2 40.0 %all-to-all-start.1 = ((bf16[8,160,128]{2,1,0:T(8,128)(2,1)}), bf16[8,160,128]{2,1,0:T(8,128)(2,1)S(1)}, u32[]{:S(2)}, u32[]{:S(2)}) async-start(bf16[8,160,128]{2,1,0:T(8,128)(2,1)} %bitcast.46), calls=%async_computation.1 | async-start | bytes 655360 | tf_op jit(solution)/shard_map/all_to_all | solution.py:58
  14.6 79.1 %reduce-scatter.2.cloned.1.call-start = ((), (), s32[]{:S(2)}) async-start(), calls=%async_computation.3 | async-start | bytes 655360 | tf_op jit(solution)/shard_map/reduce_scatter | solution.py:69
  38.1 8.9 %copy-start.1 = (bf16[512,128]{1,0:T(8,128)(2,1)S(1)}, bf16[512,128]{1,0:T(8,128)(2,1)}, u32[]{:S(2)}) copy-start(bf16[512,128]{1,0:T(8,128)(2,1)} %param.8) | copy-start | bytes 393220
  38.1 8.9 %copy-start.6 = (bf16[256,128]{1,0:T(8,128)(2,1)S(1)}, bf16[256,128]{1,0:T(8,128)(2,1)}, u32[]{:S(2)}) copy-start(bf16[256,128]{1,0:T(8,128)(2,1)} %param.14) | copy-start | bytes 196612
  46.9 0.7 copy-start.3
  48.9 2.5 %copy-start.2 = (bf16[512,128]{1,0:T(8,128)(2,1)}, bf16[512,128]{1,0:T(8,128)(2,1)S(1)}, u32[]{:S(2)}) copy-start(bf16[512,128]{1,0:T(8,128)(2,1)S(1)} %gather_fusion.1) | copy-start | bytes 393220
  49.2 2.2 copy-start.5
  71.2 22.6 %copy-start.4 = (f32[512,128]{1,0:T(8,128)S(1)}, f32[512,128]{1,0:T(8,128)}, u32[]{:S(2)}) copy-start(f32[512,128]{1,0:T(8,128)} %get-tuple-element.15) | copy-start | bytes 786436
  71.2 24.5 %copy-start.7 = (bf16[128,128]{1,0:T(8,128)(2,1)S(1)}, bf16[128,128]{1,0:T(8,128)(2,1)}, u32[]{:S(2)}) copy-start(bf16[128,128]{1,0:T(8,128)(2,1)} %param.13) | copy-start | bytes 98308
  71.2 153.0 %all-reduce.4.cloned.1.call-start = ((), (), s32[]{:S(2)}) async-start(), calls=%async_computation.4 | async-start | bytes 393216 | tf_op jit(solution)/shard_map/psum | solution.py:77
Sparse Core Ops, SparseCore 0:
  71.3 22.3 reduce-scatter.1
  100.9 123.3 all-reduce.3
where the time goes:
time: 236 us; the launch traced here: 235 us
  waiting for transfers between devices  128 us (54%)
  blocking collectives  24.4 us (10%)
  other arithmetic  22.7 us (10%)
  local copies, waits for them, and re-layouts  21.5 us (9%)
  matrix products  16.3 us (7%)
  between operations  14.3 us (6%)
  starting transfers between devices  7.47 us (3%)
    psum x1, waiting for transfers between devices, body(): grad_msg, grad_node = lax.psum((grad_msg, grad_node), ('group', 'space'))  127 us
    all_to_all x1, blocking collectives, body(): lax.all_to_all(outgoing.reshape(groups, capacity, width), 'group', split_...  17.2 us
    scatter-add x1, other arithmetic, body(): jnp.zeros(table_blocks.shape, jnp.float32).at[tile_send].add(spread)  8.79 us
    scatter-add x1, other arithmetic, body(): summed = jnp.zeros((node_count // tile_rows, tile_rows, width), jnp.float...  8.78 us
    all_to_all x1, starting transfers between devices, body(): lax.all_to_all(upstream.reshape(groups, capacity, width), 'group', split_...  7.4 us
    all_gather x1, blocking collectives, body(): ghost_table = lax.all_gather(message, 'space', axis=0, tiled=True)  7.18 us
    dot_general x1, local copies, waits for them, and re-layouts, body(): jnp.einsum('tij,tjh->tih', kernels, senders, preferred_element_type=jnp.f...  5.61 us
    dot_general x1, local copies, waits for them, and re-layouts, body(): jnp.einsum('tij,tih->tjh', kernels, agg_blocks, preferred_element_type=jn...  5.6 us
  transfers between devices with their start and end apart: 3, of which 2 were waited for; matrix products, arithmetic and copies ran while one was open for 13% of the time, Pallas kernels for 0%

commit v1 on v0

v1 whole, which is shorter than its diff:
```python
import jax
import jax.numpy as jnp
from jax import lax
from jax.experimental import pallas as pl
from jax.experimental.pallas import tpu as pltpu
from jax.sharding import PartitionSpec as P

BF = jnp.bfloat16
F32 = jnp.float32


def mm(left, right):
    return jnp.dot(left, right, preferred_element_type=F32)


def mm_nt(left, right):
    return lax.dot_general(left, right, (((1,), (1,)), ((), ())), preferred_element_type=F32)


def sigmoid(value):
    return 0.5 * jnp.tanh(0.5 * value) + 0.5


def slope_of(value):
    sig = sigmoid(value)
    return sig * (1.0 + value * (1.0 - sig))


def make_layer(node_count, width, rows, tiles, groups, spaces, capacity):
    blocks = node_count // rows
    slots = groups * capacity
    group_rows = max(16, -(-groups // 16) * 16)

    def kernel(recv, send, owner, table, own_latent, kernels, w_msg, w_node, returned, *rest):
        outgoing = rest[0]
        parts = rest[1 : 1 + spaces]
        grads, direct_out = rest[1 + spaces : 3 + spaces]
        msg, acc, spread, place, place_t = rest[3 + spaces :]
        me = lax.axis_index("space")

        owner_row = owner[...]
        hot = (
            lax.broadcasted_iota(jnp.int32, (group_rows, node_count), 0) == owner_row
        ).astype(F32)
        before = (
            lax.broadcasted_iota(jnp.int32, (node_count, node_count), 0)
            < lax.broadcasted_iota(jnp.int32, (node_count, node_count), 1)
        ).astype(F32)
        counts = mm(hot.astype(BF), before.astype(BF))
        rank = jnp.sum(counts * hot, axis=0, keepdims=True)
        slot = owner_row.astype(F32) * capacity + rank
        slot_col = jnp.transpose(jnp.broadcast_to(slot, (width, node_count)))
        slot_int = slot.astype(jnp.int32)
        slot_col = slot_col.astype(jnp.int32)
        for at in range(0, slots, 128):
            down = lax.broadcasted_iota(jnp.int32, (128, node_count), 0) + at
            place[at : at + 128, :] = (down == slot_int).astype(F32).astype(BF)
            across = lax.broadcasted_iota(jnp.int32, (node_count, 128), 1) + at
            place_t[:, at : at + 128] = (across == slot_col).astype(F32).astype(BF)

        for part in range(spaces):
            preact = mm(table[part * node_count : (part + 1) * node_count, :], w_msg[...])
            value = (preact * sigmoid(preact)).astype(BF)
            for block in range(blocks):
                msg[part * blocks + block] = value[block * rows : (block + 1) * rows, :]

        acc[...] = jnp.zeros_like(acc)

        def gather_tile(t, carry):
            r = recv[t]
            acc[r] = acc[r] + mm(kernels[t], msg[send[t]])
            return carry

        lax.fori_loop(0, tiles, gather_tile, 0, unroll=8)
        aggregate = acc[...].reshape(node_count, width).astype(BF)
        latent = own_latent[...]
        joined = jnp.concatenate([latent, aggregate], axis=1)
        mixed = mm(joined, w_node[...])
        sig = sigmoid(mixed)
        new_rows = (latent.astype(F32) + mixed * sig).astype(BF)
        outgoing[...] = mm(place[...], new_rows).astype(BF)

        incoming = mm(place_t[...], returned[...])
        slope = incoming * (sig * (1.0 + mixed * (1.0 - sig)))
        slope_t = jnp.transpose(slope).astype(BF)
        slope = slope.astype(BF)
        grads[width : 3 * width, :] = jnp.transpose(mm(slope_t, joined)).astype(BF)
        direct_out[...] = (mm_nt(slope, w_node[0:width, :]) + incoming).astype(BF)
        back_t = mm(w_node[width : 2 * width, :], slope_t).astype(BF)
        for block in range(blocks):
            acc[block] = back_t[:, block * rows : (block + 1) * rows].astype(F32)

        spread[...] = jnp.zeros_like(spread)

        def spread_tile(t, carry):
            s = send[t]
            spread[s] = spread[s] + mm(acc[recv[t]].astype(BF), kernels[t])
            return carry

        lax.fori_loop(0, tiles, spread_tile, 0, unroll=8)

        w_msg_t = jnp.transpose(w_msg[...].astype(F32)).astype(BF)
        grad_msg = jnp.zeros((width, width), F32)
        for part in range(spaces):
            target = lax.rem(me + part, spaces)
            lat = table[pl.ds(pl.multiple_of(target * node_count, node_count), node_count), :]
            preact_t = mm_nt(w_msg_t, lat)
            total = jnp.concatenate(
                [spread[target * blocks + block] for block in range(blocks)], axis=1
            )
            preact_grad = (total * slope_of(preact_t)).astype(BF)
            grad_msg += mm(preact_grad, lat)
            parts[part][...] = mm(w_msg[...], preact_grad).astype(BF)
        grads[0:width, :] = jnp.transpose(grad_msg).astype(BF)

    vmem = pl.BlockSpec(memory_space=pltpu.VMEM)
    smem = pl.BlockSpec(memory_space=pltpu.SMEM)
    return pl.pallas_call(
        kernel,
        out_shape=(
            jax.ShapeDtypeStruct((slots, width), BF),
            *[jax.ShapeDtypeStruct((width, node_count), BF)] * spaces,
            jax.ShapeDtypeStruct((3 * width, width), BF),
            jax.ShapeDtypeStruct((node_count, width), BF),
        ),
        in_specs=[smem, smem] + [vmem] * 7,
        out_specs=[vmem] * (spaces + 3),
        scratch_shapes=[
            pltpu.VMEM((spaces * blocks, rows, width), BF),
            pltpu.VMEM((blocks, rows, width), F32),
            pltpu.VMEM((spaces * blocks, width, rows), F32),
            pltpu.VMEM((slots, node_count), BF),
            pltpu.VMEM((node_count, slots), BF),
        ],
        compiler_params=pltpu.CompilerParams(vmem_limit_bytes=40 << 20),
        cost_estimate=pl.CostEstimate(
            flops=2_000_000_000, bytes_accessed=4_000_000, transcendentals=600_000
        ),
        name="layer",
    )


def finish_kernel(direct, *rest):
    total = rest[0][...].astype(F32)
    for ref in rest[1:-1]:
        total = total + ref[...].astype(F32)
    rest[-1][...] = (jnp.transpose(total) + direct[...].astype(F32)).astype(BF)


def exchange(value, axes, size, mask):
    return lax.ppermute(value, axes, [(i, i ^ mask) for i in range(size)])


def sum_all(value, axes, size):
    bits = size.bit_length() - 1
    stages = [(0, 1)] + [(at, min(2, bits - at)) for at in range(1, bits, 2)]
    for at, span in stages:
        wide = value.astype(BF)
        got = [exchange(wide, axes, size, step << at) for step in range(1, 1 << span)]
        got = [wide.astype(F32)] + [one.astype(F32) for one in got]
        value = got[0] + got[1]
        if span == 2:
            value = value + (got[2] + got[3])
    return value


def body(latent, owner_ids, tile_recv, tile_send, kernels, w_msg, w_node, upstream):
    node_count, width = latent.shape
    tiles, rows, _ = kernels.shape
    groups, spaces = lax.axis_size("group"), lax.axis_size("space")
    slots = upstream.shape[0]
    capacity = slots // groups

    def swap(value):
        return lax.all_to_all(
            value.reshape(groups, capacity, width), "group", split_axis=0, concat_axis=0, tiled=True
        ).reshape(slots, width)

    returned = swap(upstream)
    table = lax.all_gather(latent, "space", axis=0, tiled=True)
    layer = make_layer(node_count, width, rows, tiles, groups, spaces, capacity)
    outs = layer(
        tile_recv, tile_send, owner_ids.reshape(1, node_count), table, latent, kernels, w_msg,
        w_node, returned,
    )
    outgoing, parts, grads, direct = outs[0], outs[1 : 1 + spaces], outs[-2], outs[-1]
    updated = swap(outgoing)
    got = [
        lax.ppermute(parts[k], "space", [(i, (i + k) % spaces) for i in range(spaces)])
        for k in range(1, spaces)
    ]
    total = sum_all(grads, ("group", "space"), groups * spaces)
    latent_grad = pl.pallas_call(
        finish_kernel, out_shape=jax.ShapeDtypeStruct((node_count, width), BF), name="finish"
    )(direct, parts[0], *got)
    return updated, latent_grad, total[:width], total[width:]


def solution(mesh):
    split = P(("group", "space"))
    wide = P(("group", "space"), None)
    return jax.shard_map(
        body,
        mesh=mesh,
        in_specs=(wide, wide, split, split, P(("group", "space"), None, None), P(), P(), wide),
        out_specs=(wide, wide, P(), P()),
        check_vma=False,
    )
```

time: 236 us -> 63.2 us (0.27)
  waiting for transfers between devices: 128 us -> 12.2 us
  other arithmetic: 22.7 us -> 0.13 us
  blocking collectives: 24.4 us -> 7.4 us
  matrix products: 16.3 us -> 0 us
  starting transfers between devices: 7.47 us -> 21.9 us
  between operations: 14.3 us -> 0.68 us
  local copies, waits for them, and re-layouts: 21.5 us -> 10.1 us
  Pallas kernels: 0 us -> 10.2 us
    psum x1 -> x0, waiting for transfers between devices: 127 us -> none  [body(): grad_msg, grad_node = lax.psum((grad_msg, grad_node), ('group', 'space'))]
    scatter-add x2 -> x0, other arithmetic: 17.6 us -> none  [the longest x1 8.79 us: body(): jnp.zeros(table_blocks.shape, jnp.float32).at[tile_send].add(spread)]
    all_to_all x1 -> x0, blocking collectives: 17.2 us -> none  [body(): lax.all_to_all(outgoing.reshape(groups, capacity, width), 'group', split_...]
    dot_general x8 -> x0, matrix products: 16.3 us -> none  [the longest x1 5.13 us: body(): jnp.einsum('tij,tjh->tih', kernels, senders, preferred_element_type=jnp.f...]
    dot_general x2 -> x0, local copies, waits for them, and re-layouts: 11.2 us -> none  [the longest x1 5.61 us: body(): jnp.einsum('tij,tjh->tih', kernels, senders, preferred_element_type=jnp.f...]
    ppermute x0 -> x10, starting transfers between devices: none -> 11.1 us  [the longest x7 8.08 us: exchange(): return lax.ppermute(value, axes, [(i, i ^ mask) for i in range(size)])]
    pallas_call x0 -> x2, Pallas kernels: none -> 10.2 us  [the longest x1 8.27 us: body(): layer(tile_recv, tile_send, owner_ids.reshape(1, node_count), table, late...]
    ppermute x0 -> x10, waiting for transfers between devices: none -> 9.32 us  [the longest x7 9.27 us: exchange(): return lax.ppermute(value, axes, [(i, i ^ mask) for i in range(size)])]
  transfers between devices with their start and end apart: 3 -> 12, of which waited for: 2 -> 4; matrix products, arithmetic and copies ran while one was open for 13% -> 2% of each run, Pallas kernels for 0% -> 3%
where the time goes in v1:
time: 63.2 us; the launch traced here: 62.7 us
  starting transfers between devices  21.9 us (35%)
  waiting for transfers between devices  12.2 us (19%)
  Pallas kernels  10.2 us (16%)
  local copies, waits for them, and re-layouts  10.1 us (16%)
  blocking collectives  7.4 us (12%)
  between operations  0.68 us (1%)
    all_to_all x2, starting transfers between devices, swap(): lax.all_to_all(value.reshape(groups, capacity, width), 'group', split_axi...  10.9 us
    ppermute x7, waiting for transfers between devices, exchange(): return lax.ppermute(value, axes, [(i, i ^ mask) for i in range(size)])  9.27 us
    unnamed x25, local copies, waits for them, and re-layouts  8.76 us
    pallas_call x1, Pallas kernels, body(): layer(tile_recv, tile_send, owner_ids.reshape(1, node_count), table, late...  8.27 us
    ppermute x7, starting transfers between devices, exchange(): return lax.ppermute(value, axes, [(i, i ^ mask) for i in range(size)])  8.08 us
    all_gather x1, blocking collectives, body(): table = lax.all_gather(latent, 'space', axis=0, tiled=True)  7.4 us
    ppermute x3, starting transfers between devices, body(): lax.ppermute(parts[k], 'space', [(i, (i + k) % spaces) for i in range(spa...  3 us
    all_to_all x2, waiting for transfers between devices, swap(): lax.all_to_all(value.reshape(groups, capacity, width), 'group', split_axi...  2.93 us
  transfers between devices with their start and end apart: 12, of which 4 were waited for; matrix products, arithmetic and copies ran while one was open for 2% of the time, Pallas kernels for 3%

profile of v1, /device:TPU:0, one launch (start us, length us, event | category | flops | bytes accessed | tf_op | source)
XLA Modules:
  0.0 62.7 jit_solution(15800463369609144604)
XLA Ops:
  0.6 7.3 %all-to-all-start = ((bf16[8,160,128]{2,1,0:T(8,128)(2,1)}), bf16[8,160,128]{2,1,0:T(8,128)(2,1)S(1)}, u32[]{:S(2)}, u32[]{:S(2)}) async-start(bf16[8,160,128]{2,1,0:T(8,128)(2,1)} %bitcast.8), calls=%async_computation | async-start | bytes 655360 | tf_op jit(solution)/shard_map/all_to_all | solution.py:175
  7.9 7.4 %all_gather.3.table = bf16[2048,128]{1,0:T(8,128)(2,1)S(1)} all-gather(bf16[512,128]{1,0:T(8,128)(2,1)} %own_latent.1), channel_id=1, replica_groups=mesh['group'=8,'space'=4] {'space'}, dimensions={0}, use_global_device_ids=true | all-gather | bytes 655360 | tf_op jit(solution)/shard_map/all_gather | solution.py:180
  15.3 2.9 %all-to-all-done = bf16[8,160,128]{2,1,0:T(8,128)(2,1)S(1)} async-done(((bf16[8,160,128]{2,1,0:T(8,128)(2,1)}), bf16[8,160,128]{2,1,0:T(8,128)(2,1)S(1)}, u32[]{:S(2)}, u32[]{:S(2)}) %all-to-all-start) | async-done | bytes 327712 | tf_op jit(solution)/shard_map/all_to_all | solution.py:175
  18.2 0.9 %copy-done = bf16[512,128]{1,0:T(8,128)(2,1)S(1)} copy-done((bf16[512,128]{1,0:T(8,128)(2,1)S(1)}, bf16[512,128]{1,0:T(8,128)(2,1)}, u32[]{:S(2)}) %copy-start) | copy-done | bytes 131096
  19.1 1.6 %copy-done.3 = bf16[64,128,128]{2,1,0:T(8,128)(2,1)S(1)} copy-done((bf16[64,128,128]{2,1,0:T(8,128)(2,1)S(1)}, bf16[64,128,128]{2,1,0:T(8,128)(2,1)}, u32[]{:S(2)}) %copy-start.3) | copy-done | bytes 2097176
  20.7 0.8 %copy-done.4 = bf16[256,128]{1,0:T(8,128)(2,1)S(1)} copy-done((bf16[256,128]{1,0:T(8,128)(2,1)S(1)}, bf16[256,128]{1,0:T(8,128)(2,1)}, u32[]{:S(2)}) %copy-start.4) | copy-done | bytes 65560
  21.6 0.8 %copy-done.5 = bf16[128,128]{1,0:T(8,128)(2,1)S(1)} copy-done((bf16[128,128]{1,0:T(8,128)(2,1)S(1)}, bf16[128,128]{1,0:T(8,128)(2,1)}, u32[]{:S(2)}) %copy-start.5) | copy-done | bytes 32792
  22.3 0.7 %copy-done.6 = s32[512,1]{0,1:T(1,128)S(1)} copy-done((s32[512,1]{0,1:T(1,128)S(1)}, s32[512,1]{0,1:T(1,128)}, u32[]{:S(2)}) %copy-start.6) | copy-done | bytes 2072
  23.0 0.7 %copy-done.7 = s32[64]{0:T(128)S(1)} copy-done((s32[64]{0:T(128)S(1)}, s32[64]{0:T(128)}, u32[]{:S(2)}) %copy-start.7) | copy-done | bytes 280
  23.7 0.7 %copy-done.8 = s32[64]{0:T(128)S(1)} copy-done((s32[64]{0:T(128)S(1)}, s32[64]{0:T(128)}, u32[]{:S(2)}) %copy-start.8) | copy-done | bytes 280
  24.3 8.3 %layer.1 = (bf16[1280,128]{1,0:T(8,128)(2,1)}, bf16[128,512]{1,0:T(8,128)(2,1)S(1)}, bf16[128,512]{1,0:T(8,128)(2,1)S(1)}, bf16[128,512]{1,0:T(8,128)(2,1)S(1)},...) custom-call(s32[64]{0:T(128)S(1)} %copy-done.7, s32[64]{0:T(128)S(1)} %copy-done.8, ...), custom_call_target="tpu_custom_call" | custom-call | flops 2000000000 | bytes 4000000 | tf_op jit(solution)/shard_map/layer/pallas_call | solution.py:182
  32.6 0.7 %copy-done.1 = bf16[128,512]{1,0:T(8,128)(2,1)} copy-done((bf16[128,512]{1,0:T(8,128)(2,1)}, bf16[128,512]{1,0:T(8,128)(2,1)S(1)}, u32[]{:S(2)}) %copy-start.1) | copy-done | bytes 131096
  33.2 0.7 %copy-done.2 = bf16[512,128]{1,0:T(8,128)(2,1)} copy-done((bf16[512,128]{1,0:T(8,128)(2,1)}, bf16[512,128]{1,0:T(8,128)(2,1)S(1)}, u32[]{:S(2)}) %copy-start.2) | copy-done | bytes 131096
  33.9 1.3 %collective-permute-done.3 = bf16[384,128]{1,0:T(8,128)(2,1)S(1)} collective-permute-done((bf16[384,128]{1,0:T(8,128)(2,1)S(1)}, bf16[384,128]{1,0:T(8,128)(2,1)S(1)}, u32[]{:S(2)}, u32[]{:S(2)}) %collective-permute-start.3) | collective-permute-done | bytes 98336 | tf_op jit(solution)/shard_map/ppermute | solution.py:151
  35.2 2.4 %collective-permute-start.6 = (bf16[384,128]{1,0:T(8,128)(2,1)S(1)}, bf16[384,128]{1,0:T(8,128)(2,1)S(1)}, u32[]{:S(2)}, u32[]{:S(2)}) collective-permute-start(bf16[384,128]{1,0:T(8,128)(2,1)S(1)} %add_convert_fusion.1), channel_id=1, source_target_pairs={{0,6},{1,7},{2,4},{3,5},{4,2},{5,3},{6,0},{7,1},{8,14},{9,15},{10,... | collective-permute-start | bytes 294920 | tf_op jit(solution)/shard_map/ppermute | solution.py:151
  37.7 0.6 collective-permute-start.5
  38.3 0.5 collective-permute-start.4
  38.8 3.6 %all-to-all-start.1 = ((bf16[8,160,128]{2,1,0:T(8,128)(2,1)}), bf16[8,160,128]{2,1,0:T(8,128)(2,1)S(1)}, u32[]{:S(2)}, u32[]{:S(2)}) async-start(bf16[8,160,128]{2,1,0:T(8,128)(2,1)} %bitcast.3), calls=%async_computation.1 | async-start | bytes 655360 | tf_op jit(solution)/shard_map/all_to_all | solution.py:175
  42.4 1.6 %collective-permute-start.1 = (bf16[128,512]{1,0:T(8,128)(2,1)S(1)}, bf16[128,512]{1,0:T(8,128)(2,1)S(1)}, u32[]{:S(2)}, u32[]{:S(2)}) collective-permute-start(bf16[128,512]{1,0:T(8,128)(2,1)S(1)} %get-tuple-element.15), channel_id=1, source_target_pairs={{0,2},{1,3},{2,0},{3,1},{4,6},{5,7},{6,4},{7,5},{8,10},{9,11},{10,... | collective-permute-start | bytes 393224 | tf_op jit(solution)/shard_map/ppermute | solution.py:189
  44.0 1.4 %collective-permute-start.2 = (bf16[128,512]{1,0:T(8,128)(2,1)S(1)}, bf16[128,512]{1,0:T(8,128)(2,1)S(1)}, u32[]{:S(2)}, u32[]{:S(2)}) collective-permute-start(bf16[128,512]{1,0:T(8,128)(2,1)S(1)} %get-tuple-element.16), channel_id=1, source_target_pairs={{0,3},{1,0},{2,1},{3,2},{4,7},{5,4},{6,5},{7,6},{8,11},{9,8},{10,9... | collective-permute-start | bytes 393224 | tf_op jit(solution)/shard_map/ppermute | solution.py:189
  45.4 0.1 add_convert_fusion
  45.4 3.9 %collective-permute-start.9 = (bf16[384,128]{1,0:T(8,128)(2,1)S(1)}, bf16[384,128]{1,0:T(8,128)(2,1)S(1)}, u32[]{:S(2)}, u32[]{:S(2)}) collective-permute-start(bf16[384,128]{1,0:T(8,128)(2,1)S(1)} %add_convert_fusion), channel_id=1, source_target_pairs={{0,24},{1,25},{2,26},{3,27},{4,28},{5,29},{6,30},{7,31},{8,16},{9,... | collective-permute-start | bytes 294920 | tf_op jit(solution)/shard_map/ppermute | solution.py:151
  49.3 0.6 %collective-permute-start.7 = (bf16[384,128]{1,0:T(8,128)(2,1)S(1)}, bf16[384,128]{1,0:T(8,128)(2,1)S(1)}, u32[]{:S(2)}, u32[]{:S(2)}) collective-permute-start(bf16[384,128]{1,0:T(8,128)(2,1)S(1)} %add_convert_fusion), channel_id=1, source_target_pairs={{0,8},{1,9},{2,10},{3,11},{4,12},{5,13},{6,14},{7,15},{8,0},{9,1},... | collective-permute-start | bytes 294920 | tf_op jit(solution)/shard_map/ppermute | solution.py:151
  50.0 0.0 collective-permute-done.2.rest_3_
  50.0 0.6 copy-done.10
  50.6 0.1 copy-done.11
  50.7 2.0 %finish.1 = bf16[512,128]{1,0:T(8,128)(2,1)} custom-call(bf16[512,128]{1,0:T(8,128)(2,1)} %copy-done.2, bf16[128,512]{1,0:T(8,128)(2,1)} %copy-done.1, bf16[128,512]{1,0:T(8,128)(2,1)} %copy-done.9, bf16[128,512]{1,0:T(8,128)(2,1)} %copy-done.10, bf16[128,512]{1,0:T(8,128)(2,1)} %copy-done.11), custom_call_target="tpu_custom_call" | custom-call | tf_op jit(solution)/shard_map/finish/pallas_call | solution.py:193
  52.6 2.7 %collective-permute-done.9 = bf16[384,128]{1,0:T(8,128)(2,1)S(1)} collective-permute-done((bf16[384,128]{1,0:T(8,128)(2,1)S(1)}, bf16[384,128]{1,0:T(8,128)(2,1)S(1)}, u32[]{:S(2)}, u32[]{:S(2)}) %collective-permute-start.9) | collective-permute-done | bytes 98336 | tf_op jit(solution)/shard_map/ppermute | solution.py:151
  55.4 5.2 %collective-permute-done.8 = bf16[384,128]{1,0:T(8,128)(2,1)S(1)} collective-permute-done((bf16[384,128]{1,0:T(8,128)(2,1)S(1)}, bf16[384,128]{1,0:T(8,128)(2,1)S(1)}, u32[]{:S(2)}, u32[]{:S(2)}) %collective-permute-start.8) | collective-permute-done | bytes 98336 | tf_op jit(solution)/shard_map/ppermute | solution.py:151
  60.7 0.6 %slice.8 = f32[128,128]{1,0:T(8,128)} slice(f32[384,128]{1,0:T(8,128)S(1)} %add_add_fusion), slice={[0:128], [0:128]} | slice | bytes 131072 | tf_op jit(solution)/shard_map/slice | solution.py:196
  61.3 0.7 %slice.9 = f32[256,128]{1,0:T(8,128)} slice(f32[384,128]{1,0:T(8,128)S(1)} %add_add_fusion), slice={[128:384], [0:128]} | slice | bytes 262144 | tf_op jit(solution)/shard_map/slice | solution.py:196
  62.0 0.7 %copy.13 = bf16[1280,128]{1,0:T(8,128)(2,1)} copy(bf16[1280,128]{1,0:T(8,128)(2,1)S(1)} %bitcast.7) | data formatting | bytes 655360
  (25 shorter events, 0.1 us)
Async XLA Ops:
  0.6 17.6 %all-to-all-start = ((bf16[8,160,128]{2,1,0:T(8,128)(2,1)}), bf16[8,160,128]{2,1,0:T(8,128)(2,1)S(1)}, u32[]{:S(2)}, u32[]{:S(2)}) async-start(bf16[8,160,128]{2,1,0:T(8,128)(2,1)} %bitcast.8), calls=%async_computation | async-start | bytes 655360 | tf_op jit(solution)/shard_map/all_to_all | solution.py:175
  18.2 0.9 %copy-start = (bf16[512,128]{1,0:T(8,128)(2,1)S(1)}, bf16[512,128]{1,0:T(8,128)(2,1)}, u32[]{:S(2)}) copy-start(bf16[512,128]{1,0:T(8,128)(2,1)} %own_latent.1) | copy-start | bytes 393220
  19.1 1.6 %copy-start.3 = (bf16[64,128,128]{2,1,0:T(8,128)(2,1)S(1)}, bf16[64,128,128]{2,1,0:T(8,128)(2,1)}, u32[]{:S(2)}) copy-start(bf16[64,128,128]{2,1,0:T(8,128)(2,1)} %kernels.1) | copy-start | bytes 6291460
  20.7 0.8 %copy-start.4 = (bf16[256,128]{1,0:T(8,128)(2,1)S(1)}, bf16[256,128]{1,0:T(8,128)(2,1)}, u32[]{:S(2)}) copy-start(bf16[256,128]{1,0:T(8,128)(2,1)} %w_node.1) | copy-start | bytes 196612
  21.6 0.8 %copy-start.5 = (bf16[128,128]{1,0:T(8,128)(2,1)S(1)}, bf16[128,128]{1,0:T(8,128)(2,1)}, u32[]{:S(2)}) copy-start(bf16[128,128]{1,0:T(8,128)(2,1)} %w_msg.1) | copy-start | bytes 98308
  22.3 0.7 %copy-start.6 = (s32[512,1]{0,1:T(1,128)S(1)}, s32[512,1]{0,1:T(1,128)}, u32[]{:S(2)}) copy-start(s32[512,1]{0,1:T(1,128)} %param.9) | copy-start | bytes 6148
  23.0 0.7 %copy-start.7 = (s32[64]{0:T(128)S(1)}, s32[64]{0:T(128)}, u32[]{:S(2)}) copy-start(s32[64]{0:T(128)} %recv.1) | copy-start | bytes 772
  23.6 0.7 %copy-start.8 = (s32[64]{0:T(128)S(1)}, s32[64]{0:T(128)}, u32[]{:S(2)}) copy-start(s32[64]{0:T(128)} %send.1) | copy-start | bytes 772
  32.6 0.7 %copy-start.1 = (bf16[128,512]{1,0:T(8,128)(2,1)}, bf16[128,512]{1,0:T(8,128)(2,1)S(1)}, u32[]{:S(2)}) copy-start(bf16[128,512]{1,0:T(8,128)(2,1)S(1)} %get-tuple-element.13.rest_0_) | copy-start | bytes 393220
  33.2 0.7 %copy-start.2 = (bf16[512,128]{1,0:T(8,128)(2,1)}, bf16[512,128]{1,0:T(8,128)(2,1)S(1)}, u32[]{:S(2)}) copy-start(bf16[512,128]{1,0:T(8,128)(2,1)S(1)} %get-tuple-element.12.direct) | copy-start | bytes 393220
  33.9 1.3 %collective-permute-start.3 = (bf16[384,128]{1,0:T(8,128)(2,1)S(1)}, bf16[384,128]{1,0:T(8,128)(2,1)S(1)}, u32[]{:S(2)}, u32[]{:S(2)}) collective-permute-start(bf16[384,128]{1,0:T(8,128)(2,1)S(1)} %get-tuple-element.17), channel_id=1, source_target_pairs={{0,1},{1,0},{2,3},{3,2},{4,5},{5,4},{6,7},{7,6},{8,9},{9,8},{10,11... | collective-permute-start | bytes 294920 | tf_op jit(solution)/shard_map/ppermute | solution.py:151
  35.2 8.8 %collective-permute-start.6 = (bf16[384,128]{1,0:T(8,128)(2,1)S(1)}, bf16[384,128]{1,0:T(8,128)(2,1)S(1)}, u32[]{:S(2)}, u32[]{:S(2)}) collective-permute-start(bf16[384,128]{1,0:T(8,128)(2,1)S(1)} %add_convert_fusion.1), channel_id=1, source_target_pairs={{0,6},{1,7},{2,4},{3,5},{4,2},{5,3},{6,0},{7,1},{8,14},{9,15},{10,... | collective-permute-start | bytes 294920 | tf_op jit(solution)/shard_map/ppermute | solution.py:151
  37.7 7.7 %collective-permute-start.5 = (bf16[384,128]{1,0:T(8,128)(2,1)S(1)}, bf16[384,128]{1,0:T(8,128)(2,1)S(1)}, u32[]{:S(2)}, u32[]{:S(2)}) collective-permute-start(bf16[384,128]{1,0:T(8,128)(2,1)S(1)} %add_convert_fusion.1), channel_id=1, source_target_pairs={{0,4},{1,5},{2,6},{3,7},{4,0},{5,1},{6,2},{7,3},{8,12},{9,13},{10,... | collective-permute-start | bytes 294920 | tf_op jit(solution)/shard_map/ppermute | solution.py:151
  38.3 7.1 %collective-permute-start.4 = (bf16[384,128]{1,0:T(8,128)(2,1)S(1)}, bf16[384,128]{1,0:T(8,128)(2,1)S(1)}, u32[]{:S(2)}, u32[]{:S(2)}) collective-permute-start(bf16[384,128]{1,0:T(8,128)(2,1)S(1)} %add_convert_fusion.1), channel_id=1, source_target_pairs={{0,2},{1,3},{2,0},{3,1},{4,6},{5,7},{6,4},{7,5},{8,10},{9,11},{10,... | collective-permute-start | bytes 294920 | tf_op jit(solution)/shard_map/ppermute | solution.py:151
  38.8 23.2 %all-to-all-start.1 = ((bf16[8,160,128]{2,1,0:T(8,128)(2,1)}), bf16[8,160,128]{2,1,0:T(8,128)(2,1)S(1)}, u32[]{:S(2)}, u32[]{:S(2)}) async-start(bf16[8,160,128]{2,1,0:T(8,128)(2,1)} %bitcast.3), calls=%async_computation.1 | async-start | bytes 655360 | tf_op jit(solution)/shard_map/all_to_all | solution.py:175
  42.4 7.0 %collective-permute-start = (bf16[128,512]{1,0:T(8,128)(2,1)S(1)}, bf16[128,512]{1,0:T(8,128)(2,1)S(1)}, u32[]{:S(2)}, u32[]{:S(2)}) collective-permute-start(bf16[128,512]{1,0:T(8,128)(2,1)S(1)} %get-tuple-element.14), channel_id=1, source_target_pairs={{0,1},{1,2},{2,3},{3,0},{4,5},{5,6},{6,7},{7,4},{8,9},{9,10},{10,1... | collective-permute-start | bytes 393224 | tf_op jit(solution)/shard_map/ppermute | solution.py:189
  42.4 7.6 %collective-permute-start.1 = (bf16[128,512]{1,0:T(8,128)(2,1)S(1)}, bf16[128,512]{1,0:T(8,128)(2,1)S(1)}, u32[]{:S(2)}, u32[]{:S(2)}) collective-permute-start(bf16[128,512]{1,0:T(8,128)(2,1)S(1)} %get-tuple-element.15), channel_id=1, source_target_pairs={{0,2},{1,3},{2,0},{3,1},{4,6},{5,7},{6,4},{7,5},{8,10},{9,11},{10,... | collective-permute-start | bytes 393224 | tf_op jit(solution)/shard_map/ppermute | solution.py:189
  44.0 6.0 %collective-permute-start.2 = (bf16[128,512]{1,0:T(8,128)(2,1)S(1)}, bf16[128,512]{1,0:T(8,128)(2,1)S(1)}, u32[]{:S(2)}, u32[]{:S(2)}) collective-permute-start(bf16[128,512]{1,0:T(8,128)(2,1)S(1)} %get-tuple-element.16), channel_id=1, source_target_pairs={{0,3},{1,0},{2,1},{3,2},{4,7},{5,4},{6,5},{7,6},{8,11},{9,8},{10,9... | collective-permute-start | bytes 393224 | tf_op jit(solution)/shard_map/ppermute | solution.py:189
  45.4 9.9 %collective-permute-start.9 = (bf16[384,128]{1,0:T(8,128)(2,1)S(1)}, bf16[384,128]{1,0:T(8,128)(2,1)S(1)}, u32[]{:S(2)}, u32[]{:S(2)}) collective-permute-start(bf16[384,128]{1,0:T(8,128)(2,1)S(1)} %add_convert_fusion), channel_id=1, source_target_pairs={{0,24},{1,25},{2,26},{3,27},{4,28},{5,29},{6,30},{7,31},{8,16},{9,... | collective-permute-start | bytes 294920 | tf_op jit(solution)/shard_map/ppermute | solution.py:151
  49.3 11.3 %collective-permute-start.8 = (bf16[384,128]{1,0:T(8,128)(2,1)S(1)}, bf16[384,128]{1,0:T(8,128)(2,1)S(1)}, u32[]{:S(2)}, u32[]{:S(2)}) collective-permute-start(bf16[384,128]{1,0:T(8,128)(2,1)S(1)} %add_convert_fusion), channel_id=1, source_target_pairs={{0,16},{1,17},{2,18},{3,19},{4,20},{5,21},{6,22},{7,23},{8,24},{9,... | collective-permute-start | bytes 294920 | tf_op jit(solution)/shard_map/ppermute | solution.py:151
  49.3 0.7 %copy-start.9 = (bf16[128,512]{1,0:T(8,128)(2,1)}, bf16[128,512]{1,0:T(8,128)(2,1)S(1)}, u32[]{:S(2)}) copy-start(bf16[128,512]{1,0:T(8,128)(2,1)S(1)} %collective-permute-done.rest_1_) | copy-start | bytes 393220
  49.3 11.3 %collective-permute-start.7 = (bf16[384,128]{1,0:T(8,128)(2,1)S(1)}, bf16[384,128]{1,0:T(8,128)(2,1)S(1)}, u32[]{:S(2)}, u32[]{:S(2)}) collective-permute-start(bf16[384,128]{1,0:T(8,128)(2,1)S(1)} %add_convert_fusion), channel_id=1, source_target_pairs={{0,8},{1,9},{2,10},{3,11},{4,12},{5,13},{6,14},{7,15},{8,0},{9,1},... | collective-permute-start | bytes 294920 | tf_op jit(solution)/shard_map/ppermute | solution.py:151
  50.0 0.6 %copy-start.10 = (bf16[128,512]{1,0:T(8,128)(2,1)}, bf16[128,512]{1,0:T(8,128)(2,1)S(1)}, u32[]{:S(2)}) copy-start(bf16[128,512]{1,0:T(8,128)(2,1)S(1)} %collective-permute-done.1.rest_2_) | copy-start | bytes 393220
  50.0 0.6 %copy-start.11 = (bf16[128,512]{1,0:T(8,128)(2,1)}, bf16[128,512]{1,0:T(8,128)(2,1)S(1)}, u32[]{:S(2)}) copy-start(bf16[128,512]{1,0:T(8,128)(2,1)S(1)} %collective-permute-done.2.rest_3_) | copy-start | bytes 393220

commit v2 on v0

v2 whole, which is shorter than its diff:
```python
import jax
import jax.numpy as jnp
from jax import lax
from jax.experimental import pallas as pl
from jax.experimental.pallas import tpu as pltpu
from jax.sharding import PartitionSpec as P

BF = jnp.bfloat16
F32 = jnp.float32
VMEM = pl.BlockSpec(memory_space=pltpu.VMEM)
ANY = pl.BlockSpec(memory_space=pltpu.HBM)


def mm(left, right):
    return jnp.dot(left, right, preferred_element_type=F32)


def mm_nt(left, right):
    return lax.dot_general(left, right, (((1,), (1,)), ((), ())), preferred_element_type=F32)


def sigmoid(value):
    return 0.5 * jnp.tanh(0.5 * value) + 0.5


def slope_of(value):
    sig = sigmoid(value)
    return sig * (1.0 + value * (1.0 - sig))


def in_hbm(value):
    return pltpu.with_memory_space_constraint(value, pltpu.HBM)


def iota(shape, axis):
    return lax.broadcasted_iota(jnp.int32, shape, axis)


class Sizes:
    def __init__(self, latent, kernels, upstream):
        self.nodes, self.width = latent.shape
        self.tiles, self.rows, _ = kernels.shape
        self.groups, self.spaces = lax.axis_size("group"), lax.axis_size("space")
        self.slots = upstream.shape[0]
        self.capacity = self.slots // self.groups
        self.blocks = self.nodes // self.rows
        self.half = self.spaces // 2
        self.hot = max(16, -(-self.groups // 16) * 16)

    def place_of(self, sender):
        me = lax.axis_index("space")
        device = sender // self.blocks
        step = lax.rem((me >> 1) - (device >> 1) + self.half, self.half)
        other = (me & 1) ^ (device & 1)
        return (2 * step + other) * self.blocks + lax.rem(sender, self.blocks)


def forward_call(z):
    def kernel(recv_hbm, send_hbm, owner_hbm, kern_hbm, w_msg_hbm, w_node_hbm, lat_hbm, *rest):
        others, rest = rest[: z.spaces - 1], rest[z.spaces - 1 :]
        outgoing, slot_out, factor, agg, pre_slope = rest[:5]
        recv, send, owner, w_msg, w_node, kern, msg, acc, place, latent, sems = rest[5:]
        lats = (latent, *others)
        copies = [
            pltpu.make_async_copy(src, dst, sems.at[i])
            for i, (src, dst) in enumerate(
                [
                    (owner_hbm, owner),
                    (w_msg_hbm, w_msg),
                    (lat_hbm, latent),
                    (recv_hbm, recv),
                    (send_hbm, send),
                    (kern_hbm, kern),
                    (w_node_hbm, w_node),
                ]
            )
        ]
        for copy in copies:
            copy.start()
        copies[0].wait()

        owner_row = owner[...]
        hot = (iota((z.hot, z.nodes), 0) == owner_row).astype(F32)
        before = (iota((z.nodes, z.nodes), 0) < iota((z.nodes, z.nodes), 1)).astype(F32)
        counts = mm(hot.astype(BF), before.astype(BF))
        rank = jnp.sum(counts * hot, axis=0, keepdims=True)
        slot = owner_row.astype(F32) * z.capacity + rank
        slot_row = slot.astype(jnp.int32)
        slot_out[...] = slot
        for at in range(0, z.slots, 128):
            down = iota((128, z.nodes), 0) + at
            place[at : at + 128, :] = (down == slot_row).astype(F32).astype(BF)

        copies[1].wait()
        copies[2].wait()
        for part in range(z.spaces):
            preact = mm(lats[part][...], w_msg[...])
            value = (preact * sigmoid(preact)).astype(BF)
            for block in range(z.blocks):
                msg[part * z.blocks + block] = value[block * z.rows : (block + 1) * z.rows, :]

        for copy in copies[3:]:
            copy.wait()
        acc[...] = jnp.zeros_like(acc)

        def gather_tile(t, carry):
            r = recv[t]
            acc[r] = acc[r] + mm(kern[t], msg[z.place_of(send[t])])
            return carry

        lax.fori_loop(0, z.tiles, gather_tile, 0, unroll=8)
        aggregate = acc[...].reshape(z.nodes, z.width).astype(BF)
        agg[...] = aggregate
        own = latent[...]
        mixed = mm(jnp.concatenate([own, aggregate], axis=1), w_node[...])
        sig = sigmoid(mixed)
        factor[...] = sig * (1.0 + mixed * (1.0 - sig))
        new_rows = (own.astype(F32) + mixed * sig).astype(BF)
        outgoing[...] = mm(place[...], new_rows).astype(BF)

        w_msg_t = jnp.transpose(w_msg[...].astype(F32)).astype(BF)
        for part in range(z.spaces):
            pre_slope[part] = slope_of(mm_nt(w_msg_t, lats[part][...]))

    return pl.pallas_call(
        kernel,
        out_shape=(
            jax.ShapeDtypeStruct((z.slots, z.width), BF),
            jax.ShapeDtypeStruct((1, z.nodes), F32),
            jax.ShapeDtypeStruct((z.nodes, z.width), F32),
            jax.ShapeDtypeStruct((z.nodes, z.width), BF),
            jax.ShapeDtypeStruct((z.spaces, z.width, z.nodes), F32),
        ),
        in_specs=[ANY] * 7 + [VMEM] * (z.spaces - 1),
        out_specs=[VMEM] * 5,
        scratch_shapes=[
            pltpu.SMEM((z.tiles,), jnp.int32),
            pltpu.SMEM((z.tiles,), jnp.int32),
            pltpu.VMEM((1, z.nodes), jnp.int32),
            pltpu.VMEM((z.width, z.width), BF),
            pltpu.VMEM((2 * z.width, z.width), BF),
            pltpu.VMEM((z.tiles, z.rows, z.rows), BF),
            pltpu.VMEM((z.spaces * z.blocks, z.rows, z.width), BF),
            pltpu.VMEM((z.blocks, z.rows, z.width), F32),
            pltpu.VMEM((z.slots, z.nodes), BF),
            pltpu.VMEM((z.nodes, z.width), BF),
            pltpu.SemaphoreType.DMA((7,)),
        ],
        cost_estimate=pl.CostEstimate(
            flops=10_000_000_000, bytes_accessed=1000, transcendentals=0
        ),
        compiler_params=pltpu.CompilerParams(vmem_limit_bytes=24 << 20),
        name="forward",
    )


def backward_call(z):
    lanes = 2 * z.half * z.nodes
    low = z.width // 2

    def kernel(recv_hbm, send_hbm, kern_hbm, w_msg_hbm, w_node_hbm, lat_hbm, returned, slot,
               factor, agg, pre_slope, *rest):
        others, rest = rest[: z.spaces - 1], rest[z.spaces - 1 :]
        payload, keep, grad_keep, direct = rest[:4]
        recv, send, w_msg, w_node, kern, place_t, back, spread, latent, sems = rest[4:]
        lats = (latent, *others)
        copies = [
            pltpu.make_async_copy(src, dst, sems.at[i])
            for i, (src, dst) in enumerate(
                [
                    (w_node_hbm, w_node),
                    (recv_hbm, recv),
                    (send_hbm, send),
                    (kern_hbm, kern),
                    (w_msg_hbm, w_msg),
                    (lat_hbm, latent),
                ]
            )
        ]
        for copy in copies:
            copy.start()
        slot_col = jnp.transpose(jnp.broadcast_to(slot[...], (128, z.nodes))).astype(jnp.int32)
        for at in range(0, z.slots, 128):
            across = iota((z.nodes, 128), 1) + at
            place_t[:, at : at + 128] = (across == slot_col).astype(F32).astype(BF)
        incoming = mm(place_t[...], returned[...])
        slope = incoming * factor[...]
        slope_t = jnp.transpose(slope).astype(BF)
        slope = slope.astype(BF)
        copies[0].wait()
        back_t = mm(w_node[z.width : 2 * z.width, :], slope_t).astype(BF)
        for block in range(z.blocks):
            back[block] = back_t[:, block * z.rows : (block + 1) * z.rows]
        spread[...] = jnp.zeros_like(spread)
        for copy in copies[1:]:
            copy.wait()

        def spread_tile(t, carry):
            s = z.place_of(send[t])
            spread[s] = spread[s] + mm(back[recv[t]], kern[t])
            return carry

        lax.fori_loop(0, z.tiles, spread_tile, 0, unroll=8)

        joined = jnp.concatenate([lats[0][...], agg[...]], axis=1)
        grad_node = mm(slope_t, joined)
        direct[...] = (mm_nt(slope, w_node[0 : z.width, :]) + incoming).astype(BF)
        grad_msg = jnp.zeros((z.width, z.width), F32)
        for step in range(z.half):
            for other in range(2):
                part = 2 * ((-step) % z.half) + other
                total = jnp.concatenate(
                    [spread[part * z.blocks + block] for block in range(z.blocks)], axis=1
                )
                preact_grad = (total * pre_slope[part]).astype(BF)
                grad_msg += mm(preact_grad, lats[part][...])
                back_lat = mm(w_msg[...], preact_grad)
                if other:
                    at = step * z.nodes
                    payload[:, at : at + z.nodes] = back_lat[:low].astype(BF)
                    at += z.half * z.nodes
                    payload[:, at : at + z.nodes] = back_lat[low:].astype(BF)
                else:
                    keep[step] = back_lat
        grads = jnp.concatenate([grad_msg, grad_node], axis=1)
        first = (lax.axis_index("space") & 1) == 0
        grad_keep[...] = jnp.where(first, grads[:low], grads[low:])
        payload[:, lanes:] = jnp.where(first, grads[low:], grads[:low]).astype(BF)

    return pl.pallas_call(
        kernel,
        out_shape=(
            jax.ShapeDtypeStruct((low, lanes + 3 * z.width), BF),
            jax.ShapeDtypeStruct((z.half, z.width, z.nodes), F32),
            jax.ShapeDtypeStruct((low, 3 * z.width), F32),
            jax.ShapeDtypeStruct((z.nodes, z.width), BF),
        ),
        in_specs=[ANY] * 6 + [VMEM] * (4 + z.spaces),
        out_specs=[VMEM] * 4,
        scratch_shapes=[
            pltpu.SMEM((z.tiles,), jnp.int32),
            pltpu.SMEM((z.tiles,), jnp.int32),
            pltpu.VMEM((z.width, z.width), BF),
            pltpu.VMEM((2 * z.width, z.width), BF),
            pltpu.VMEM((z.tiles, z.rows, z.rows), BF),
            pltpu.VMEM((z.nodes, z.slots), BF),
            pltpu.VMEM((z.blocks, z.width, z.rows), BF),
            pltpu.VMEM((z.spaces * z.blocks, z.width, z.rows), F32),
            pltpu.VMEM((z.nodes, z.width), BF),
            pltpu.SemaphoreType.DMA((6,)),
        ],
        cost_estimate=pl.CostEstimate(
            flops=1000000, bytes_accessed=1000, transcendentals=0
        ),
        compiler_params=pltpu.CompilerParams(vmem_limit_bytes=24 << 20),
        name="backward",
    )


def pair_call(z):
    lanes = 2 * z.half * z.nodes
    low = z.width // 2

    def kernel(payload, keep, grad_keep, *outs):
        grad, own, sent = outs[0], outs[1], outs[2:]
        grad[...] = (grad_keep[...] + payload[:, lanes:].astype(F32)).astype(BF)
        for step in range(z.half):
            at = step * z.nodes
            top = payload[:, at : at + z.nodes].astype(F32)
            at += z.half * z.nodes
            bottom = payload[:, at : at + z.nodes].astype(F32)
            total = keep[step] + jnp.concatenate([top, bottom], axis=0)
            if step:
                sent[step - 1][...] = total.astype(BF)
            else:
                own[...] = total

    return pl.pallas_call(
        kernel,
        out_shape=(
            jax.ShapeDtypeStruct((low, 3 * z.width), BF),
            jax.ShapeDtypeStruct((z.width, z.nodes), F32),
            *[jax.ShapeDtypeStruct((z.width, z.nodes), BF)] * (z.half - 1),
        ),
        in_specs=[VMEM] * 3,
        out_specs=[VMEM] * (1 + z.half),
        compiler_params=pltpu.CompilerParams(vmem_limit_bytes=8 << 20),
        name="pair",
    )


def finish_call(z):
    def kernel(direct, own, *rest):
        total = own[...]
        for ref in rest[:-1]:
            total = total + ref[...].astype(F32)
        rest[-1][...] = (jnp.transpose(total) + direct[...].astype(F32)).astype(BF)

    return pl.pallas_call(
        kernel,
        out_shape=jax.ShapeDtypeStruct((z.nodes, z.width), BF),
        in_specs=[VMEM] * (1 + z.half),
        compiler_params=pltpu.CompilerParams(vmem_limit_bytes=8 << 20),
        name="finish",
    )


def weights_call(z):
    def kernel(mine, other, updated, grad_msg, grad_node, updated_out, sem):
        copy = pltpu.make_async_copy(updated, updated_out, sem)
        copy.start()
        first = (lax.axis_index("space") & 1) == 0
        mine, other = mine[...], other[...]
        total = jnp.concatenate(
            [jnp.where(first, mine, other), jnp.where(first, other, mine)], axis=0
        )
        grad_msg[...] = jnp.transpose(total[:, : z.width])
        grad_node[...] = jnp.transpose(total[:, z.width :])
        copy.wait()

    return pl.pallas_call(
        kernel,
        out_shape=(
            jax.ShapeDtypeStruct((z.width, z.width), F32),
            jax.ShapeDtypeStruct((2 * z.width, z.width), F32),
            jax.ShapeDtypeStruct((z.slots, z.width), BF),
        ),
        in_specs=[VMEM] * 3,
        out_specs=[pl.BlockSpec(), pl.BlockSpec(), ANY],
        scratch_shapes=[pltpu.SemaphoreType.DMA],
        compiler_params=pltpu.CompilerParams(vmem_limit_bytes=8 << 20),
        name="weights",
    )


def body(latent, owner_ids, tile_recv, tile_send, kernels, w_msg, w_node, upstream):
    z = Sizes(latent, kernels, upstream)
    devices = z.groups * z.spaces

    def swap(value):
        return lax.all_to_all(
            value.reshape(z.groups, z.capacity, z.width),
            "group", split_axis=0, concat_axis=0, tiled=True,
        ).reshape(z.slots, z.width)

    def to_core(value):
        return lax.ppermute(value, "space", [(i, i ^ 1) for i in range(z.spaces)])

    def along(value, step):
        return lax.ppermute(
            value, "space", [(i, (i + 2 * step) % z.spaces) for i in range(z.spaces)]
        )

    def flip(value, mask):
        return lax.ppermute(value, ("group", "space"), [(i, i ^ mask) for i in range(devices)])

    lats = [
        lax.ppermute(
            latent, "space", [(i, (i + 2 * step) % z.spaces ^ other) for i in range(z.spaces)]
        )
        for step in range(z.half)
        for other in range(2)
        if step or other
    ]
    returned = swap(upstream)
    params = [in_hbm(one) for one in (tile_recv, tile_send, kernels, w_msg, w_node, latent)]
    owners = in_hbm(owner_ids.reshape(1, z.nodes))
    outgoing, slot, factor, agg, pre_slope = forward_call(z)(
        params[0], params[1], owners, *params[2:], *lats
    )
    updated = swap(outgoing)
    payload, keep, grad_keep, direct = backward_call(z)(
        *params, returned, slot, factor, agg, pre_slope, *lats
    )
    grad, own, *sent = pair_call(z)(to_core(payload), keep, grad_keep)

    bits = devices.bit_length() - 1
    for at in range(1, bits, 2):
        span = min(2, bits - at)
        grad = grad.astype(BF)
        got = [grad] + [flip(grad, step << at) for step in range(1, 1 << span)]
        got = [one.astype(F32) for one in got]
        grad = got[0] + got[1]
        if span == 2:
            grad = grad + (got[2] + got[3])
    got = [along(part, step + 1) for step, part in enumerate(sent)]
    latent_grad = finish_call(z)(direct, own, *got)
    grad, updated = lax.optimization_barrier((grad, updated))
    grad_msg, grad_node, updated = weights_call(z)(grad, to_core(grad), updated)
    return updated, latent_grad, grad_msg, grad_node


def solution(mesh):
    split = P(("group", "space"))
    wide = P(("group", "space"), None)
    return jax.shard_map(
        body,
        mesh=mesh,
        in_specs=(wide, wide, split, split, P(("group", "space"), None, None), P(), P(), wide),
        out_specs=(wide, wide, P(), P()),
        check_vma=False,
    )
```

time: 236 us -> 49.4 us (0.21)
  waiting for transfers between devices: 128 us -> 13.5 us
  blocking collectives: 24.4 us -> 0 us
  other arithmetic: 22.7 us -> 0.05 us
  local copies, waits for them, and re-layouts: 21.5 us -> 0 us
  matrix products: 16.3 us -> 0 us
  starting transfers between devices: 7.47 us -> 22.4 us
  between operations: 14.3 us -> 0.7 us
  Pallas kernels: 0 us -> 12.3 us
    psum x1 -> x0, waiting for transfers between devices: 127 us -> none  [body(): grad_msg, grad_node = lax.psum((grad_msg, grad_node), ('group', 'space'))]
    scatter-add x2 -> x0, other arithmetic: 17.6 us -> none  [the longest x1 8.79 us: body(): jnp.zeros(table_blocks.shape, jnp.float32).at[tile_send].add(spread)]
    all_to_all x1 -> x0, blocking collectives: 17.2 us -> none  [body(): lax.all_to_all(outgoing.reshape(groups, capacity, width), 'group', split_...]
    dot_general x8 -> x0, matrix products: 16.3 us -> none  [the longest x1 5.13 us: body(): jnp.einsum('tij,tjh->tih', kernels, senders, preferred_element_type=jnp.f...]
    ppermute x0 -> x12, starting transfers between devices: none -> 12.8 us  [the longest x6 8.4 us: flip(): lax.ppermute(value, ('group', 'space'), [(i, i ^ mask) for i in range(dev...]
    pallas_call x0 -> x5, Pallas kernels: none -> 12.3 us  [the longest x1 5.38 us: body(): forward_call(z)(params[0], params[1], owners, *params[2:], *lats)]
    dot_general x2 -> x0, local copies, waits for them, and re-layouts: 11.2 us -> none  [the longest x1 5.61 us: body(): jnp.einsum('tij,tjh->tih', kernels, senders, preferred_element_type=jnp.f...]
    ppermute x0 -> x12, waiting for transfers between devices: none -> 8.58 us  [the longest x6 7.71 us: flip(): lax.ppermute(value, ('group', 'space'), [(i, i ^ mask) for i in range(dev...]
  transfers between devices with their start and end apart: 3 -> 14, of which waited for: 2 -> 7; matrix products, arithmetic and copies ran while one was open for 13% -> 0% of each run, Pallas kernels for 0% -> 13%
where the time goes in v2:
time: 49.4 us; the launch traced here: 49 us
  starting transfers between devices  22.4 us (45%)
  waiting for transfers between devices  13.5 us (27%)
  Pallas kernels  12.3 us (25%)
  between operations  0.7 us (1%)
    all_to_all x2, starting transfers between devices, swap(): lax.all_to_all(value.reshape(z.groups, z.capacity, z.width), 'group', spl...  9.67 us
    ppermute x6, starting transfers between devices, flip(): lax.ppermute(value, ('group', 'space'), [(i, i ^ mask) for i in range(dev...  8.4 us
    ppermute x6, waiting for transfers between devices, flip(): lax.ppermute(value, ('group', 'space'), [(i, i ^ mask) for i in range(dev...  7.71 us
    pallas_call x1, Pallas kernels, body(): forward_call(z)(params[0], params[1], owners, *params[2:], *lats)  5.38 us
    all_to_all x2, waiting for transfers between devices, swap(): lax.all_to_all(value.reshape(z.groups, z.capacity, z.width), 'group', spl...  4.93 us
    pallas_call x1, Pallas kernels, body(): backward_call(z)(*params, returned, slot, factor, agg, pre_slope, *lats)  4.67 us
    ppermute x3, starting transfers between devices, body(): lax.ppermute(latent, 'space', [(i, (i + 2 * step) % z.spaces ^ other) for...  3.15 us
    pallas_call x1, Pallas kernels, body(): grad_msg, grad_node, updated = weights_call(z)(grad, to_core(grad), updated)  1.41 us
  transfers between devices with their start and end apart: 14, of which 7 were waited for; matrix products, arithmetic and copies ran while one was open for 0% of the time, Pallas kernels for 13%

profile of v2, /device:TPU:0, one launch (start us, length us, event | category | flops | bytes accessed | tf_op | source)
XLA Modules:
  0.0 49.0 jit_solution(3325008924363446164)
XLA Ops:
  0.6 2.5 %collective-permute-start.2 = (bf16[512,128]{1,0:T(8,128)(2,1)}, bf16[512,128]{1,0:T(8,128)(2,1)S(1)}, u32[]{:S(2)}, u32[]{:S(2)}) collective-permute-start(bf16[512,128]{1,0:T(8,128)(2,1)} %lat_hbm.3), channel_id=1, source_target_pairs={{0,3},{1,2},{2,1},{3,0},{4,7},{5,6},{6,5},{7,4},{8,11},{9,10},{10,... | collective-permute-start | bytes 393224 | tf_op jit(solution)/shard_map/ppermute | solution.py:358
  3.1 0.6 %collective-permute-start.1 = (bf16[512,128]{1,0:T(8,128)(2,1)}, bf16[512,128]{1,0:T(8,128)(2,1)S(1)}, u32[]{:S(2)}, u32[]{:S(2)}) collective-permute-start(bf16[512,128]{1,0:T(8,128)(2,1)} %lat_hbm.3), channel_id=1, source_target_pairs={{0,2},{1,3},{2,0},{3,1},{4,6},{5,7},{6,4},{7,5},{8,10},{9,11},{10,... | collective-permute-start | bytes 393224 | tf_op jit(solution)/shard_map/ppermute | solution.py:358
  3.7 0.0 collective-permute-start
  3.8 6.0 %all-to-all-start = ((bf16[8,160,128]{2,1,0:T(8,128)(2,1)}), bf16[8,160,128]{2,1,0:T(8,128)(2,1)S(1)}, u32[]{:S(2)}, u32[]{:S(2)}) async-start(bf16[8,160,128]{2,1,0:T(8,128)(2,1)} %bitcast.7), calls=%async_computation | async-start | bytes 655360 | tf_op jit(solution)/shard_map/all_to_all | solution.py:341
  9.8 0.0 collective-permute-done.2.rest_2_
  9.8 0.4 collective-permute-done.1.rest_1_
  10.2 0.0 collective-permute-done.rest_0_
  10.2 5.4 %forward.1 = (bf16[1280,128]{1,0:T(8,128)(2,1)}, f32[1,512]{1,0:T(1,128)S(1)}, f32[512,128]{1,0:T(8,128)S(1)}, bf16[512,128]{1,0:T(8,128)(2,1)S(1)}, f32[4,128,512]{2,1,0:T(8,128)S(1)}) custom-call(s32[64]{0:T(128)} %recv_hbm.3, s32[64]{0:T(128)} %send_hbm.3, s32[1,512]{1,0:T(1,128)} %bitcast.8, bf16[64,128,128]{2,1,0:T(8,128)(2,1)} %kern_hbm.3, ...), custom_call_target="tpu_custom_call" | custom-call | flops 10000000000 | bytes 1000 | tf_op jit(solution)/shard_map/forward/pallas_call | solution.py:368
  15.6 4.9 %all-to-all-done = bf16[8,160,128]{2,1,0:T(8,128)(2,1)S(1)} async-done(((bf16[8,160,128]{2,1,0:T(8,128)(2,1)}), bf16[8,160,128]{2,1,0:T(8,128)(2,1)S(1)}, u32[]{:S(2)}, u32[]{:S(2)}) %all-to-all-start) | async-done | bytes 327712 | tf_op jit(solution)/shard_map/all_to_all | solution.py:341
  20.5 4.7 %backward.1 = (bf16[64,2432]{1,0:T(8,128)(2,1)S(1)}, f32[2,128,512]{2,1,0:T(8,128)S(1)}, f32[64,384]{1,0:T(8,128)S(1)}, bf16[512,128]{1,0:T(8,128)(2,1)S(1)}) custom-call(s32[64]{0:T(128)} %recv_hbm.3, s32[64]{0:T(128)} %send_hbm.3, bf16[64,128,128]{2,1,0:T(8,128)(2,1)} %kern_hbm.3, bf16[128,128]{1,0:T(8,128)(2,1)} %w_msg_hbm.3, ...), custom_call_target="tpu_custom_call" | custom-call | flops 1000000 | bytes 1000 | tf_op jit(solution)/shard_map/backward/pallas_call | solution.py:372
  25.2 0.1 collective-permute-start.3
  25.3 3.6 %all-to-all-start.1 = ((bf16[8,160,128]{2,1,0:T(8,128)(2,1)}), bf16[8,160,128]{2,1,0:T(8,128)(2,1)S(1)}, u32[]{:S(2)}, u32[]{:S(2)}) async-start(bf16[8,160,128]{2,1,0:T(8,128)(2,1)} %bitcast.3), calls=%async_computation.1 | async-start | bytes 655360 | tf_op jit(solution)/shard_map/all_to_all | solution.py:341
  28.9 0.0 collective-permute-done.3.payload
  28.9 0.1 pair.1
  29.0 2.9 %collective-permute-start.6 = (bf16[64,384]{1,0:T(8,128)(2,1)S(1)}, bf16[64,384]{1,0:T(8,128)(2,1)S(1)}, u32[]{:S(2)}, u32[]{:S(2)}) collective-permute-start(bf16[64,384]{1,0:T(8,128)(2,1)S(1)} %get-tuple-element.28), channel_id=1, source_target_pairs={{0,6},{1,7},{2,4},{3,5},{4,2},{5,3},{6,0},{7,1},{8,14},{9,15},{10,... | collective-permute-start | bytes 147464 | tf_op jit(solution)/shard_map/ppermute | solution.py:355
  31.9 0.0 collective-permute-start.5
  31.9 0.6 %collective-permute-start.4 = (bf16[64,384]{1,0:T(8,128)(2,1)S(1)}, bf16[64,384]{1,0:T(8,128)(2,1)S(1)}, u32[]{:S(2)}, u32[]{:S(2)}) collective-permute-start(bf16[64,384]{1,0:T(8,128)(2,1)S(1)} %get-tuple-element.28), channel_id=1, source_target_pairs={{0,2},{1,3},{2,0},{3,1},{4,6},{5,7},{6,4},{7,5},{8,10},{9,11},{10,... | collective-permute-start | bytes 147464 | tf_op jit(solution)/shard_map/ppermute | solution.py:355
  32.5 4.3 %collective-permute-done.6 = bf16[64,384]{1,0:T(8,128)(2,1)S(1)} collective-permute-done((bf16[64,384]{1,0:T(8,128)(2,1)S(1)}, bf16[64,384]{1,0:T(8,128)(2,1)S(1)}, u32[]{:S(2)}, u32[]{:S(2)}) %collective-permute-start.6) | collective-permute-done | bytes 49184 | tf_op jit(solution)/shard_map/ppermute | solution.py:355
  36.8 0.2 collective-permute-done.5
  37.0 0.0 collective-permute-done.4
  37.0 4.2 %collective-permute-start.9 = (bf16[64,384]{1,0:T(8,128)(2,1)S(1)}, bf16[64,384]{1,0:T(8,128)(2,1)S(1)}, u32[]{:S(2)}, u32[]{:S(2)}) collective-permute-start(bf16[64,384]{1,0:T(8,128)(2,1)S(1)} %add_convert_fusion), channel_id=1, source_target_pairs={{0,24},{1,25},{2,26},{3,27},{4,28},{5,29},{6,30},{7,31},{8,16},{9,... | collective-permute-start | bytes 147464 | tf_op jit(solution)/shard_map/ppermute | solution.py:355
  41.2 0.0 collective-permute-start.8
  41.2 0.6 %collective-permute-start.7 = (bf16[64,384]{1,0:T(8,128)(2,1)S(1)}, bf16[64,384]{1,0:T(8,128)(2,1)S(1)}, u32[]{:S(2)}, u32[]{:S(2)}) collective-permute-start(bf16[64,384]{1,0:T(8,128)(2,1)S(1)} %add_convert_fusion), channel_id=1, source_target_pairs={{0,8},{1,9},{2,10},{3,11},{4,12},{5,13},{6,14},{7,15},{8,0},{9,1},... | collective-permute-start | bytes 147464 | tf_op jit(solution)/shard_map/ppermute | solution.py:355
  41.9 1.1 %collective-permute-start.11 = (bf16[128,512]{1,0:T(8,128)(2,1)S(1)}, bf16[128,512]{1,0:T(8,128)(2,1)S(1)}, u32[]{:S(2)}, u32[]{:S(2)}) collective-permute-start(bf16[128,512]{1,0:T(8,128)(2,1)S(1)} %get-tuple-element.35), channel_id=1, source_target_pairs={{0,2},{1,3},{2,0},{3,1},{4,6},{5,7},{6,4},{7,5},{8,10},{9,11},{10,... | collective-permute-start | bytes 393224 | tf_op jit(solution)/shard_map/ppermute | solution.py:350
  42.9 0.5 %collective-permute-done.9 = bf16[64,384]{1,0:T(8,128)(2,1)S(1)} collective-permute-done((bf16[64,384]{1,0:T(8,128)(2,1)S(1)}, bf16[64,384]{1,0:T(8,128)(2,1)S(1)}, u32[]{:S(2)}, u32[]{:S(2)}) %collective-permute-start.9) | collective-permute-done | bytes 49184 | tf_op jit(solution)/shard_map/ppermute | solution.py:355
  43.5 2.7 %collective-permute-done.8 = bf16[64,384]{1,0:T(8,128)(2,1)S(1)} collective-permute-done((bf16[64,384]{1,0:T(8,128)(2,1)S(1)}, bf16[64,384]{1,0:T(8,128)(2,1)S(1)}, u32[]{:S(2)}, u32[]{:S(2)}) %collective-permute-start.8) | collective-permute-done | bytes 49184 | tf_op jit(solution)/shard_map/ppermute | solution.py:355
  46.2 0.0 collective-permute-done.7
  46.2 0.0 all-to-all-done.1
  46.2 0.1 collective-permute-start.10
  46.3 0.5 %collective-permute-done.11.rest_0_ = bf16[128,512]{1,0:T(8,128)(2,1)S(1)} collective-permute-done((bf16[128,512]{1,0:T(8,128)(2,1)S(1)}, bf16[128,512]{1,0:T(8,128)(2,1)S(1)}, u32[]{:S(2)}, u32[]{:S(2)}) %collective-permute-start.11) | collective-permute-done | bytes 131104 | tf_op jit(solution)/shard_map/ppermute | solution.py:350
  46.8 0.8 %finish.1 = bf16[512,128]{1,0:T(8,128)(2,1)} custom-call(bf16[512,128]{1,0:T(8,128)(2,1)S(1)} %get-tuple-element.33.direct, f32[128,512]{1,0:T(8,128)S(1)} %get-tuple-element.34.own, bf16[128,512]{1,0:T(8,128)(2,1)S(1)} %collective-permute-done.11.rest_0_), custom_call_target="tpu_custom_call" | custom-call | tf_op jit(solution)/shard_map/finish/pallas_call | solution.py:387
  47.6 1.4 %weights.1 = (f32[128,128]{1,0:T(8,128)}, f32[256,128]{1,0:T(8,128)}, bf16[1280,128]{1,0:T(8,128)(2,1)}) custom-call(f32[64,384]{1,0:T(8,128)S(1)} %add_add_fusion.mine, f32[64,384]{1,0:T(8,128)S(1)} %collective-permute-done.10.other, bf16[1280,128]{1,0:T(8,128)(2,1)S(1)} %bitcast.6), custom_call_target="tpu_custom_call" | custom-call | tf_op jit(solution)/shard_map/weights/pallas_call | solution.py:389
  (3 shorter events, 0.1 us)
Async XLA Ops:
  0.6 9.2 %collective-permute-start.2 = (bf16[512,128]{1,0:T(8,128)(2,1)}, bf16[512,128]{1,0:T(8,128)(2,1)S(1)}, u32[]{:S(2)}, u32[]{:S(2)}) collective-permute-start(bf16[512,128]{1,0:T(8,128)(2,1)} %lat_hbm.3), channel_id=1, source_target_pairs={{0,3},{1,2},{2,1},{3,0},{4,7},{5,6},{6,5},{7,4},{8,11},{9,10},{10,... | collective-permute-start | bytes 393224 | tf_op jit(solution)/shard_map/ppermute | solution.py:358
  3.1 7.1 %collective-permute-start.1 = (bf16[512,128]{1,0:T(8,128)(2,1)}, bf16[512,128]{1,0:T(8,128)(2,1)S(1)}, u32[]{:S(2)}, u32[]{:S(2)}) collective-permute-start(bf16[512,128]{1,0:T(8,128)(2,1)} %lat_hbm.3), channel_id=1, source_target_pairs={{0,2},{1,3},{2,0},{3,1},{4,6},{5,7},{6,4},{7,5},{8,10},{9,11},{10,... | collective-permute-start | bytes 393224 | tf_op jit(solution)/shard_map/ppermute | solution.py:358
  3.7 6.4 %collective-permute-start = (bf16[512,128]{1,0:T(8,128)(2,1)}, bf16[512,128]{1,0:T(8,128)(2,1)S(1)}, u32[]{:S(2)}, u32[]{:S(2)}) collective-permute-start(bf16[512,128]{1,0:T(8,128)(2,1)} %lat_hbm.3), channel_id=1, source_target_pairs={{0,1},{1,0},{2,3},{3,2},{4,5},{5,4},{6,7},{7,6},{8,9},{9,8},{10,11... | collective-permute-start | bytes 393224 | tf_op jit(solution)/shard_map/ppermute | solution.py:358
  3.8 16.7 %all-to-all-start = ((bf16[8,160,128]{2,1,0:T(8,128)(2,1)}), bf16[8,160,128]{2,1,0:T(8,128)(2,1)S(1)}, u32[]{:S(2)}, u32[]{:S(2)}) async-start(bf16[8,160,128]{2,1,0:T(8,128)(2,1)} %bitcast.7), calls=%async_computation | async-start | bytes 655360 | tf_op jit(solution)/shard_map/all_to_all | solution.py:341
  25.2 3.7 %collective-permute-start.3 = (bf16[64,2432]{1,0:T(8,128)(2,1)S(1)}, bf16[64,2432]{1,0:T(8,128)(2,1)S(1)}, u32[]{:S(2)}, u32[]{:S(2)}) collective-permute-start(bf16[64,2432]{1,0:T(8,128)(2,1)S(1)} %get-tuple-element.25), channel_id=1, source_target_pairs={{0,1},{1,0},{2,3},{3,2},{4,5},{5,4},{6,7},{7,6},{8,9},{9,8},{10,11... | collective-permute-start | bytes 933896 | tf_op jit(solution)/shard_map/ppermute | solution.py:347
  25.3 21.0 %all-to-all-start.1 = ((bf16[8,160,128]{2,1,0:T(8,128)(2,1)}), bf16[8,160,128]{2,1,0:T(8,128)(2,1)S(1)}, u32[]{:S(2)}, u32[]{:S(2)}) async-start(bf16[8,160,128]{2,1,0:T(8,128)(2,1)} %bitcast.3), calls=%async_computation.1 | async-start | bytes 655360 | tf_op jit(solution)/shard_map/all_to_all | solution.py:341
  29.0 7.8 %collective-permute-start.6 = (bf16[64,384]{1,0:T(8,128)(2,1)S(1)}, bf16[64,384]{1,0:T(8,128)(2,1)S(1)}, u32[]{:S(2)}, u32[]{:S(2)}) collective-permute-start(bf16[64,384]{1,0:T(8,128)(2,1)S(1)} %get-tuple-element.28), channel_id=1, source_target_pairs={{0,6},{1,7},{2,4},{3,5},{4,2},{5,3},{6,0},{7,1},{8,14},{9,15},{10,... | collective-permute-start | bytes 147464 | tf_op jit(solution)/shard_map/ppermute | solution.py:355
  31.9 5.1 %collective-permute-start.5 = (bf16[64,384]{1,0:T(8,128)(2,1)S(1)}, bf16[64,384]{1,0:T(8,128)(2,1)S(1)}, u32[]{:S(2)}, u32[]{:S(2)}) collective-permute-start(bf16[64,384]{1,0:T(8,128)(2,1)S(1)} %get-tuple-element.28), channel_id=1, source_target_pairs={{0,4},{1,5},{2,6},{3,7},{4,0},{5,1},{6,2},{7,3},{8,12},{9,13},{10,... | collective-permute-start | bytes 147464 | tf_op jit(solution)/shard_map/ppermute | solution.py:355
  31.9 5.1 %collective-permute-start.4 = (bf16[64,384]{1,0:T(8,128)(2,1)S(1)}, bf16[64,384]{1,0:T(8,128)(2,1)S(1)}, u32[]{:S(2)}, u32[]{:S(2)}) collective-permute-start(bf16[64,384]{1,0:T(8,128)(2,1)S(1)} %get-tuple-element.28), channel_id=1, source_target_pairs={{0,2},{1,3},{2,0},{3,1},{4,6},{5,7},{6,4},{7,5},{8,10},{9,11},{10,... | collective-permute-start | bytes 147464 | tf_op jit(solution)/shard_map/ppermute | solution.py:355
  37.0 6.5 %collective-permute-start.9 = (bf16[64,384]{1,0:T(8,128)(2,1)S(1)}, bf16[64,384]{1,0:T(8,128)(2,1)S(1)}, u32[]{:S(2)}, u32[]{:S(2)}) collective-permute-start(bf16[64,384]{1,0:T(8,128)(2,1)S(1)} %add_convert_fusion), channel_id=1, source_target_pairs={{0,24},{1,25},{2,26},{3,27},{4,28},{5,29},{6,30},{7,31},{8,16},{9,... | collective-permute-start | bytes 147464 | tf_op jit(solution)/shard_map/ppermute | solution.py:355
  41.2 5.0 %collective-permute-start.8 = (bf16[64,384]{1,0:T(8,128)(2,1)S(1)}, bf16[64,384]{1,0:T(8,128)(2,1)S(1)}, u32[]{:S(2)}, u32[]{:S(2)}) collective-permute-start(bf16[64,384]{1,0:T(8,128)(2,1)S(1)} %add_convert_fusion), channel_id=1, source_target_pairs={{0,16},{1,17},{2,18},{3,19},{4,20},{5,21},{6,22},{7,23},{8,24},{9,... | collective-permute-start | bytes 147464 | tf_op jit(solution)/shard_map/ppermute | solution.py:355
  41.2 5.0 %collective-permute-start.7 = (bf16[64,384]{1,0:T(8,128)(2,1)S(1)}, bf16[64,384]{1,0:T(8,128)(2,1)S(1)}, u32[]{:S(2)}, u32[]{:S(2)}) collective-permute-start(bf16[64,384]{1,0:T(8,128)(2,1)S(1)} %add_convert_fusion), channel_id=1, source_target_pairs={{0,8},{1,9},{2,10},{3,11},{4,12},{5,13},{6,14},{7,15},{8,0},{9,1},... | collective-permute-start | bytes 147464 | tf_op jit(solution)/shard_map/ppermute | solution.py:355
  41.9 5.0 %collective-permute-start.11 = (bf16[128,512]{1,0:T(8,128)(2,1)S(1)}, bf16[128,512]{1,0:T(8,128)(2,1)S(1)}, u32[]{:S(2)}, u32[]{:S(2)}) collective-permute-start(bf16[128,512]{1,0:T(8,128)(2,1)S(1)} %get-tuple-element.35), channel_id=1, source_target_pairs={{0,2},{1,3},{2,0},{3,1},{4,6},{5,7},{6,4},{7,5},{8,10},{9,11},{10,... | collective-permute-start | bytes 393224 | tf_op jit(solution)/shard_map/ppermute | solution.py:350
  46.2 1.4 %collective-permute-start.10 = (f32[64,384]{1,0:T(8,128)S(1)}, f32[64,384]{1,0:T(8,128)S(1)}, u32[]{:S(2)}, u32[]{:S(2)}) collective-permute-start(f32[64,384]{1,0:T(8,128)S(1)} %add_add_fusion.mine), channel_id=1, source_target_pairs={{0,1},{1,0},{2,3},{3,2},{4,5},{5,4},{6,7},{7,6},{8,9},{9,8},{10,11... | collective-permute-start | bytes 294920 | tf_op jit(solution)/shard_map/ppermute | solution.py:347

commit v3 on v2

--- a/solution.py
+++ b/solution.py
@@ -6,6 +6,7 @@
 from jax.sharding import PartitionSpec as P
 
 BF = jnp.bfloat16
+CHUNKS = 4
 F32 = jnp.float32
 VMEM = pl.BlockSpec(memory_space=pltpu.VMEM)
 ANY = pl.BlockSpec(memory_space=pltpu.HBM)
@@ -45,7 +46,24 @@
         self.capacity = self.slots // self.groups
         self.blocks = self.nodes // self.rows
         self.half = self.spaces // 2
+        self.chunk = self.tiles // CHUNKS
         self.hot = max(16, -(-self.groups // 16) * 16)
+
+    def tile_copies(self, kern_hbm, kern, sems, first):
+        return [
+            pltpu.make_async_copy(
+                kern_hbm.at[pl.ds(i * self.chunk, self.chunk)],
+                kern.at[pl.ds(i * self.chunk, self.chunk)],
+                sems.at[first + i],
+            )
+            for i in range(CHUNKS)
+        ]
+
+    def each_tile(self, step, copies):
+        for i, copy in enumerate(copies):
+            copy.wait()
+            for t in range(i * self.chunk, (i + 1) * self.chunk):
+                step(t)
 
     def place_of(self, sender):
         me = lax.axis_index("space")
@@ -70,11 +88,11 @@
                     (lat_hbm, latent),
                     (recv_hbm, recv),
                     (send_hbm, send),
-                    (kern_hbm, kern),
                     (w_node_hbm, w_node),
                 ]
             )
         ]
+        copies += z.tile_copies(kern_hbm, kern, sems, len(copies))
         for copy in copies:
             copy.start()
         copies[0].wait()
@@ -99,16 +117,15 @@
             for block in range(z.blocks):
                 msg[part * z.blocks + block] = value[block * z.rows : (block + 1) * z.rows, :]
 
-        for copy in copies[3:]:
+        for copy in copies[3:6]:
             copy.wait()
         acc[...] = jnp.zeros_like(acc)
 
-        def gather_tile(t, carry):
+        def gather_tile(t):
             r = recv[t]
             acc[r] = acc[r] + mm(kern[t], msg[z.place_of(send[t])])
-            return carry
-
-        lax.fori_loop(0, z.tiles, gather_tile, 0, unroll=8)
+
+        z.each_tile(gather_tile, copies[6:])
         aggregate = acc[...].reshape(z.nodes, z.width).astype(BF)
         agg[...] = aggregate
         own = latent[...]
@@ -144,7 +161,7 @@
             pltpu.VMEM((z.blocks, z.rows, z.width), F32),
             pltpu.VMEM((z.slots, z.nodes), BF),
             pltpu.VMEM((z.nodes, z.width), BF),
-            pltpu.SemaphoreType.DMA((7,)),
+            pltpu.SemaphoreType.DMA((6 + CHUNKS,)),
         ],
         cost_estimate=pl.CostEstimate(
             flops=10_000_000_000, bytes_accessed=1000, transcendentals=0
@@ -171,12 +188,12 @@
                     (w_node_hbm, w_node),
                     (recv_hbm, recv),
                     (send_hbm, send),
-                    (kern_hbm, kern),
                     (w_msg_hbm, w_msg),
                     (lat_hbm, latent),
                 ]
             )
         ]
+        copies += z.tile_copies(kern_hbm, kern, sems, len(copies))
         for copy in copies:
             copy.start()
         slot_col = jnp.transpose(jnp.broadcast_to(slot[...], (128, z.nodes))).astype(jnp.int32)
@@ -192,15 +209,16 @@
         for block in range(z.blocks):
             back[block] = back_t[:, block * z.rows : (block + 1) * z.rows]
         spread[...] = jnp.zeros_like(spread)
-        for copy in copies[1:]:
-            copy.wait()
-
-        def spread_tile(t, carry):
+        copies[1].wait()
+        copies[2].wait()
+
+        def spread_tile(t):
             s = z.place_of(send[t])
             spread[s] = spread[s] + mm(back[recv[t]], kern[t])
-            return carry
-
-        lax.fori_loop(0, z.tiles, spread_tile, 0, unroll=8)
+
+        z.each_tile(spread_tile, copies[5:])
+        copies[3].wait()
+        copies[4].wait()
 
         joined = jnp.concatenate([lats[0][...], agg[...]], axis=1)
         grad_node = mm(slope_t, joined)
@@ -247,7 +265,7 @@
             pltpu.VMEM((z.blocks, z.width, z.rows), BF),
             pltpu.VMEM((z.spaces * z.blocks, z.width, z.rows), F32),
             pltpu.VMEM((z.nodes, z.width), BF),
-            pltpu.SemaphoreType.DMA((6,)),
+            pltpu.SemaphoreType.DMA((5 + CHUNKS,)),
         ],
         cost_estimate=pl.CostEstimate(
             flops=1000000, bytes_accessed=1000, transcendentals=0
@@ -306,9 +324,7 @@
 
 
 def weights_call(z):
-    def kernel(mine, other, updated, grad_msg, grad_node, updated_out, sem):
-        copy = pltpu.make_async_copy(updated, updated_out, sem)
-        copy.start()
+    def kernel(mine, other, grad_msg, grad_node):
         first = (lax.axis_index("space") & 1) == 0
         mine, other = mine[...], other[...]
         total = jnp.concatenate(
@@ -316,20 +332,33 @@
         )
         grad_msg[...] = jnp.transpose(total[:, : z.width])
         grad_node[...] = jnp.transpose(total[:, z.width :])
-        copy.wait()
 
     return pl.pallas_call(
         kernel,
         out_shape=(
             jax.ShapeDtypeStruct((z.width, z.width), F32),
             jax.ShapeDtypeStruct((2 * z.width, z.width), F32),
-            jax.ShapeDtypeStruct((z.slots, z.width), BF),
-        ),
-        in_specs=[VMEM] * 3,
-        out_specs=[pl.BlockSpec(), pl.BlockSpec(), ANY],
+        ),
+        in_specs=[VMEM] * 2,
+        compiler_params=pltpu.CompilerParams(vmem_limit_bytes=8 << 20),
+        name="weights",
+    )
+
+
+def emit_call(z):
+    def kernel(rows, out, sem):
+        copy = pltpu.make_async_copy(rows, out, sem)
+        copy.start()
+        copy.wait()
+
+    return pl.pallas_call(
+        kernel,
+        out_shape=jax.ShapeDtypeStruct((z.slots, z.width), BF),
+        in_specs=[VMEM],
+        out_specs=ANY,
         scratch_shapes=[pltpu.SemaphoreType.DMA],
         compiler_params=pltpu.CompilerParams(vmem_limit_bytes=8 << 20),
-        name="weights",
+        name="emit",
     )
 
 
@@ -374,19 +403,23 @@
     )
     grad, own, *sent = pair_call(z)(to_core(payload), keep, grad_keep)
 
+    got = [along(part, step + 1) for step, part in enumerate(sent)]
+    latent_grad = finish_call(z)(direct, own, *got)
+
     bits = devices.bit_length() - 1
     for at in range(1, bits, 2):
         span = min(2, bits - at)
         grad = grad.astype(BF)
         got = [grad] + [flip(grad, step << at) for step in range(1, 1 << span)]
+        if at + 2 >= bits:
+            got[-1], latent_grad = lax.optimization_barrier((got[-1], latent_grad))
         got = [one.astype(F32) for one in got]
         grad = got[0] + got[1]
         if span == 2:
             grad = grad + (got[2] + got[3])
-    got = [along(part, step + 1) for step, part in enumerate(sent)]
-    latent_grad = finish_call(z)(direct, own, *got)
     grad, updated = lax.optimization_barrier((grad, updated))
-    grad_msg, grad_node, updated = weights_call(z)(grad, to_core(grad), updated)
+    updated = emit_call(z)(updated)
+    grad_msg, grad_node = weights_call(z)(grad, to_core(grad))
     return updated, latent_grad, grad_msg, grad_node
 
 

time: 49.4 us -> 48.4 us (0.980)
  Pallas kernels: 12.3 us -> 11 us
    ppermute x6, waiting for transfers between devices: 7.71 us -> 6.62 us  [flip(): lax.ppermute(value, ('group', 'space'), [(i, i ^ mask) for i in range(dev...]
    all_to_all x2, waiting for transfers between devices: 4.93 us -> 5.94 us  [swap(): lax.all_to_all(value.reshape(z.groups, z.capacity, z.width), 'group', spl...]
    pallas_call x1, Pallas kernels: 5.38 us -> 4.37 us  [body(): forward_call(z)(params[0], params[1], owners, *params[2:], *lats)]
    ppermute x2, waiting for transfers between devices: 0.01 us -> 0.55 us  [to_core(): return lax.ppermute(value, 'space', [(i, i ^ 1) for i in range(z.spaces)])]
    ppermute x1, waiting for transfers between devices: 0.5 us -> 0.01 us  [along(): lax.ppermute(value, 'space', [(i, (i + 2 * step) % z.spaces) for i in ran...]
    pallas_call x1 -> x2, Pallas kernels: 1.41 us -> 1.53 us  [the longest x1 0.79 us: body(): grad_msg, grad_node = weights_call(z)(grad, to_core(grad))]
  transfers between devices with their start and end apart: 14 -> 14, of which waited for: 7 -> 7; matrix products, arithmetic and copies ran while one was open for 0% -> 0% of each run, Pallas kernels for 13% -> 12%
where the time goes in v3:
time: 48.4 us; the launch traced here: 48 us
  starting transfers between devices  22.8 us (47%)
  waiting for transfers between devices  13.5 us (28%)
  Pallas kernels  11 us (23%)
  between operations  0.71 us (1%)
    all_to_all x2, starting transfers between devices, swap(): lax.all_to_all(value.reshape(z.groups, z.capacity, z.width), 'group', spl...  9.68 us
    ppermute x6, starting transfers between devices, flip(): lax.ppermute(value, ('group', 'space'), [(i, i ^ mask) for i in range(dev...  8.49 us
    ppermute x6, waiting for transfers between devices, flip(): lax.ppermute(value, ('group', 'space'), [(i, i ^ mask) for i in range(dev...  6.62 us
    all_to_all x2, waiting for transfers between devices, swap(): lax.all_to_all(value.reshape(z.groups, z.capacity, z.width), 'group', spl...  5.94 us
    pallas_call x1, Pallas kernels, body(): forward_call(z)(params[0], params[1], owners, *params[2:], *lats)  4.37 us
    pallas_call x1, Pallas kernels, body(): backward_call(z)(*params, returned, slot, factor, agg, pre_slope, *lats)  4.21 us
    ppermute x3, starting transfers between devices, body(): lax.ppermute(latent, 'space', [(i, (i + 2 * step) % z.spaces ^ other) for...  3.15 us
    ppermute x1, starting transfers between devices, along(): lax.ppermute(value, 'space', [(i, (i + 2 * step) % z.spaces) for i in ran...  1.38 us
  transfers between devices with their start and end apart: 14, of which 7 were waited for; matrix products, arithmetic and copies ran while one was open for 0% of the time, Pallas kernels for 12%

profile of v3, /device:TPU:0, one launch (start us, length us, event | category | flops | bytes accessed | tf_op | source)
XLA Modules:
  0.0 48.0 jit_solution(11714000208276313729)
XLA Ops:
  0.6 2.5 %collective-permute-start.2 = (bf16[512,128]{1,0:T(8,128)(2,1)}, bf16[512,128]{1,0:T(8,128)(2,1)S(1)}, u32[]{:S(2)}, u32[]{:S(2)}) collective-permute-start(bf16[512,128]{1,0:T(8,128)(2,1)} %lat_hbm.3), channel_id=1, source_target_pairs={{0,3},{1,2},{2,1},{3,0},{4,7},{5,6},{6,5},{7,4},{8,11},{9,10},{10,... | collective-permute-start | bytes 393224 | tf_op jit(solution)/shard_map/ppermute | solution.py:387
  3.1 0.6 %collective-permute-start.1 = (bf16[512,128]{1,0:T(8,128)(2,1)}, bf16[512,128]{1,0:T(8,128)(2,1)S(1)}, u32[]{:S(2)}, u32[]{:S(2)}) collective-permute-start(bf16[512,128]{1,0:T(8,128)(2,1)} %lat_hbm.3), channel_id=1, source_target_pairs={{0,2},{1,3},{2,0},{3,1},{4,6},{5,7},{6,4},{7,5},{8,10},{9,11},{10,... | collective-permute-start | bytes 393224 | tf_op jit(solution)/shard_map/ppermute | solution.py:387
  3.7 0.0 collective-permute-start
  3.8 6.0 %all-to-all-start = ((bf16[8,160,128]{2,1,0:T(8,128)(2,1)}), bf16[8,160,128]{2,1,0:T(8,128)(2,1)S(1)}, u32[]{:S(2)}, u32[]{:S(2)}) async-start(bf16[8,160,128]{2,1,0:T(8,128)(2,1)} %bitcast.7), calls=%async_computation | async-start | bytes 655360 | tf_op jit(solution)/shard_map/all_to_all | solution.py:370
  9.8 0.0 collective-permute-done.2.rest_2_
  9.8 0.4 collective-permute-done.1.rest_1_
  10.2 4.4 %forward.1 = (bf16[1280,128]{1,0:T(8,128)(2,1)}, f32[1,512]{1,0:T(1,128)S(1)}, f32[512,128]{1,0:T(8,128)S(1)}, bf16[512,128]{1,0:T(8,128)(2,1)S(1)}, f32[4,128,512]{2,1,0:T(8,128)S(1)}) custom-call(s32[64]{0:T(128)} %recv_hbm.3, s32[64]{0:T(128)} %send_hbm.3, s32[1,512]{1,0:T(1,128)} %bitcast.8, bf16[64,128,128]{2,1,0:T(8,128)(2,1)} %kern_hbm.3, ...), custom_call_target="tpu_custom_call" | custom-call | flops 10000000000 | bytes 1000 | tf_op jit(solution)/shard_map/forward/pallas_call | solution.py:397
  14.6 5.9 %all-to-all-done = bf16[8,160,128]{2,1,0:T(8,128)(2,1)S(1)} async-done(((bf16[8,160,128]{2,1,0:T(8,128)(2,1)}), bf16[8,160,128]{2,1,0:T(8,128)(2,1)S(1)}, u32[]{:S(2)}, u32[]{:S(2)}) %all-to-all-start) | async-done | bytes 327712 | tf_op jit(solution)/shard_map/all_to_all | solution.py:370
  20.5 4.2 %backward.1 = (bf16[64,2432]{1,0:T(8,128)(2,1)S(1)}, f32[2,128,512]{2,1,0:T(8,128)S(1)}, f32[64,384]{1,0:T(8,128)S(1)}, bf16[512,128]{1,0:T(8,128)(2,1)S(1)}) custom-call(s32[64]{0:T(128)} %recv_hbm.3, s32[64]{0:T(128)} %send_hbm.3, bf16[64,128,128]{2,1,0:T(8,128)(2,1)} %kern_hbm.3, bf16[128,128]{1,0:T(8,128)(2,1)} %w_msg_hbm.3, ...), custom_call_target="tpu_custom_call" | custom-call | flops 1000000 | bytes 1000 | tf_op jit(solution)/shard_map/backward/pallas_call | solution.py:401
  24.7 0.1 collective-permute-start.3
  24.8 3.7 %all-to-all-start.1 = ((bf16[8,160,128]{2,1,0:T(8,128)(2,1)}), bf16[8,160,128]{2,1,0:T(8,128)(2,1)S(1)}, u32[]{:S(2)}, u32[]{:S(2)}) async-start(bf16[8,160,128]{2,1,0:T(8,128)(2,1)} %bitcast.3), calls=%async_computation.1 | async-start | bytes 655360 | tf_op jit(solution)/shard_map/all_to_all | solution.py:370
  28.5 0.0 collective-permute-done.3.payload
  28.5 0.1 pair.1
  28.5 2.9 %collective-permute-start.6 = (bf16[64,384]{1,0:T(8,128)(2,1)S(1)}, bf16[64,384]{1,0:T(8,128)(2,1)S(1)}, u32[]{:S(2)}, u32[]{:S(2)}) collective-permute-start(bf16[64,384]{1,0:T(8,128)(2,1)S(1)} %get-tuple-element.29), channel_id=1, source_target_pairs={{0,6},{1,7},{2,4},{3,5},{4,2},{5,3},{6,0},{7,1},{8,14},{9,15},{10,... | collective-permute-start | bytes 147464 | tf_op jit(solution)/shard_map/ppermute | solution.py:384
  31.4 0.0 collective-permute-start.5
  31.4 0.6 %collective-permute-start.4 = (bf16[64,384]{1,0:T(8,128)(2,1)S(1)}, bf16[64,384]{1,0:T(8,128)(2,1)S(1)}, u32[]{:S(2)}, u32[]{:S(2)}) collective-permute-start(bf16[64,384]{1,0:T(8,128)(2,1)S(1)} %get-tuple-element.29), channel_id=1, source_target_pairs={{0,2},{1,3},{2,0},{3,1},{4,6},{5,7},{6,4},{7,5},{8,10},{9,11},{10,... | collective-permute-start | bytes 147464 | tf_op jit(solution)/shard_map/ppermute | solution.py:384
  32.1 1.4 %collective-permute-start.10 = (bf16[128,512]{1,0:T(8,128)(2,1)S(1)}, bf16[128,512]{1,0:T(8,128)(2,1)S(1)}, u32[]{:S(2)}, u32[]{:S(2)}) collective-permute-start(bf16[128,512]{1,0:T(8,128)(2,1)S(1)} %get-tuple-element.32), channel_id=1, source_target_pairs={{0,2},{1,3},{2,0},{3,1},{4,6},{5,7},{6,4},{7,5},{8,10},{9,11},{10,... | collective-permute-start | bytes 393224 | tf_op jit(solution)/shard_map/ppermute | solution.py:379
  33.5 2.9 %collective-permute-done.6 = bf16[64,384]{1,0:T(8,128)(2,1)S(1)} collective-permute-done((bf16[64,384]{1,0:T(8,128)(2,1)S(1)}, bf16[64,384]{1,0:T(8,128)(2,1)S(1)}, u32[]{:S(2)}, u32[]{:S(2)}) %collective-permute-start.6) | collective-permute-done | bytes 49184 | tf_op jit(solution)/shard_map/ppermute | solution.py:384
  36.4 0.2 collective-permute-done.5
  36.5 0.0 collective-permute-done.4
  36.6 4.3 %collective-permute-start.9 = (bf16[64,384]{1,0:T(8,128)(2,1)S(1)}, bf16[64,384]{1,0:T(8,128)(2,1)S(1)}, u32[]{:S(2)}, u32[]{:S(2)}) collective-permute-start(bf16[64,384]{1,0:T(8,128)(2,1)S(1)} %add_convert_fusion), channel_id=1, source_target_pairs={{0,24},{1,25},{2,26},{3,27},{4,28},{5,29},{6,30},{7,31},{8,16},{9,... | collective-permute-start | bytes 147464 | tf_op jit(solution)/shard_map/ppermute | solution.py:384
  40.9 0.0 collective-permute-start.8
  40.9 0.6 %collective-permute-start.7 = (bf16[64,384]{1,0:T(8,128)(2,1)S(1)}, bf16[64,384]{1,0:T(8,128)(2,1)S(1)}, u32[]{:S(2)}, u32[]{:S(2)}) collective-permute-start(bf16[64,384]{1,0:T(8,128)(2,1)S(1)} %add_convert_fusion), channel_id=1, source_target_pairs={{0,8},{1,9},{2,10},{3,11},{4,12},{5,13},{6,14},{7,15},{8,0},{9,1},... | collective-permute-start | bytes 147464 | tf_op jit(solution)/shard_map/ppermute | solution.py:384
  41.5 0.0 collective-permute-done.10.rest_0_
  41.5 0.8 %finish.1 = bf16[512,128]{1,0:T(8,128)(2,1)} custom-call(bf16[512,128]{1,0:T(8,128)(2,1)S(1)} %get-tuple-element.30.direct, f32[128,512]{1,0:T(8,128)S(1)} %get-tuple-element.31.own, bf16[128,512]{1,0:T(8,128)(2,1)S(1)} %collective-permute-done.10.rest_0_), custom_call_target="tpu_custom_call" | custom-call | tf_op jit(solution)/shard_map/finish/pallas_call | solution.py:407
  42.3 0.7 %collective-permute-done.9 = bf16[64,384]{1,0:T(8,128)(2,1)S(1)} collective-permute-done((bf16[64,384]{1,0:T(8,128)(2,1)S(1)}, bf16[64,384]{1,0:T(8,128)(2,1)S(1)}, u32[]{:S(2)}, u32[]{:S(2)}) %collective-permute-start.9) | collective-permute-done | bytes 49184 | tf_op jit(solution)/shard_map/ppermute | solution.py:384
  43.0 2.8 %collective-permute-done.8 = bf16[64,384]{1,0:T(8,128)(2,1)S(1)} collective-permute-done((bf16[64,384]{1,0:T(8,128)(2,1)S(1)}, bf16[64,384]{1,0:T(8,128)(2,1)S(1)}, u32[]{:S(2)}, u32[]{:S(2)}) %collective-permute-start.8) | collective-permute-done | bytes 49184 | tf_op jit(solution)/shard_map/ppermute | solution.py:384
  45.8 0.0 collective-permute-done.7
  45.9 0.1 collective-permute-start.11
  46.0 0.7 %emit.1 = bf16[1280,128]{1,0:T(8,128)(2,1)} custom-call(bf16[1280,128]{1,0:T(8,128)(2,1)S(1)} %bitcast.6), custom_call_target="tpu_custom_call" | custom-call | tf_op jit(solution)/shard_map/emit/pallas_call | solution.py:421
  46.7 0.5 %collective-permute-done.11.other = f32[64,384]{1,0:T(8,128)S(1)} collective-permute-done((f32[64,384]{1,0:T(8,128)S(1)}, f32[64,384]{1,0:T(8,128)S(1)}, u32[]{:S(2)}, u32[]{:S(2)}) %collective-permute-start.11) | collective-permute-done | bytes 98336 | tf_op jit(solution)/shard_map/ppermute | solution.py:376
  47.3 0.8 %weights.1 = (f32[128,128]{1,0:T(8,128)}, f32[256,128]{1,0:T(8,128)}) custom-call(f32[64,384]{1,0:T(8,128)S(1)} %add_add_fusion.mine, f32[64,384]{1,0:T(8,128)S(1)} %collective-permute-done.11.other), custom_call_target="tpu_custom_call" | custom-call | tf_op jit(solution)/shard_map/weights/pallas_call | solution.py:422
  (4 shorter events, 0.1 us)
Async XLA Ops:
  0.6 9.2 %collective-permute-start.2 = (bf16[512,128]{1,0:T(8,128)(2,1)}, bf16[512,128]{1,0:T(8,128)(2,1)S(1)}, u32[]{:S(2)}, u32[]{:S(2)}) collective-permute-start(bf16[512,128]{1,0:T(8,128)(2,1)} %lat_hbm.3), channel_id=1, source_target_pairs={{0,3},{1,2},{2,1},{3,0},{4,7},{5,6},{6,5},{7,4},{8,11},{9,10},{10,... | collective-permute-start | bytes 393224 | tf_op jit(solution)/shard_map/ppermute | solution.py:387
  3.1 7.1 %collective-permute-start.1 = (bf16[512,128]{1,0:T(8,128)(2,1)}, bf16[512,128]{1,0:T(8,128)(2,1)S(1)}, u32[]{:S(2)}, u32[]{:S(2)}) collective-permute-start(bf16[512,128]{1,0:T(8,128)(2,1)} %lat_hbm.3), channel_id=1, source_target_pairs={{0,2},{1,3},{2,0},{3,1},{4,6},{5,7},{6,4},{7,5},{8,10},{9,11},{10,... | collective-permute-start | bytes 393224 | tf_op jit(solution)/shard_map/ppermute | solution.py:387
  3.7 6.4 %collective-permute-start = (bf16[512,128]{1,0:T(8,128)(2,1)}, bf16[512,128]{1,0:T(8,128)(2,1)S(1)}, u32[]{:S(2)}, u32[]{:S(2)}) collective-permute-start(bf16[512,128]{1,0:T(8,128)(2,1)} %lat_hbm.3), channel_id=1, source_target_pairs={{0,1},{1,0},{2,3},{3,2},{4,5},{5,4},{6,7},{7,6},{8,9},{9,8},{10,11... | collective-permute-start | bytes 393224 | tf_op jit(solution)/shard_map/ppermute | solution.py:387
  3.8 16.7 %all-to-all-start = ((bf16[8,160,128]{2,1,0:T(8,128)(2,1)}), bf16[8,160,128]{2,1,0:T(8,128)(2,1)S(1)}, u32[]{:S(2)}, u32[]{:S(2)}) async-start(bf16[8,160,128]{2,1,0:T(8,128)(2,1)} %bitcast.7), calls=%async_computation | async-start | bytes 655360 | tf_op jit(solution)/shard_map/all_to_all | solution.py:370
  24.7 3.7 %collective-permute-start.3 = (bf16[64,2432]{1,0:T(8,128)(2,1)S(1)}, bf16[64,2432]{1,0:T(8,128)(2,1)S(1)}, u32[]{:S(2)}, u32[]{:S(2)}) collective-permute-start(bf16[64,2432]{1,0:T(8,128)(2,1)S(1)} %get-tuple-element.26), channel_id=1, source_target_pairs={{0,1},{1,0},{2,3},{3,2},{4,5},{5,4},{6,7},{7,6},{8,9},{9,8},{10,11... | collective-permute-start | bytes 933896 | tf_op jit(solution)/shard_map/ppermute | solution.py:376
  24.8 21.1 %all-to-all-start.1 = ((bf16[8,160,128]{2,1,0:T(8,128)(2,1)}), bf16[8,160,128]{2,1,0:T(8,128)(2,1)S(1)}, u32[]{:S(2)}, u32[]{:S(2)}) async-start(bf16[8,160,128]{2,1,0:T(8,128)(2,1)} %bitcast.3), calls=%async_computation.1 | async-start | bytes 655360 | tf_op jit(solution)/shard_map/all_to_all | solution.py:370
  28.5 7.8 %collective-permute-start.6 = (bf16[64,384]{1,0:T(8,128)(2,1)S(1)}, bf16[64,384]{1,0:T(8,128)(2,1)S(1)}, u32[]{:S(2)}, u32[]{:S(2)}) collective-permute-start(bf16[64,384]{1,0:T(8,128)(2,1)S(1)} %get-tuple-element.29), channel_id=1, source_target_pairs={{0,6},{1,7},{2,4},{3,5},{4,2},{5,3},{6,0},{7,1},{8,14},{9,15},{10,... | collective-permute-start | bytes 147464 | tf_op jit(solution)/shard_map/ppermute | solution.py:384
  31.4 5.1 %collective-permute-start.5 = (bf16[64,384]{1,0:T(8,128)(2,1)S(1)}, bf16[64,384]{1,0:T(8,128)(2,1)S(1)}, u32[]{:S(2)}, u32[]{:S(2)}) collective-permute-start(bf16[64,384]{1,0:T(8,128)(2,1)S(1)} %get-tuple-element.29), channel_id=1, source_target_pairs={{0,4},{1,5},{2,6},{3,7},{4,0},{5,1},{6,2},{7,3},{8,12},{9,13},{10,... | collective-permute-start | bytes 147464 | tf_op jit(solution)/shard_map/ppermute | solution.py:384
  31.4 5.1 %collective-permute-start.4 = (bf16[64,384]{1,0:T(8,128)(2,1)S(1)}, bf16[64,384]{1,0:T(8,128)(2,1)S(1)}, u32[]{:S(2)}, u32[]{:S(2)}) collective-permute-start(bf16[64,384]{1,0:T(8,128)(2,1)S(1)} %get-tuple-element.29), channel_id=1, source_target_pairs={{0,2},{1,3},{2,0},{3,1},{4,6},{5,7},{6,4},{7,5},{8,10},{9,11},{10,... | collective-permute-start | bytes 147464 | tf_op jit(solution)/shard_map/ppermute | solution.py:384
  32.1 9.4 %collective-permute-start.10 = (bf16[128,512]{1,0:T(8,128)(2,1)S(1)}, bf16[128,512]{1,0:T(8,128)(2,1)S(1)}, u32[]{:S(2)}, u32[]{:S(2)}) collective-permute-start(bf16[128,512]{1,0:T(8,128)(2,1)S(1)} %get-tuple-element.32), channel_id=1, source_target_pairs={{0,2},{1,3},{2,0},{3,1},{4,6},{5,7},{6,4},{7,5},{8,10},{9,11},{10,... | collective-permute-start | bytes 393224 | tf_op jit(solution)/shard_map/ppermute | solution.py:379
  36.6 6.5 %collective-permute-start.9 = (bf16[64,384]{1,0:T(8,128)(2,1)S(1)}, bf16[64,384]{1,0:T(8,128)(2,1)S(1)}, u32[]{:S(2)}, u32[]{:S(2)}) collective-permute-start(bf16[64,384]{1,0:T(8,128)(2,1)S(1)} %add_convert_fusion), channel_id=1, source_target_pairs={{0,24},{1,25},{2,26},{3,27},{4,28},{5,29},{6,30},{7,31},{8,16},{9,... | collective-permute-start | bytes 147464 | tf_op jit(solution)/shard_map/ppermute | solution.py:384
  40.9 5.0 %collective-permute-start.8 = (bf16[64,384]{1,0:T(8,128)(2,1)S(1)}, bf16[64,384]{1,0:T(8,128)(2,1)S(1)}, u32[]{:S(2)}, u32[]{:S(2)}) collective-permute-start(bf16[64,384]{1,0:T(8,128)(2,1)S(1)} %add_convert_fusion), channel_id=1, source_target_pairs={{0,16},{1,17},{2,18},{3,19},{4,20},{5,21},{6,22},{7,23},{8,24},{9,... | collective-permute-start | bytes 147464 | tf_op jit(solution)/shard_map/ppermute | solution.py:384
  40.9 5.0 %collective-permute-start.7 = (bf16[64,384]{1,0:T(8,128)(2,1)S(1)}, bf16[64,384]{1,0:T(8,128)(2,1)S(1)}, u32[]{:S(2)}, u32[]{:S(2)}) collective-permute-start(bf16[64,384]{1,0:T(8,128)(2,1)S(1)} %add_convert_fusion), channel_id=1, source_target_pairs={{0,8},{1,9},{2,10},{3,11},{4,12},{5,13},{6,14},{7,15},{8,0},{9,1},... | collective-permute-start | bytes 147464 | tf_op jit(solution)/shard_map/ppermute | solution.py:384
  45.9 1.4 %collective-permute-start.11 = (f32[64,384]{1,0:T(8,128)S(1)}, f32[64,384]{1,0:T(8,128)S(1)}, u32[]{:S(2)}, u32[]{:S(2)}) collective-permute-start(f32[64,384]{1,0:T(8,128)S(1)} %add_add_fusion.mine), channel_id=1, source_target_pairs={{0,1},{1,0},{2,3},{3,2},{4,5},{5,4},{6,7},{7,6},{8,9},{9,8},{10,11... | collective-permute-start | bytes 294920 | tf_op jit(solution)/shard_map/ppermute | solution.py:376

commit v4 on v3

--- a/solution.py
+++ b/solution.py
@@ -6,7 +6,7 @@
 from jax.sharding import PartitionSpec as P
 
 BF = jnp.bfloat16
-CHUNKS = 4
+CHUNKS = 2
 F32 = jnp.float32
 VMEM = pl.BlockSpec(memory_space=pltpu.VMEM)
 ANY = pl.BlockSpec(memory_space=pltpu.HBM)
@@ -131,7 +131,7 @@
         own = latent[...]
         mixed = mm(jnp.concatenate([own, aggregate], axis=1), w_node[...])
         sig = sigmoid(mixed)
-        factor[...] = sig * (1.0 + mixed * (1.0 - sig))
+        factor[...] = jnp.transpose(sig * (1.0 + mixed * (1.0 - sig)))
         new_rows = (own.astype(F32) + mixed * sig).astype(BF)
         outgoing[...] = mm(place[...], new_rows).astype(BF)
 
@@ -144,7 +144,7 @@
         out_shape=(
             jax.ShapeDtypeStruct((z.slots, z.width), BF),
             jax.ShapeDtypeStruct((1, z.nodes), F32),
-            jax.ShapeDtypeStruct((z.nodes, z.width), F32),
+            jax.ShapeDtypeStruct((z.width, z.nodes), F32),
             jax.ShapeDtypeStruct((z.nodes, z.width), BF),
             jax.ShapeDtypeStruct((z.spaces, z.width, z.nodes), F32),
         ),
@@ -179,7 +179,7 @@
                factor, agg, pre_slope, *rest):
         others, rest = rest[: z.spaces - 1], rest[z.spaces - 1 :]
         payload, keep, grad_keep, direct = rest[:4]
-        recv, send, w_msg, w_node, kern, place_t, back, spread, latent, sems = rest[4:]
+        recv, send, w_msg, w_node, kern, place, back, spread, latent, sems = rest[4:]
         lats = (latent, *others)
         copies = [
             pltpu.make_async_copy(src, dst, sems.at[i])
@@ -196,16 +196,17 @@
         copies += z.tile_copies(kern_hbm, kern, sems, len(copies))
         for copy in copies:
             copy.start()
-        slot_col = jnp.transpose(jnp.broadcast_to(slot[...], (128, z.nodes))).astype(jnp.int32)
+        slot_row = slot[...].astype(jnp.int32)
         for at in range(0, z.slots, 128):
-            across = iota((z.nodes, 128), 1) + at
-            place_t[:, at : at + 128] = (across == slot_col).astype(F32).astype(BF)
-        incoming = mm(place_t[...], returned[...])
-        slope = incoming * factor[...]
-        slope_t = jnp.transpose(slope).astype(BF)
-        slope = slope.astype(BF)
+            down = iota((128, z.nodes), 0) + at
+            place[at : at + 128, :] = (down == slot_row).astype(F32).astype(BF)
+        returned_t = jnp.transpose(returned[...].astype(F32)).astype(BF)
+        incoming_t = mm(returned_t, place[...])
+        slope_t = (incoming_t * factor[...]).astype(BF)
         copies[0].wait()
-        back_t = mm(w_node[z.width : 2 * z.width, :], slope_t).astype(BF)
+        rows_t = mm(w_node[...], slope_t)
+        direct[...] = rows_t[: z.width] + incoming_t
+        back_t = rows_t[z.width :].astype(BF)
         for block in range(z.blocks):
             back[block] = back_t[:, block * z.rows : (block + 1) * z.rows]
         spread[...] = jnp.zeros_like(spread)
@@ -222,7 +223,6 @@
 
         joined = jnp.concatenate([lats[0][...], agg[...]], axis=1)
         grad_node = mm(slope_t, joined)
-        direct[...] = (mm_nt(slope, w_node[0 : z.width, :]) + incoming).astype(BF)
         grad_msg = jnp.zeros((z.width, z.width), F32)
         for step in range(z.half):
             for other in range(2):
@@ -251,7 +251,7 @@
             jax.ShapeDtypeStruct((low, lanes + 3 * z.width), BF),
             jax.ShapeDtypeStruct((z.half, z.width, z.nodes), F32),
             jax.ShapeDtypeStruct((low, 3 * z.width), F32),
-            jax.ShapeDtypeStruct((z.nodes, z.width), BF),
+            jax.ShapeDtypeStruct((z.width, z.nodes), F32),
         ),
         in_specs=[ANY] * 6 + [VMEM] * (4 + z.spaces),
         out_specs=[VMEM] * 4,
@@ -261,7 +261,7 @@
             pltpu.VMEM((z.width, z.width), BF),
             pltpu.VMEM((2 * z.width, z.width), BF),
             pltpu.VMEM((z.tiles, z.rows, z.rows), BF),
-            pltpu.VMEM((z.nodes, z.slots), BF),
+            pltpu.VMEM((z.slots, z.nodes), BF),
             pltpu.VMEM((z.blocks, z.width, z.rows), BF),
             pltpu.VMEM((z.spaces * z.blocks, z.width, z.rows), F32),
             pltpu.VMEM((z.nodes, z.width), BF),
@@ -309,10 +309,10 @@
 
 def finish_call(z):
     def kernel(direct, own, *rest):
-        total = own[...]
+        total = own[...] + direct[...]
         for ref in rest[:-1]:
             total = total + ref[...].astype(F32)
-        rest[-1][...] = (jnp.transpose(total) + direct[...].astype(F32)).astype(BF)
+        rest[-1][...] = jnp.transpose(total).astype(BF)
 
     return pl.pallas_call(
         kernel,
@@ -407,19 +407,19 @@
     latent_grad = finish_call(z)(direct, own, *got)
 
     bits = devices.bit_length() - 1
-    for at in range(1, bits, 2):
+    for at in reversed(range(1, bits, 2)):
         span = min(2, bits - at)
         grad = grad.astype(BF)
         got = [grad] + [flip(grad, step << at) for step in range(1, 1 << span)]
-        if at + 2 >= bits:
+        if at == 1:
             got[-1], latent_grad = lax.optimization_barrier((got[-1], latent_grad))
         got = [one.astype(F32) for one in got]
         grad = got[0] + got[1]
         if span == 2:
             grad = grad + (got[2] + got[3])
-    grad, updated = lax.optimization_barrier((grad, updated))
+    grad_msg, grad_node = weights_call(z)(grad, to_core(grad))
+    grad_msg, updated = lax.optimization_barrier((grad_msg, updated))
     updated = emit_call(z)(updated)
-    grad_msg, grad_node = weights_call(z)(grad, to_core(grad))
     return updated, latent_grad, grad_msg, grad_node
 
 

time: 48.4 us -> 44.6 us (0.921)
  waiting for transfers between devices: 13.5 us -> 11.6 us
  Pallas kernels: 11 us -> 9.51 us
  starting transfers between devices: 22.8 us -> 22.3 us
    ppermute x6, waiting for transfers between devices: 6.62 us -> 1.14 us  [flip(): lax.ppermute(value, ('group', 'space'), [(i, i ^ mask) for i in range(dev...]
    ppermute x2, waiting for transfers between devices: 0.55 us -> 2.88 us  [to_core(): return lax.ppermute(value, 'space', [(i, i ^ 1) for i in range(z.spaces)])]
    pallas_call x1, Pallas kernels: 4.21 us -> 3.09 us  [body(): backward_call(z)(*params, returned, slot, factor, agg, pre_slope, *lats)]
    ppermute x1, waiting for transfers between devices: 0.01 us -> 0.95 us  [along(): lax.ppermute(value, 'space', [(i, (i + 2 * step) % z.spaces) for i in ran...]
    ppermute x6, starting transfers between devices: 8.49 us -> 8.01 us  [flip(): lax.ppermute(value, ('group', 'space'), [(i, i ^ mask) for i in range(dev...]
  transfers between devices with their start and end apart: 14 -> 14, of which waited for: 7 -> 6; matrix products, arithmetic and copies ran while one was open for 0% -> 0% of each run, Pallas kernels for 12% -> 13%
where the time goes in v4:
time: 44.6 us; the launch traced here: 44.2 us
  starting transfers between devices  22.3 us (50%)
  waiting for transfers between devices  11.6 us (26%)
  Pallas kernels  9.51 us (21%)
  between operations  0.7 us (2%)
    all_to_all x2, starting transfers between devices, swap(): lax.all_to_all(value.reshape(z.groups, z.capacity, z.width), 'group', spl...  9.66 us
    ppermute x6, starting transfers between devices, flip(): lax.ppermute(value, ('group', 'space'), [(i, i ^ mask) for i in range(dev...  8.01 us
    all_to_all x2, waiting for transfers between devices, swap(): lax.all_to_all(value.reshape(z.groups, z.capacity, z.width), 'group', spl...  6.25 us
    pallas_call x1, Pallas kernels, body(): forward_call(z)(params[0], params[1], owners, *params[2:], *lats)  4.06 us
    ppermute x3, starting transfers between devices, body(): lax.ppermute(latent, 'space', [(i, (i + 2 * step) % z.spaces ^ other) for...  3.15 us
    pallas_call x1, Pallas kernels, body(): backward_call(z)(*params, returned, slot, factor, agg, pre_slope, *lats)  3.09 us
    ppermute x2, waiting for transfers between devices, to_core(): return lax.ppermute(value, 'space', [(i, i ^ 1) for i in range(z.spaces)])  2.88 us
    ppermute x1, starting transfers between devices, along(): lax.ppermute(value, 'space', [(i, (i + 2 * step) % z.spaces) for i in ran...  1.38 us
  transfers between devices with their start and end apart: 14, of which 6 were waited for; matrix products, arithmetic and copies ran while one was open for 0% of the time, Pallas kernels for 13%

profile of v4, /device:TPU:0, one launch (start us, length us, event | category | flops | bytes accessed | tf_op | source)
XLA Modules:
  0.0 44.2 jit_solution(6357832394740984696)
XLA Ops:
  0.6 2.5 %collective-permute-start.2 = (bf16[512,128]{1,0:T(8,128)(2,1)}, bf16[512,128]{1,0:T(8,128)(2,1)S(1)}, u32[]{:S(2)}, u32[]{:S(2)}) collective-permute-start(bf16[512,128]{1,0:T(8,128)(2,1)} %lat_hbm.3), channel_id=1, source_target_pairs={{0,3},{1,2},{2,1},{3,0},{4,7},{5,6},{6,5},{7,4},{8,11},{9,10},{10,... | collective-permute-start | bytes 393224 | tf_op jit(solution)/shard_map/ppermute | solution.py:387
  3.1 0.6 %collective-permute-start.1 = (bf16[512,128]{1,0:T(8,128)(2,1)}, bf16[512,128]{1,0:T(8,128)(2,1)S(1)}, u32[]{:S(2)}, u32[]{:S(2)}) collective-permute-start(bf16[512,128]{1,0:T(8,128)(2,1)} %lat_hbm.3), channel_id=1, source_target_pairs={{0,2},{1,3},{2,0},{3,1},{4,6},{5,7},{6,4},{7,5},{8,10},{9,11},{10,... | collective-permute-start | bytes 393224 | tf_op jit(solution)/shard_map/ppermute | solution.py:387
  3.7 0.0 collective-permute-start
  3.8 6.0 %all-to-all-start = ((bf16[8,160,128]{2,1,0:T(8,128)(2,1)}), bf16[8,160,128]{2,1,0:T(8,128)(2,1)S(1)}, u32[]{:S(2)}, u32[]{:S(2)}) async-start(bf16[8,160,128]{2,1,0:T(8,128)(2,1)} %bitcast.7), calls=%async_computation | async-start | bytes 655360 | tf_op jit(solution)/shard_map/all_to_all | solution.py:370
  9.8 0.0 collective-permute-done.2.rest_2_
  9.8 0.4 collective-permute-done.1.rest_1_
  10.2 4.1 %forward.1 = (bf16[1280,128]{1,0:T(8,128)(2,1)}, f32[1,512]{1,0:T(1,128)S(1)}, f32[128,512]{1,0:T(8,128)S(1)}, bf16[512,128]{1,0:T(8,128)(2,1)S(1)}, f32[4,128,512]{2,1,0:T(8,128)S(1)}) custom-call(s32[64]{0:T(128)} %recv_hbm.3, s32[64]{0:T(128)} %send_hbm.3, s32[1,512]{1,0:T(1,128)} %bitcast.8, bf16[64,128,128]{2,1,0:T(8,128)(2,1)} %kern_hbm.3, ...), custom_call_target="tpu_custom_call" | custom-call | flops 10000000000 | bytes 1000 | tf_op jit(solution)/shard_map/forward/pallas_call | solution.py:397
  14.2 6.2 %all-to-all-done = bf16[8,160,128]{2,1,0:T(8,128)(2,1)S(1)} async-done(((bf16[8,160,128]{2,1,0:T(8,128)(2,1)}), bf16[8,160,128]{2,1,0:T(8,128)(2,1)S(1)}, u32[]{:S(2)}, u32[]{:S(2)}) %all-to-all-start) | async-done | bytes 327712 | tf_op jit(solution)/shard_map/all_to_all | solution.py:370
  20.5 3.1 %backward.1 = (bf16[64,2432]{1,0:T(8,128)(2,1)S(1)}, f32[2,128,512]{2,1,0:T(8,128)S(1)}, f32[64,384]{1,0:T(8,128)S(1)}, f32[128,512]{1,0:T(8,128)S(1)}) custom-call(s32[64]{0:T(128)} %recv_hbm.3, s32[64]{0:T(128)} %send_hbm.3, bf16[64,128,128]{2,1,0:T(8,128)(2,1)} %kern_hbm.3, bf16[128,128]{1,0:T(8,128)(2,1)} %w_msg_hbm.3, bf16[256,128]{1,0:T(8,128)(2,1)} %w_node_hbm.3, ...), custom_call_target="tpu_custom_call" | custom-call | flops 1000000 | bytes 1000 | tf_op jit(solution)/shard_map/backward/pallas_call | solution.py:401
  23.6 0.1 collective-permute-start.3
  23.7 1.6 %collective-permute-done.3.payload = bf16[64,2432]{1,0:T(8,128)(2,1)S(1)} collective-permute-done((bf16[64,2432]{1,0:T(8,128)(2,1)S(1)}, bf16[64,2432]{1,0:T(8,128)(2,1)S(1)}, u32[]{:S(2)}, u32[]{:S(2)}) %collective-permute-start.3) | collective-permute-done | bytes 311328 | tf_op jit(solution)/shard_map/ppermute | solution.py:376
  25.3 0.1 pair.1
  25.3 1.2 %collective-permute-start.6 = (bf16[64,384]{1,0:T(8,128)(2,1)S(1)}, bf16[64,384]{1,0:T(8,128)(2,1)S(1)}, u32[]{:S(2)}, u32[]{:S(2)}) collective-permute-start(bf16[64,384]{1,0:T(8,128)(2,1)S(1)} %get-tuple-element.29), channel_id=1, source_target_pairs={{0,24},{1,25},{2,26},{3,27},{4,28},{5,29},{6,30},{7,31},{8,16},{9,... | collective-permute-start | bytes 147464 | tf_op jit(solution)/shard_map/ppermute | solution.py:384
  26.6 1.3 %collective-permute-start.5 = (bf16[64,384]{1,0:T(8,128)(2,1)S(1)}, bf16[64,384]{1,0:T(8,128)(2,1)S(1)}, u32[]{:S(2)}, u32[]{:S(2)}) collective-permute-start(bf16[64,384]{1,0:T(8,128)(2,1)S(1)} %get-tuple-element.29), channel_id=1, source_target_pairs={{0,16},{1,17},{2,18},{3,19},{4,20},{5,21},{6,22},{7,23},{8,24},{9,... | collective-permute-start | bytes 147464 | tf_op jit(solution)/shard_map/ppermute | solution.py:384
  27.9 1.9 %collective-permute-start.4 = (bf16[64,384]{1,0:T(8,128)(2,1)S(1)}, bf16[64,384]{1,0:T(8,128)(2,1)S(1)}, u32[]{:S(2)}, u32[]{:S(2)}) collective-permute-start(bf16[64,384]{1,0:T(8,128)(2,1)S(1)} %get-tuple-element.29), channel_id=1, source_target_pairs={{0,8},{1,9},{2,10},{3,11},{4,12},{5,13},{6,14},{7,15},{8,0},{9,1},... | collective-permute-start | bytes 147464 | tf_op jit(solution)/shard_map/ppermute | solution.py:384
  29.8 3.6 %all-to-all-start.1 = ((bf16[8,160,128]{2,1,0:T(8,128)(2,1)}), bf16[8,160,128]{2,1,0:T(8,128)(2,1)S(1)}, u32[]{:S(2)}, u32[]{:S(2)}) async-start(bf16[8,160,128]{2,1,0:T(8,128)(2,1)} %bitcast.3), calls=%async_computation.1 | async-start | bytes 655360 | tf_op jit(solution)/shard_map/all_to_all | solution.py:370
  33.4 1.4 %collective-permute-start.10 = (bf16[128,512]{1,0:T(8,128)(2,1)S(1)}, bf16[128,512]{1,0:T(8,128)(2,1)S(1)}, u32[]{:S(2)}, u32[]{:S(2)}) collective-permute-start(bf16[128,512]{1,0:T(8,128)(2,1)S(1)} %get-tuple-element.32), channel_id=1, source_target_pairs={{0,2},{1,3},{2,0},{3,1},{4,6},{5,7},{6,4},{7,5},{8,10},{9,11},{10,... | collective-permute-start | bytes 393224 | tf_op jit(solution)/shard_map/ppermute | solution.py:379
  34.8 0.0 collective-permute-done.6
  34.8 0.0 collective-permute-done.5
  34.8 2.2 %collective-permute-start.9 = (bf16[64,384]{1,0:T(8,128)(2,1)S(1)}, bf16[64,384]{1,0:T(8,128)(2,1)S(1)}, u32[]{:S(2)}, u32[]{:S(2)}) collective-permute-start(bf16[64,384]{1,0:T(8,128)(2,1)S(1)} %add_convert_fusion), channel_id=1, source_target_pairs={{0,6},{1,7},{2,4},{3,5},{4,2},{5,3},{6,0},{7,1},{8,14},{9,15},{10,... | collective-permute-start | bytes 147464 | tf_op jit(solution)/shard_map/ppermute | solution.py:384
  37.0 0.0 collective-permute-start.8
  37.0 1.4 %collective-permute-start.7 = (bf16[64,384]{1,0:T(8,128)(2,1)S(1)}, bf16[64,384]{1,0:T(8,128)(2,1)S(1)}, u32[]{:S(2)}, u32[]{:S(2)}) collective-permute-start(bf16[64,384]{1,0:T(8,128)(2,1)S(1)} %add_convert_fusion), channel_id=1, source_target_pairs={{0,2},{1,3},{2,0},{3,1},{4,6},{5,7},{6,4},{7,5},{8,10},{9,11},{10,... | collective-permute-start | bytes 147464 | tf_op jit(solution)/shard_map/ppermute | solution.py:384
  38.4 1.0 %collective-permute-done.10.rest_0_ = bf16[128,512]{1,0:T(8,128)(2,1)S(1)} collective-permute-done((bf16[128,512]{1,0:T(8,128)(2,1)S(1)}, bf16[128,512]{1,0:T(8,128)(2,1)S(1)}, u32[]{:S(2)}, u32[]{:S(2)}) %collective-permute-start.10) | collective-permute-done | bytes 131104 | tf_op jit(solution)/shard_map/ppermute | solution.py:379
  39.4 0.8 %finish.1 = bf16[512,128]{1,0:T(8,128)(2,1)} custom-call(f32[128,512]{1,0:T(8,128)S(1)} %get-tuple-element.30.direct, f32[128,512]{1,0:T(8,128)S(1)} %get-tuple-element.31.own, bf16[128,512]{1,0:T(8,128)(2,1)S(1)} %collective-permute-done.10.rest_0_), custom_call_target="tpu_custom_call" | custom-call | tf_op jit(solution)/shard_map/finish/pallas_call | solution.py:407
  40.1 1.1 %collective-permute-done.9 = bf16[64,384]{1,0:T(8,128)(2,1)S(1)} collective-permute-done((bf16[64,384]{1,0:T(8,128)(2,1)S(1)}, bf16[64,384]{1,0:T(8,128)(2,1)S(1)}, u32[]{:S(2)}, u32[]{:S(2)}) %collective-permute-start.9) | collective-permute-done | bytes 49184 | tf_op jit(solution)/shard_map/ppermute | solution.py:384
  41.3 0.0 collective-permute-done.8
  41.3 0.0 collective-permute-done.7
  41.3 0.1 collective-permute-start.11
  41.4 1.3 %collective-permute-done.11.other = f32[64,384]{1,0:T(8,128)S(1)} collective-permute-done((f32[64,384]{1,0:T(8,128)S(1)}, f32[64,384]{1,0:T(8,128)S(1)}, u32[]{:S(2)}, u32[]{:S(2)}) %collective-permute-start.11) | collective-permute-done | bytes 98336 | tf_op jit(solution)/shard_map/ppermute | solution.py:376
  42.7 0.8 %weights.1 = (f32[128,128]{1,0:T(8,128)}, f32[256,128]{1,0:T(8,128)}) custom-call(f32[64,384]{1,0:T(8,128)S(1)} %add_add_fusion.mine, f32[64,384]{1,0:T(8,128)S(1)} %collective-permute-done.11.other), custom_call_target="tpu_custom_call" | custom-call | tf_op jit(solution)/shard_map/weights/pallas_call | solution.py:420
  43.5 0.0 all-to-all-done.1
  43.5 0.7 %emit.1 = bf16[1280,128]{1,0:T(8,128)(2,1)} custom-call(bf16[1280,128]{1,0:T(8,128)(2,1)S(1)} %bitcast.6), custom_call_target="tpu_custom_call" | custom-call | tf_op jit(solution)/shard_map/emit/pallas_call | solution.py:422
  (4 shorter events, 0.1 us)
Async XLA Ops:
  0.6 9.2 %collective-permute-start.2 = (bf16[512,128]{1,0:T(8,128)(2,1)}, bf16[512,128]{1,0:T(8,128)(2,1)S(1)}, u32[]{:S(2)}, u32[]{:S(2)}) collective-permute-start(bf16[512,128]{1,0:T(8,128)(2,1)} %lat_hbm.3), channel_id=1, source_target_pairs={{0,3},{1,2},{2,1},{3,0},{4,7},{5,6},{6,5},{7,4},{8,11},{9,10},{10,... | collective-permute-start | bytes 393224 | tf_op jit(solution)/shard_map/ppermute | solution.py:387
  3.1 7.1 %collective-permute-start.1 = (bf16[512,128]{1,0:T(8,128)(2,1)}, bf16[512,128]{1,0:T(8,128)(2,1)S(1)}, u32[]{:S(2)}, u32[]{:S(2)}) collective-permute-start(bf16[512,128]{1,0:T(8,128)(2,1)} %lat_hbm.3), channel_id=1, source_target_pairs={{0,2},{1,3},{2,0},{3,1},{4,6},{5,7},{6,4},{7,5},{8,10},{9,11},{10,... | collective-permute-start | bytes 393224 | tf_op jit(solution)/shard_map/ppermute | solution.py:387
  3.7 6.4 %collective-permute-start = (bf16[512,128]{1,0:T(8,128)(2,1)}, bf16[512,128]{1,0:T(8,128)(2,1)S(1)}, u32[]{:S(2)}, u32[]{:S(2)}) collective-permute-start(bf16[512,128]{1,0:T(8,128)(2,1)} %lat_hbm.3), channel_id=1, source_target_pairs={{0,1},{1,0},{2,3},{3,2},{4,5},{5,4},{6,7},{7,6},{8,9},{9,8},{10,11... | collective-permute-start | bytes 393224 | tf_op jit(solution)/shard_map/ppermute | solution.py:387
  3.8 16.7 %all-to-all-start = ((bf16[8,160,128]{2,1,0:T(8,128)(2,1)}), bf16[8,160,128]{2,1,0:T(8,128)(2,1)S(1)}, u32[]{:S(2)}, u32[]{:S(2)}) async-start(bf16[8,160,128]{2,1,0:T(8,128)(2,1)} %bitcast.7), calls=%async_computation | async-start | bytes 655360 | tf_op jit(solution)/shard_map/all_to_all | solution.py:370
  23.6 1.7 %collective-permute-start.3 = (bf16[64,2432]{1,0:T(8,128)(2,1)S(1)}, bf16[64,2432]{1,0:T(8,128)(2,1)S(1)}, u32[]{:S(2)}, u32[]{:S(2)}) collective-permute-start(bf16[64,2432]{1,0:T(8,128)(2,1)S(1)} %get-tuple-element.26), channel_id=1, source_target_pairs={{0,1},{1,0},{2,3},{3,2},{4,5},{5,4},{6,7},{7,6},{8,9},{9,8},{10,11... | collective-permute-start | bytes 933896 | tf_op jit(solution)/shard_map/ppermute | solution.py:376
  25.3 9.5 %collective-permute-start.6 = (bf16[64,384]{1,0:T(8,128)(2,1)S(1)}, bf16[64,384]{1,0:T(8,128)(2,1)S(1)}, u32[]{:S(2)}, u32[]{:S(2)}) collective-permute-start(bf16[64,384]{1,0:T(8,128)(2,1)S(1)} %get-tuple-element.29), channel_id=1, source_target_pairs={{0,24},{1,25},{2,26},{3,27},{4,28},{5,29},{6,30},{7,31},{8,16},{9,... | collective-permute-start | bytes 147464 | tf_op jit(solution)/shard_map/ppermute | solution.py:384
  26.6 8.2 %collective-permute-start.5 = (bf16[64,384]{1,0:T(8,128)(2,1)S(1)}, bf16[64,384]{1,0:T(8,128)(2,1)S(1)}, u32[]{:S(2)}, u32[]{:S(2)}) collective-permute-start(bf16[64,384]{1,0:T(8,128)(2,1)S(1)} %get-tuple-element.29), channel_id=1, source_target_pairs={{0,16},{1,17},{2,18},{3,19},{4,20},{5,21},{6,22},{7,23},{8,24},{9,... | collective-permute-start | bytes 147464 | tf_op jit(solution)/shard_map/ppermute | solution.py:384
  27.9 6.9 %collective-permute-start.4 = (bf16[64,384]{1,0:T(8,128)(2,1)S(1)}, bf16[64,384]{1,0:T(8,128)(2,1)S(1)}, u32[]{:S(2)}, u32[]{:S(2)}) collective-permute-start(bf16[64,384]{1,0:T(8,128)(2,1)S(1)} %get-tuple-element.29), channel_id=1, source_target_pairs={{0,8},{1,9},{2,10},{3,11},{4,12},{5,13},{6,14},{7,15},{8,0},{9,1},... | collective-permute-start | bytes 147464 | tf_op jit(solution)/shard_map/ppermute | solution.py:384
  29.8 13.7 %all-to-all-start.1 = ((bf16[8,160,128]{2,1,0:T(8,128)(2,1)}), bf16[8,160,128]{2,1,0:T(8,128)(2,1)S(1)}, u32[]{:S(2)}, u32[]{:S(2)}) async-start(bf16[8,160,128]{2,1,0:T(8,128)(2,1)} %bitcast.3), calls=%async_computation.1 | async-start | bytes 655360 | tf_op jit(solution)/shard_map/all_to_all | solution.py:370
  33.4 5.9 %collective-permute-start.10 = (bf16[128,512]{1,0:T(8,128)(2,1)S(1)}, bf16[128,512]{1,0:T(8,128)(2,1)S(1)}, u32[]{:S(2)}, u32[]{:S(2)}) collective-permute-start(bf16[128,512]{1,0:T(8,128)(2,1)S(1)} %get-tuple-element.32), channel_id=1, source_target_pairs={{0,2},{1,3},{2,0},{3,1},{4,6},{5,7},{6,4},{7,5},{8,10},{9,11},{10,... | collective-permute-start | bytes 393224 | tf_op jit(solution)/shard_map/ppermute | solution.py:379
  34.8 6.4 %collective-permute-start.9 = (bf16[64,384]{1,0:T(8,128)(2,1)S(1)}, bf16[64,384]{1,0:T(8,128)(2,1)S(1)}, u32[]{:S(2)}, u32[]{:S(2)}) collective-permute-start(bf16[64,384]{1,0:T(8,128)(2,1)S(1)} %add_convert_fusion), channel_id=1, source_target_pairs={{0,6},{1,7},{2,4},{3,5},{4,2},{5,3},{6,0},{7,1},{8,14},{9,15},{10,... | collective-permute-start | bytes 147464 | tf_op jit(solution)/shard_map/ppermute | solution.py:384
  37.0 4.2 %collective-permute-start.8 = (bf16[64,384]{1,0:T(8,128)(2,1)S(1)}, bf16[64,384]{1,0:T(8,128)(2,1)S(1)}, u32[]{:S(2)}, u32[]{:S(2)}) collective-permute-start(bf16[64,384]{1,0:T(8,128)(2,1)S(1)} %add_convert_fusion), channel_id=1, source_target_pairs={{0,4},{1,5},{2,6},{3,7},{4,0},{5,1},{6,2},{7,3},{8,12},{9,13},{10,... | collective-permute-start | bytes 147464 | tf_op jit(solution)/shard_map/ppermute | solution.py:384
  37.0 4.2 %collective-permute-start.7 = (bf16[64,384]{1,0:T(8,128)(2,1)S(1)}, bf16[64,384]{1,0:T(8,128)(2,1)S(1)}, u32[]{:S(2)}, u32[]{:S(2)}) collective-permute-start(bf16[64,384]{1,0:T(8,128)(2,1)S(1)} %add_convert_fusion), channel_id=1, source_target_pairs={{0,2},{1,3},{2,0},{3,1},{4,6},{5,7},{6,4},{7,5},{8,10},{9,11},{10,... | collective-permute-start | bytes 147464 | tf_op jit(solution)/shard_map/ppermute | solution.py:384
  41.3 1.4 %collective-permute-start.11 = (f32[64,384]{1,0:T(8,128)S(1)}, f32[64,384]{1,0:T(8,128)S(1)}, u32[]{:S(2)}, u32[]{:S(2)}) collective-permute-start(f32[64,384]{1,0:T(8,128)S(1)} %add_add_fusion.mine), channel_id=1, source_target_pairs={{0,1},{1,0},{2,3},{3,2},{4,5},{5,4},{6,7},{7,6},{8,9},{9,8},{10,11... | collective-permute-start | bytes 294920 | tf_op jit(solution)/shard_map/ppermute | solution.py:376

commit v5 on v4

--- a/solution.py
+++ b/solution.py
@@ -164,7 +164,7 @@
             pltpu.SemaphoreType.DMA((6 + CHUNKS,)),
         ],
         cost_estimate=pl.CostEstimate(
-            flops=10_000_000_000, bytes_accessed=1000, transcendentals=0
+            flops=4400000000, bytes_accessed=1000, transcendentals=0
         ),
         compiler_params=pltpu.CompilerParams(vmem_limit_bytes=24 << 20),
         name="forward",
@@ -383,14 +383,11 @@
     def flip(value, mask):
         return lax.ppermute(value, ("group", "space"), [(i, i ^ mask) for i in range(devices)])
 
-    lats = [
-        lax.ppermute(
-            latent, "space", [(i, (i + 2 * step) % z.spaces ^ other) for i in range(z.spaces)]
-        )
-        for step in range(z.half)
-        for other in range(2)
-        if step or other
-    ]
+    far = [along(latent, step) for step in range(1, z.half)]
+    near = to_core(lax.optimization_barrier((latent, *far))[0])
+    lats = [near]
+    for part in far:
+        lats += [part, to_core(part)]
     returned = swap(upstream)
     params = [in_hbm(one) for one in (tile_recv, tile_send, kernels, w_msg, w_node, latent)]
     owners = in_hbm(owner_ids.reshape(1, z.nodes))

time: 44.6 us -> 43.4 us (0.973)
  waiting for transfers between devices: 11.6 us -> 11 us
  starting transfers between devices: 22.3 us -> 21.8 us
    ppermute x3 -> x0, starting transfers between devices: 3.15 us -> none  [body(): lax.ppermute(latent, 'space', [(i, (i + 2 * step) % z.spaces ^ other) for...]
    ppermute x1 -> x2, starting transfers between devices: 1.38 us -> 3.54 us  [along(): lax.ppermute(value, 'space', [(i, (i + 2 * step) % z.spaces) for i in ran...]
    all_to_all x2, waiting for transfers between devices: 6.25 us -> 4.34 us  [swap(): lax.all_to_all(value.reshape(z.groups, z.capacity, z.width), 'group', spl...]
    ppermute x1 -> x2, waiting for transfers between devices: 0.95 us -> 2.01 us  [along(): lax.ppermute(value, 'space', [(i, (i + 2 * step) % z.spaces) for i in ran...]
    ppermute x2 -> x4, waiting for transfers between devices: 2.88 us -> 3.93 us  [to_core(): return lax.ppermute(value, 'space', [(i, i ^ 1) for i in range(z.spaces)])]
    ppermute x2 -> x4, starting transfers between devices: 0.14 us -> 0.71 us  [to_core(): return lax.ppermute(value, 'space', [(i, i ^ 1) for i in range(z.spaces)])]
  transfers between devices with their start and end apart: 14 -> 14, of which waited for: 6 -> 7; matrix products, arithmetic and copies ran while one was open for 0% -> 0% of each run, Pallas kernels for 13% -> 13%
where the time goes in v5:
time: 43.4 us; the launch traced here: 43.1 us
  starting transfers between devices  21.8 us (50%)
  waiting for transfers between devices  11 us (25%)
  Pallas kernels  9.5 us (22%)
  between operations  0.7 us (2%)
    all_to_all x2, starting transfers between devices, swap(): lax.all_to_all(value.reshape(z.groups, z.capacity, z.width), 'group', spl...  9.4 us
    ppermute x6, starting transfers between devices, flip(): lax.ppermute(value, ('group', 'space'), [(i, i ^ mask) for i in range(dev...  8.13 us
    all_to_all x2, waiting for transfers between devices, swap(): lax.all_to_all(value.reshape(z.groups, z.capacity, z.width), 'group', spl...  4.34 us
    pallas_call x1, Pallas kernels, body(): forward_call(z)(params[0], params[1], owners, *params[2:], *lats)  4.06 us
    ppermute x4, waiting for transfers between devices, to_core(): return lax.ppermute(value, 'space', [(i, i ^ 1) for i in range(z.spaces)])  3.93 us
    ppermute x2, starting transfers between devices, along(): lax.ppermute(value, 'space', [(i, (i + 2 * step) % z.spaces) for i in ran...  3.54 us
    pallas_call x1, Pallas kernels, body(): backward_call(z)(*params, returned, slot, factor, agg, pre_slope, *lats)  3.08 us
    ppermute x2, waiting for transfers between devices, along(): lax.ppermute(value, 'space', [(i, (i + 2 * step) % z.spaces) for i in ran...  2.01 us
  transfers between devices with their start and end apart: 14, of which 7 were waited for; matrix products, arithmetic and copies ran while one was open for 0% of the time, Pallas kernels for 13%

profile of v5, /device:TPU:0, one launch (start us, length us, event | category | flops | bytes accessed | tf_op | source)
XLA Modules:
  0.0 43.1 jit_solution(14587562083860701723)
XLA Ops:
  0.6 3.0 %collective-permute-start = (bf16[512,128]{1,0:T(8,128)(2,1)}, bf16[512,128]{1,0:T(8,128)(2,1)S(1)}, u32[]{:S(2)}, u32[]{:S(2)}) collective-permute-start(bf16[512,128]{1,0:T(8,128)(2,1)} %lat_hbm.3), channel_id=1, source_target_pairs={{0,2},{1,3},{2,0},{3,1},{4,6},{5,7},{6,4},{7,5},{8,10},{9,11},{10,... | collective-permute-start | bytes 393224 | tf_op jit(solution)/shard_map/ppermute | solution.py:379
  3.7 5.8 %all-to-all-start = ((bf16[8,160,128]{2,1,0:T(8,128)(2,1)}), bf16[8,160,128]{2,1,0:T(8,128)(2,1)S(1)}, u32[]{:S(2)}, u32[]{:S(2)}) async-start(bf16[8,160,128]{2,1,0:T(8,128)(2,1)} %bitcast.7), calls=%async_computation | async-start | bytes 655360 | tf_op jit(solution)/shard_map/all_to_all | solution.py:370
  9.5 0.1 collective-permute-start.1
  9.6 0.5 %collective-permute-start.2 = (bf16[512,128]{1,0:T(8,128)(2,1)S(1)}, bf16[512,128]{1,0:T(8,128)(2,1)S(1)}, u32[]{:S(2)}, u32[]{:S(2)}) collective-permute-start(bf16[512,128]{1,0:T(8,128)(2,1)S(1)} %collective-permute-done.rest_1_), channel_id=1, source_target_pairs={{0,1},{1,0},{2,3},{3,2},{4,5},{5,4},{6,7},{7,6},{8,9},{9,8},{10,11... | collective-permute-start | bytes 393224 | tf_op jit(solution)/shard_map/ppermute | solution.py:376
  10.1 1.0 %collective-permute-done.1.rest_0_ = bf16[512,128]{1,0:T(8,128)(2,1)S(1)} collective-permute-done((bf16[512,128]{1,0:T(8,128)(2,1)}, bf16[512,128]{1,0:T(8,128)(2,1)S(1)}, u32[]{:S(2)}, u32[]{:S(2)}) %collective-permute-start.1) | collective-permute-done | bytes 131104 | tf_op jit(solution)/shard_map/ppermute | solution.py:376
  11.1 0.0 collective-permute-done.2.rest_2_
  11.1 4.1 %forward.1 = (bf16[1280,128]{1,0:T(8,128)(2,1)}, f32[1,512]{1,0:T(1,128)S(1)}, f32[128,512]{1,0:T(8,128)S(1)}, bf16[512,128]{1,0:T(8,128)(2,1)S(1)}, f32[4,128,512]{2,1,0:T(8,128)S(1)}) custom-call(s32[64]{0:T(128)} %recv_hbm.3, s32[64]{0:T(128)} %send_hbm.3, s32[1,512]{1,0:T(1,128)} %bitcast.8, bf16[64,128,128]{2,1,0:T(8,128)(2,1)} %kern_hbm.3, ...), custom_call_target="tpu_custom_call" | custom-call | flops 4400000000 | bytes 1000 | tf_op jit(solution)/shard_map/forward/pallas_call | solution.py:394
  15.2 4.3 %all-to-all-done = bf16[8,160,128]{2,1,0:T(8,128)(2,1)S(1)} async-done(((bf16[8,160,128]{2,1,0:T(8,128)(2,1)}), bf16[8,160,128]{2,1,0:T(8,128)(2,1)S(1)}, u32[]{:S(2)}, u32[]{:S(2)}) %all-to-all-start) | async-done | bytes 327712 | tf_op jit(solution)/shard_map/all_to_all | solution.py:370
  19.5 3.1 %backward.1 = (bf16[64,2432]{1,0:T(8,128)(2,1)S(1)}, f32[2,128,512]{2,1,0:T(8,128)S(1)}, f32[64,384]{1,0:T(8,128)S(1)}, f32[128,512]{1,0:T(8,128)S(1)}) custom-call(s32[64]{0:T(128)} %recv_hbm.3, s32[64]{0:T(128)} %send_hbm.3, bf16[64,128,128]{2,1,0:T(8,128)(2,1)} %kern_hbm.3, bf16[128,128]{1,0:T(8,128)(2,1)} %w_msg_hbm.3, bf16[256,128]{1,0:T(8,128)(2,1)} %w_node_hbm.3, ...), custom_call_target="tpu_custom_call" | custom-call | flops 1000000 | bytes 1000 | tf_op jit(solution)/shard_map/backward/pallas_call | solution.py:398
  22.6 0.1 collective-permute-start.3
  22.7 1.6 %collective-permute-done.3.payload = bf16[64,2432]{1,0:T(8,128)(2,1)S(1)} collective-permute-done((bf16[64,2432]{1,0:T(8,128)(2,1)S(1)}, bf16[64,2432]{1,0:T(8,128)(2,1)S(1)}, u32[]{:S(2)}, u32[]{:S(2)}) %collective-permute-start.3) | collective-permute-done | bytes 311328 | tf_op jit(solution)/shard_map/ppermute | solution.py:376
  24.3 0.1 pair.1
  24.3 1.2 %collective-permute-start.6 = (bf16[64,384]{1,0:T(8,128)(2,1)S(1)}, bf16[64,384]{1,0:T(8,128)(2,1)S(1)}, u32[]{:S(2)}, u32[]{:S(2)}) collective-permute-start(bf16[64,384]{1,0:T(8,128)(2,1)S(1)} %get-tuple-element.31), channel_id=1, source_target_pairs={{0,24},{1,25},{2,26},{3,27},{4,28},{5,29},{6,30},{7,31},{8,16},{9,... | collective-permute-start | bytes 147464 | tf_op jit(solution)/shard_map/ppermute | solution.py:384
  25.5 1.3 %collective-permute-start.5 = (bf16[64,384]{1,0:T(8,128)(2,1)S(1)}, bf16[64,384]{1,0:T(8,128)(2,1)S(1)}, u32[]{:S(2)}, u32[]{:S(2)}) collective-permute-start(bf16[64,384]{1,0:T(8,128)(2,1)S(1)} %get-tuple-element.31), channel_id=1, source_target_pairs={{0,16},{1,17},{2,18},{3,19},{4,20},{5,21},{6,22},{7,23},{8,24},{9,... | collective-permute-start | bytes 147464 | tf_op jit(solution)/shard_map/ppermute | solution.py:384
  26.8 1.9 %collective-permute-start.4 = (bf16[64,384]{1,0:T(8,128)(2,1)S(1)}, bf16[64,384]{1,0:T(8,128)(2,1)S(1)}, u32[]{:S(2)}, u32[]{:S(2)}) collective-permute-start(bf16[64,384]{1,0:T(8,128)(2,1)S(1)} %get-tuple-element.31), channel_id=1, source_target_pairs={{0,8},{1,9},{2,10},{3,11},{4,12},{5,13},{6,14},{7,15},{8,0},{9,1},... | collective-permute-start | bytes 147464 | tf_op jit(solution)/shard_map/ppermute | solution.py:384
  28.8 3.6 %all-to-all-start.1 = ((bf16[8,160,128]{2,1,0:T(8,128)(2,1)}), bf16[8,160,128]{2,1,0:T(8,128)(2,1)S(1)}, u32[]{:S(2)}, u32[]{:S(2)}) async-start(bf16[8,160,128]{2,1,0:T(8,128)(2,1)} %bitcast.3), calls=%async_computation.1 | async-start | bytes 655360 | tf_op jit(solution)/shard_map/all_to_all | solution.py:370
  32.4 0.5 %collective-permute-start.10 = (bf16[128,512]{1,0:T(8,128)(2,1)S(1)}, bf16[128,512]{1,0:T(8,128)(2,1)S(1)}, u32[]{:S(2)}, u32[]{:S(2)}) collective-permute-start(bf16[128,512]{1,0:T(8,128)(2,1)S(1)} %get-tuple-element.34), channel_id=1, source_target_pairs={{0,2},{1,3},{2,0},{3,1},{4,6},{5,7},{6,4},{7,5},{8,10},{9,11},{10,... | collective-permute-start | bytes 393224 | tf_op jit(solution)/shard_map/ppermute | solution.py:379
  32.9 0.0 collective-permute-done.6
  32.9 0.0 collective-permute-done.5
  32.9 3.0 %collective-permute-start.9 = (bf16[64,384]{1,0:T(8,128)(2,1)S(1)}, bf16[64,384]{1,0:T(8,128)(2,1)S(1)}, u32[]{:S(2)}, u32[]{:S(2)}) collective-permute-start(bf16[64,384]{1,0:T(8,128)(2,1)S(1)} %add_convert_fusion), channel_id=1, source_target_pairs={{0,6},{1,7},{2,4},{3,5},{4,2},{5,3},{6,0},{7,1},{8,14},{9,15},{10,... | collective-permute-start | bytes 147464 | tf_op jit(solution)/shard_map/ppermute | solution.py:384
  36.0 0.0 collective-permute-start.8
  36.0 0.6 %collective-permute-start.7 = (bf16[64,384]{1,0:T(8,128)(2,1)S(1)}, bf16[64,384]{1,0:T(8,128)(2,1)S(1)}, u32[]{:S(2)}, u32[]{:S(2)}) collective-permute-start(bf16[64,384]{1,0:T(8,128)(2,1)S(1)} %add_convert_fusion), channel_id=1, source_target_pairs={{0,2},{1,3},{2,0},{3,1},{4,6},{5,7},{6,4},{7,5},{8,10},{9,11},{10,... | collective-permute-start | bytes 147464 | tf_op jit(solution)/shard_map/ppermute | solution.py:384
  36.6 2.0 %collective-permute-done.10.rest_0_ = bf16[128,512]{1,0:T(8,128)(2,1)S(1)} collective-permute-done((bf16[128,512]{1,0:T(8,128)(2,1)S(1)}, bf16[128,512]{1,0:T(8,128)(2,1)S(1)}, u32[]{:S(2)}, u32[]{:S(2)}) %collective-permute-start.10) | collective-permute-done | bytes 131104 | tf_op jit(solution)/shard_map/ppermute | solution.py:379
  38.6 0.8 %finish.1 = bf16[512,128]{1,0:T(8,128)(2,1)} custom-call(f32[128,512]{1,0:T(8,128)S(1)} %get-tuple-element.32.direct, f32[128,512]{1,0:T(8,128)S(1)} %get-tuple-element.33.own, bf16[128,512]{1,0:T(8,128)(2,1)S(1)} %collective-permute-done.10.rest_0_), custom_call_target="tpu_custom_call" | custom-call | tf_op jit(solution)/shard_map/finish/pallas_call | solution.py:404
  39.4 0.1 collective-permute-done.9
  39.5 0.7 %collective-permute-done.8 = bf16[64,384]{1,0:T(8,128)(2,1)S(1)} collective-permute-done((bf16[64,384]{1,0:T(8,128)(2,1)S(1)}, bf16[64,384]{1,0:T(8,128)(2,1)S(1)}, u32[]{:S(2)}, u32[]{:S(2)}) %collective-permute-start.8) | collective-permute-done | bytes 49184 | tf_op jit(solution)/shard_map/ppermute | solution.py:384
  40.1 0.0 collective-permute-done.7
  40.2 0.1 collective-permute-start.11
  40.2 1.3 %collective-permute-done.11.other = f32[64,384]{1,0:T(8,128)S(1)} collective-permute-done((f32[64,384]{1,0:T(8,128)S(1)}, f32[64,384]{1,0:T(8,128)S(1)}, u32[]{:S(2)}, u32[]{:S(2)}) %collective-permute-start.11) | collective-permute-done | bytes 98336 | tf_op jit(solution)/shard_map/ppermute | solution.py:376
  41.5 0.8 %weights.1 = (f32[128,128]{1,0:T(8,128)}, f32[256,128]{1,0:T(8,128)}) custom-call(f32[64,384]{1,0:T(8,128)S(1)} %add_add_fusion.mine, f32[64,384]{1,0:T(8,128)S(1)} %collective-permute-done.11.other), custom_call_target="tpu_custom_call" | custom-call | tf_op jit(solution)/shard_map/weights/pallas_call | solution.py:417
  42.3 0.0 all-to-all-done.1
  42.3 0.7 %emit.1 = bf16[1280,128]{1,0:T(8,128)(2,1)} custom-call(bf16[1280,128]{1,0:T(8,128)(2,1)S(1)} %bitcast.6), custom_call_target="tpu_custom_call" | custom-call | tf_op jit(solution)/shard_map/emit/pallas_call | solution.py:419
  (4 shorter events, 0.1 us)
Async XLA Ops:
  0.6 8.8 %collective-permute-start = (bf16[512,128]{1,0:T(8,128)(2,1)}, bf16[512,128]{1,0:T(8,128)(2,1)S(1)}, u32[]{:S(2)}, u32[]{:S(2)}) collective-permute-start(bf16[512,128]{1,0:T(8,128)(2,1)} %lat_hbm.3), channel_id=1, source_target_pairs={{0,2},{1,3},{2,0},{3,1},{4,6},{5,7},{6,4},{7,5},{8,10},{9,11},{10,... | collective-permute-start | bytes 393224 | tf_op jit(solution)/shard_map/ppermute | solution.py:379
  3.7 15.8 %all-to-all-start = ((bf16[8,160,128]{2,1,0:T(8,128)(2,1)}), bf16[8,160,128]{2,1,0:T(8,128)(2,1)S(1)}, u32[]{:S(2)}, u32[]{:S(2)}) async-start(bf16[8,160,128]{2,1,0:T(8,128)(2,1)} %bitcast.7), calls=%async_computation | async-start | bytes 655360 | tf_op jit(solution)/shard_map/all_to_all | solution.py:370
  9.5 1.6 %collective-permute-start.1 = (bf16[512,128]{1,0:T(8,128)(2,1)}, bf16[512,128]{1,0:T(8,128)(2,1)S(1)}, u32[]{:S(2)}, u32[]{:S(2)}) collective-permute-start(bf16[512,128]{1,0:T(8,128)(2,1)} %lat_hbm.3), channel_id=1, source_target_pairs={{0,1},{1,0},{2,3},{3,2},{4,5},{5,4},{6,7},{7,6},{8,9},{9,8},{10,11... | collective-permute-start | bytes 393224 | tf_op jit(solution)/shard_map/ppermute | solution.py:376
  9.6 1.5 %collective-permute-start.2 = (bf16[512,128]{1,0:T(8,128)(2,1)S(1)}, bf16[512,128]{1,0:T(8,128)(2,1)S(1)}, u32[]{:S(2)}, u32[]{:S(2)}) collective-permute-start(bf16[512,128]{1,0:T(8,128)(2,1)S(1)} %collective-permute-done.rest_1_), channel_id=1, source_target_pairs={{0,1},{1,0},{2,3},{3,2},{4,5},{5,4},{6,7},{7,6},{8,9},{9,8},{10,11... | collective-permute-start | bytes 393224 | tf_op jit(solution)/shard_map/ppermute | solution.py:376
  22.6 1.7 %collective-permute-start.3 = (bf16[64,2432]{1,0:T(8,128)(2,1)S(1)}, bf16[64,2432]{1,0:T(8,128)(2,1)S(1)}, u32[]{:S(2)}, u32[]{:S(2)}) collective-permute-start(bf16[64,2432]{1,0:T(8,128)(2,1)S(1)} %get-tuple-element.28), channel_id=1, source_target_pairs={{0,1},{1,0},{2,3},{3,2},{4,5},{5,4},{6,7},{7,6},{8,9},{9,8},{10,11... | collective-permute-start | bytes 933896 | tf_op jit(solution)/shard_map/ppermute | solution.py:376
  24.3 8.6 %collective-permute-start.6 = (bf16[64,384]{1,0:T(8,128)(2,1)S(1)}, bf16[64,384]{1,0:T(8,128)(2,1)S(1)}, u32[]{:S(2)}, u32[]{:S(2)}) collective-permute-start(bf16[64,384]{1,0:T(8,128)(2,1)S(1)} %get-tuple-element.31), channel_id=1, source_target_pairs={{0,24},{1,25},{2,26},{3,27},{4,28},{5,29},{6,30},{7,31},{8,16},{9,... | collective-permute-start | bytes 147464 | tf_op jit(solution)/shard_map/ppermute | solution.py:384
  25.5 7.4 %collective-permute-start.5 = (bf16[64,384]{1,0:T(8,128)(2,1)S(1)}, bf16[64,384]{1,0:T(8,128)(2,1)S(1)}, u32[]{:S(2)}, u32[]{:S(2)}) collective-permute-start(bf16[64,384]{1,0:T(8,128)(2,1)S(1)} %get-tuple-element.31), channel_id=1, source_target_pairs={{0,16},{1,17},{2,18},{3,19},{4,20},{5,21},{6,22},{7,23},{8,24},{9,... | collective-permute-start | bytes 147464 | tf_op jit(solution)/shard_map/ppermute | solution.py:384
  26.8 6.1 %collective-permute-start.4 = (bf16[64,384]{1,0:T(8,128)(2,1)S(1)}, bf16[64,384]{1,0:T(8,128)(2,1)S(1)}, u32[]{:S(2)}, u32[]{:S(2)}) collective-permute-start(bf16[64,384]{1,0:T(8,128)(2,1)S(1)} %get-tuple-element.31), channel_id=1, source_target_pairs={{0,8},{1,9},{2,10},{3,11},{4,12},{5,13},{6,14},{7,15},{8,0},{9,1},... | collective-permute-start | bytes 147464 | tf_op jit(solution)/shard_map/ppermute | solution.py:384
  28.8 13.5 %all-to-all-start.1 = ((bf16[8,160,128]{2,1,0:T(8,128)(2,1)}), bf16[8,160,128]{2,1,0:T(8,128)(2,1)S(1)}, u32[]{:S(2)}, u32[]{:S(2)}) async-start(bf16[8,160,128]{2,1,0:T(8,128)(2,1)} %bitcast.3), calls=%async_computation.1 | async-start | bytes 655360 | tf_op jit(solution)/shard_map/all_to_all | solution.py:370
  32.4 6.3 %collective-permute-start.10 = (bf16[128,512]{1,0:T(8,128)(2,1)S(1)}, bf16[128,512]{1,0:T(8,128)(2,1)S(1)}, u32[]{:S(2)}, u32[]{:S(2)}) collective-permute-start(bf16[128,512]{1,0:T(8,128)(2,1)S(1)} %get-tuple-element.34), channel_id=1, source_target_pairs={{0,2},{1,3},{2,0},{3,1},{4,6},{5,7},{6,4},{7,5},{8,10},{9,11},{10,... | collective-permute-start | bytes 393224 | tf_op jit(solution)/shard_map/ppermute | solution.py:379
  32.9 6.5 %collective-permute-start.9 = (bf16[64,384]{1,0:T(8,128)(2,1)S(1)}, bf16[64,384]{1,0:T(8,128)(2,1)S(1)}, u32[]{:S(2)}, u32[]{:S(2)}) collective-permute-start(bf16[64,384]{1,0:T(8,128)(2,1)S(1)} %add_convert_fusion), channel_id=1, source_target_pairs={{0,6},{1,7},{2,4},{3,5},{4,2},{5,3},{6,0},{7,1},{8,14},{9,15},{10,... | collective-permute-start | bytes 147464 | tf_op jit(solution)/shard_map/ppermute | solution.py:384
  36.0 4.2 %collective-permute-start.8 = (bf16[64,384]{1,0:T(8,128)(2,1)S(1)}, bf16[64,384]{1,0:T(8,128)(2,1)S(1)}, u32[]{:S(2)}, u32[]{:S(2)}) collective-permute-start(bf16[64,384]{1,0:T(8,128)(2,1)S(1)} %add_convert_fusion), channel_id=1, source_target_pairs={{0,4},{1,5},{2,6},{3,7},{4,0},{5,1},{6,2},{7,3},{8,12},{9,13},{10,... | collective-permute-start | bytes 147464 | tf_op jit(solution)/shard_map/ppermute | solution.py:384
  36.0 4.1 %collective-permute-start.7 = (bf16[64,384]{1,0:T(8,128)(2,1)S(1)}, bf16[64,384]{1,0:T(8,128)(2,1)S(1)}, u32[]{:S(2)}, u32[]{:S(2)}) collective-permute-start(bf16[64,384]{1,0:T(8,128)(2,1)S(1)} %add_convert_fusion), channel_id=1, source_target_pairs={{0,2},{1,3},{2,0},{3,1},{4,6},{5,7},{6,4},{7,5},{8,10},{9,11},{10,... | collective-permute-start | bytes 147464 | tf_op jit(solution)/shard_map/ppermute | solution.py:384
  40.2 1.4 %collective-permute-start.11 = (f32[64,384]{1,0:T(8,128)S(1)}, f32[64,384]{1,0:T(8,128)S(1)}, u32[]{:S(2)}, u32[]{:S(2)}) collective-permute-start(f32[64,384]{1,0:T(8,128)S(1)} %add_add_fusion.mine), channel_id=1, source_target_pairs={{0,1},{1,0},{2,3},{3,2},{4,5},{5,4},{6,7},{7,6},{8,9},{9,8},{10,11... | collective-permute-start | bytes 294920 | tf_op jit(solution)/shard_map/ppermute | solution.py:376

commit v6 on v5

--- a/solution.py
+++ b/solution.py
@@ -133,7 +133,8 @@
         sig = sigmoid(mixed)
         factor[...] = jnp.transpose(sig * (1.0 + mixed * (1.0 - sig)))
         new_rows = (own.astype(F32) + mixed * sig).astype(BF)
-        outgoing[...] = mm(place[...], new_rows).astype(BF)
+        for at in range(0, z.slots, 256):
+            outgoing[at : at + 256, :] = mm(place[at : at + 256, :], new_rows).astype(BF)
 
         w_msg_t = jnp.transpose(w_msg[...].astype(F32)).astype(BF)
         for part in range(z.spaces):
@@ -178,8 +179,8 @@
     def kernel(recv_hbm, send_hbm, kern_hbm, w_msg_hbm, w_node_hbm, lat_hbm, returned, slot,
                factor, agg, pre_slope, *rest):
         others, rest = rest[: z.spaces - 1], rest[z.spaces - 1 :]
-        payload, keep, grad_keep, direct = rest[:4]
-        recv, send, w_msg, w_node, kern, place, back, spread, latent, sems = rest[4:]
+        payload, keep, grad_send, grad_keep, direct = rest[:5]
+        recv, send, w_msg, w_node, kern, place, back, spread, latent, sems = rest[5:]
         lats = (latent, *others)
         copies = [
             pltpu.make_async_copy(src, dst, sems.at[i])
@@ -243,18 +244,19 @@
         grads = jnp.concatenate([grad_msg, grad_node], axis=1)
         first = (lax.axis_index("space") & 1) == 0
         grad_keep[...] = jnp.where(first, grads[:low], grads[low:])
-        payload[:, lanes:] = jnp.where(first, grads[low:], grads[:low]).astype(BF)
+        grad_send[...] = jnp.where(first, grads[low:], grads[:low]).astype(BF)
 
     return pl.pallas_call(
         kernel,
         out_shape=(
-            jax.ShapeDtypeStruct((low, lanes + 3 * z.width), BF),
+            jax.ShapeDtypeStruct((low, lanes), BF),
             jax.ShapeDtypeStruct((z.half, z.width, z.nodes), F32),
+            jax.ShapeDtypeStruct((low, 3 * z.width), BF),
             jax.ShapeDtypeStruct((low, 3 * z.width), F32),
             jax.ShapeDtypeStruct((z.width, z.nodes), F32),
         ),
         in_specs=[ANY] * 6 + [VMEM] * (4 + z.spaces),
-        out_specs=[VMEM] * 4,
+        out_specs=[VMEM] * 5,
         scratch_shapes=[
             pltpu.SMEM((z.tiles,), jnp.int32),
             pltpu.SMEM((z.tiles,), jnp.int32),
@@ -276,12 +278,7 @@
 
 
 def pair_call(z):
-    lanes = 2 * z.half * z.nodes
-    low = z.width // 2
-
-    def kernel(payload, keep, grad_keep, *outs):
-        grad, own, sent = outs[0], outs[1], outs[2:]
-        grad[...] = (grad_keep[...] + payload[:, lanes:].astype(F32)).astype(BF)
+    def kernel(payload, keep, own, *sent):
         for step in range(z.half):
             at = step * z.nodes
             top = payload[:, at : at + z.nodes].astype(F32)
@@ -296,12 +293,11 @@
     return pl.pallas_call(
         kernel,
         out_shape=(
-            jax.ShapeDtypeStruct((low, 3 * z.width), BF),
             jax.ShapeDtypeStruct((z.width, z.nodes), F32),
             *[jax.ShapeDtypeStruct((z.width, z.nodes), BF)] * (z.half - 1),
         ),
-        in_specs=[VMEM] * 3,
-        out_specs=[VMEM] * (1 + z.half),
+        in_specs=[VMEM] * 2,
+        out_specs=[VMEM] * z.half,
         compiler_params=pltpu.CompilerParams(vmem_limit_bytes=8 << 20),
         name="pair",
     )
@@ -395,10 +391,11 @@
         params[0], params[1], owners, *params[2:], *lats
     )
     updated = swap(outgoing)
-    payload, keep, grad_keep, direct = backward_call(z)(
+    payload, keep, grad_send, grad_keep, direct = backward_call(z)(
         *params, returned, slot, factor, agg, pre_slope, *lats
     )
-    grad, own, *sent = pair_call(z)(to_core(payload), keep, grad_keep)
+    grad = grad_keep + to_core(grad_send).astype(F32)
+    own, *sent = pair_call(z)(to_core(payload), keep)
 
     got = [along(part, step + 1) for step, part in enumerate(sent)]
     latent_grad = finish_call(z)(direct, own, *got)

time: 43.4 us -> 43.2 us (level)
  waiting for transfers between devices: 11 us -> 10.4 us
  starting transfers between devices: 21.8 us -> 22.3 us
    ppermute x4 -> x5, waiting for transfers between devices: 3.93 us -> 3.06 us  [to_core(): return lax.ppermute(value, 'space', [(i, i ^ 1) for i in range(z.spaces)])]
    ppermute x4 -> x5, starting transfers between devices: 0.71 us -> 1.21 us  [to_core(): return lax.ppermute(value, 'space', [(i, i ^ 1) for i in range(z.spaces)])]
  transfers between devices with their start and end apart: 14 -> 15, of which waited for: 7 -> 6; matrix products, arithmetic and copies ran while one was open for 0% -> 0% of each run, Pallas kernels for 13% -> 13%
where the time goes in v6:
time: 43.2 us; the launch traced here: 42.8 us
  starting transfers between devices  22.3 us (52%)
  waiting for transfers between devices  10.4 us (24%)
  Pallas kernels  9.32 us (22%)
  between operations  0.72 us (2%)
    all_to_all x2, starting transfers between devices, swap(): lax.all_to_all(value.reshape(z.groups, z.capacity, z.width), 'group', spl...  9.4 us
    ppermute x6, starting transfers between devices, flip(): lax.ppermute(value, ('group', 'space'), [(i, i ^ mask) for i in range(dev...  8.12 us
    all_to_all x2, waiting for transfers between devices, swap(): lax.all_to_all(value.reshape(z.groups, z.capacity, z.width), 'group', spl...  4.51 us
    pallas_call x1, Pallas kernels, body(): forward_call(z)(params[0], params[1], owners, *params[2:], *lats)  3.89 us
    ppermute x2, starting transfers between devices, along(): lax.ppermute(value, 'space', [(i, (i + 2 * step) % z.spaces) for i in ran...  3.61 us
    pallas_call x1, Pallas kernels, body(): backward_call(z)(*params, returned, slot, factor, agg, pre_slope, *lats)  3.08 us
    ppermute x5, waiting for transfers between devices, to_core(): return lax.ppermute(value, 'space', [(i, i ^ 1) for i in range(z.spaces)])  3.06 us
    ppermute x2, waiting for transfers between devices, along(): lax.ppermute(value, 'space', [(i, (i + 2 * step) % z.spaces) for i in ran...  2.02 us
  transfers between devices with their start and end apart: 15, of which 6 were waited for; matrix products, arithmetic and copies ran while one was open for 0% of the time, Pallas kernels for 13%

profile of v6, /device:TPU:0, one launch (start us, length us, event | category | flops | bytes accessed | tf_op | source)
XLA Modules:
  0.0 42.8 jit_solution(13826280486440982285)
XLA Ops:
  0.6 3.0 %collective-permute-start = (bf16[512,128]{1,0:T(8,128)(2,1)}, bf16[512,128]{1,0:T(8,128)(2,1)S(1)}, u32[]{:S(2)}, u32[]{:S(2)}) collective-permute-start(bf16[512,128]{1,0:T(8,128)(2,1)} %lat_hbm.3), channel_id=1, source_target_pairs={{0,2},{1,3},{2,0},{3,1},{4,6},{5,7},{6,4},{7,5},{8,10},{9,11},{10,... | collective-permute-start | bytes 393224 | tf_op jit(solution)/shard_map/ppermute | solution.py:375
  3.7 5.8 %all-to-all-start = ((bf16[8,160,128]{2,1,0:T(8,128)(2,1)}), bf16[8,160,128]{2,1,0:T(8,128)(2,1)S(1)}, u32[]{:S(2)}, u32[]{:S(2)}) async-start(bf16[8,160,128]{2,1,0:T(8,128)(2,1)} %bitcast.7), calls=%async_computation | async-start | bytes 655360 | tf_op jit(solution)/shard_map/all_to_all | solution.py:366
  9.5 0.0 collective-permute-done.rest_1_
  9.5 0.1 collective-permute-start.1
  9.6 0.5 %collective-permute-start.2 = (bf16[512,128]{1,0:T(8,128)(2,1)S(1)}, bf16[512,128]{1,0:T(8,128)(2,1)S(1)}, u32[]{:S(2)}, u32[]{:S(2)}) collective-permute-start(bf16[512,128]{1,0:T(8,128)(2,1)S(1)} %collective-permute-done.rest_1_), channel_id=1, source_target_pairs={{0,1},{1,0},{2,3},{3,2},{4,5},{5,4},{6,7},{7,6},{8,9},{9,8},{10,11... | collective-permute-start | bytes 393224 | tf_op jit(solution)/shard_map/ppermute | solution.py:372
  10.1 1.0 %collective-permute-done.1.rest_0_ = bf16[512,128]{1,0:T(8,128)(2,1)S(1)} collective-permute-done((bf16[512,128]{1,0:T(8,128)(2,1)}, bf16[512,128]{1,0:T(8,128)(2,1)S(1)}, u32[]{:S(2)}, u32[]{:S(2)}) %collective-permute-start.1) | collective-permute-done | bytes 131104 | tf_op jit(solution)/shard_map/ppermute | solution.py:372
  11.1 0.0 collective-permute-done.2.rest_2_
  11.1 3.9 %forward.1 = (bf16[1280,128]{1,0:T(8,128)(2,1)}, f32[1,512]{1,0:T(1,128)S(1)}, f32[128,512]{1,0:T(8,128)S(1)}, bf16[512,128]{1,0:T(8,128)(2,1)S(1)}, f32[4,128,512]{2,1,0:T(8,128)S(1)}) custom-call(s32[64]{0:T(128)} %recv_hbm.3, s32[64]{0:T(128)} %send_hbm.3, s32[1,512]{1,0:T(1,128)} %bitcast.8, bf16[64,128,128]{2,1,0:T(8,128)(2,1)} %kern_hbm.3, ...), custom_call_target="tpu_custom_call" | custom-call | flops 4400000000 | bytes 1000 | tf_op jit(solution)/shard_map/forward/pallas_call | solution.py:390
  15.0 4.5 %all-to-all-done = bf16[8,160,128]{2,1,0:T(8,128)(2,1)S(1)} async-done(((bf16[8,160,128]{2,1,0:T(8,128)(2,1)}), bf16[8,160,128]{2,1,0:T(8,128)(2,1)S(1)}, u32[]{:S(2)}, u32[]{:S(2)}) %all-to-all-start) | async-done | bytes 327712 | tf_op jit(solution)/shard_map/all_to_all | solution.py:366
  19.5 3.1 %backward.1 = (bf16[64,2048]{1,0:T(8,128)(2,1)S(1)}, f32[2,128,512]{2,1,0:T(8,128)S(1)}, bf16[64,384]{1,0:T(8,128)(2,1)S(1)}, f32[64,384]{1,0:T(8,128)S(1)}, f32[128,512]{1,0:T(8,128)S(1)}) custom-call(s32[64]{0:T(128)} %recv_hbm.3, s32[64]{0:T(128)} %send_hbm.3, bf16[64,128,128]{2,1,0:T(8,128)(2,1)} %kern_hbm.3, bf16[128,128]{1,0:T(8,128)(2,1)} %w_msg_hbm.3, ...), custom_call_target="tpu_custom_call" | custom-call | flops 1000000 | bytes 1000 | tf_op jit(solution)/shard_map/backward/pallas_call | solution.py:394
  22.6 0.1 collective-permute-start.3
  22.7 0.5 %collective-permute-start.10 = (bf16[64,2048]{1,0:T(8,128)(2,1)S(1)}, bf16[64,2048]{1,0:T(8,128)(2,1)S(1)}, u32[]{:S(2)}, u32[]{:S(2)}) collective-permute-start(bf16[64,2048]{1,0:T(8,128)(2,1)S(1)} %get-tuple-element.31), channel_id=1, source_target_pairs={{0,1},{1,0},{2,3},{3,2},{4,5},{5,4},{6,7},{7,6},{8,9},{9,8},{10,11... | collective-permute-start | bytes 786440 | tf_op jit(solution)/shard_map/ppermute | solution.py:372
  23.2 0.7 %collective-permute-done.3 = bf16[64,384]{1,0:T(8,128)(2,1)S(1)} collective-permute-done((bf16[64,384]{1,0:T(8,128)(2,1)S(1)}, bf16[64,384]{1,0:T(8,128)(2,1)S(1)}, u32[]{:S(2)}, u32[]{:S(2)}) %collective-permute-start.3) | collective-permute-done | bytes 49184 | tf_op jit(solution)/shard_map/ppermute | solution.py:372
  23.9 1.2 %collective-permute-start.6 = (bf16[64,384]{1,0:T(8,128)(2,1)S(1)}, bf16[64,384]{1,0:T(8,128)(2,1)S(1)}, u32[]{:S(2)}, u32[]{:S(2)}) collective-permute-start(bf16[64,384]{1,0:T(8,128)(2,1)S(1)} %add_convert_fusion.1), channel_id=1, source_target_pairs={{0,24},{1,25},{2,26},{3,27},{4,28},{5,29},{6,30},{7,31},{8,16},{9,... | collective-permute-start | bytes 147464 | tf_op jit(solution)/shard_map/ppermute | solution.py:380
  25.1 1.3 %collective-permute-start.5 = (bf16[64,384]{1,0:T(8,128)(2,1)S(1)}, bf16[64,384]{1,0:T(8,128)(2,1)S(1)}, u32[]{:S(2)}, u32[]{:S(2)}) collective-permute-start(bf16[64,384]{1,0:T(8,128)(2,1)S(1)} %add_convert_fusion.1), channel_id=1, source_target_pairs={{0,16},{1,17},{2,18},{3,19},{4,20},{5,21},{6,22},{7,23},{8,24},{9,... | collective-permute-start | bytes 147464 | tf_op jit(solution)/shard_map/ppermute | solution.py:380
  26.4 1.9 %collective-permute-start.4 = (bf16[64,384]{1,0:T(8,128)(2,1)S(1)}, bf16[64,384]{1,0:T(8,128)(2,1)S(1)}, u32[]{:S(2)}, u32[]{:S(2)}) collective-permute-start(bf16[64,384]{1,0:T(8,128)(2,1)S(1)} %add_convert_fusion.1), channel_id=1, source_target_pairs={{0,8},{1,9},{2,10},{3,11},{4,12},{5,13},{6,14},{7,15},{8,0},{9,1},... | collective-permute-start | bytes 147464 | tf_op jit(solution)/shard_map/ppermute | solution.py:380
  28.4 3.6 %all-to-all-start.1 = ((bf16[8,160,128]{2,1,0:T(8,128)(2,1)}), bf16[8,160,128]{2,1,0:T(8,128)(2,1)S(1)}, u32[]{:S(2)}, u32[]{:S(2)}) async-start(bf16[8,160,128]{2,1,0:T(8,128)(2,1)} %bitcast.3), calls=%async_computation.1 | async-start | bytes 655360 | tf_op jit(solution)/shard_map/all_to_all | solution.py:366
  32.0 0.0 collective-permute-done.10.payload
  32.0 0.6 %collective-permute-start.11 = (bf16[128,512]{1,0:T(8,128)(2,1)S(1)}, bf16[128,512]{1,0:T(8,128)(2,1)S(1)}, u32[]{:S(2)}, u32[]{:S(2)}) collective-permute-start(bf16[128,512]{1,0:T(8,128)(2,1)S(1)} %get-tuple-element.34), channel_id=1, source_target_pairs={{0,2},{1,3},{2,0},{3,1},{4,6},{5,7},{6,4},{7,5},{8,10},{9,11},{10,... | collective-permute-start | bytes 393224 | tf_op jit(solution)/shard_map/ppermute | solution.py:375
  32.6 0.0 collective-permute-done.6
  32.6 0.0 collective-permute-done.5
  32.6 3.0 %collective-permute-start.9 = (bf16[64,384]{1,0:T(8,128)(2,1)S(1)}, bf16[64,384]{1,0:T(8,128)(2,1)S(1)}, u32[]{:S(2)}, u32[]{:S(2)}) collective-permute-start(bf16[64,384]{1,0:T(8,128)(2,1)S(1)} %add_convert_fusion), channel_id=1, source_target_pairs={{0,6},{1,7},{2,4},{3,5},{4,2},{5,3},{6,0},{7,1},{8,14},{9,15},{10,... | collective-permute-start | bytes 147464 | tf_op jit(solution)/shard_map/ppermute | solution.py:380
  35.7 0.0 collective-permute-start.8
  35.7 0.6 %collective-permute-start.7 = (bf16[64,384]{1,0:T(8,128)(2,1)S(1)}, bf16[64,384]{1,0:T(8,128)(2,1)S(1)}, u32[]{:S(2)}, u32[]{:S(2)}) collective-permute-start(bf16[64,384]{1,0:T(8,128)(2,1)S(1)} %add_convert_fusion), channel_id=1, source_target_pairs={{0,2},{1,3},{2,0},{3,1},{4,6},{5,7},{6,4},{7,5},{8,10},{9,11},{10,... | collective-permute-start | bytes 147464 | tf_op jit(solution)/shard_map/ppermute | solution.py:380
  36.3 2.0 %collective-permute-done.11.rest_0_ = bf16[128,512]{1,0:T(8,128)(2,1)S(1)} collective-permute-done((bf16[128,512]{1,0:T(8,128)(2,1)S(1)}, bf16[128,512]{1,0:T(8,128)(2,1)S(1)}, u32[]{:S(2)}, u32[]{:S(2)}) %collective-permute-start.11) | collective-permute-done | bytes 131104 | tf_op jit(solution)/shard_map/ppermute | solution.py:375
  38.3 0.8 %finish.1 = bf16[512,128]{1,0:T(8,128)(2,1)} custom-call(f32[128,512]{1,0:T(8,128)S(1)} %get-tuple-element.30.direct, f32[128,512]{1,0:T(8,128)S(1)} %get-tuple-element.33.own, bf16[128,512]{1,0:T(8,128)(2,1)S(1)} %collective-permute-done.11.rest_0_), custom_call_target="tpu_custom_call" | custom-call | tf_op jit(solution)/shard_map/finish/pallas_call | solution.py:401
  39.1 0.8 %collective-permute-done.8 = bf16[64,384]{1,0:T(8,128)(2,1)S(1)} collective-permute-done((bf16[64,384]{1,0:T(8,128)(2,1)S(1)}, bf16[64,384]{1,0:T(8,128)(2,1)S(1)}, u32[]{:S(2)}, u32[]{:S(2)}) %collective-permute-start.8) | collective-permute-done | bytes 49184 | tf_op jit(solution)/shard_map/ppermute | solution.py:380
  39.9 0.1 collective-permute-start.12
  40.0 1.3 %collective-permute-done.12.other = f32[64,384]{1,0:T(8,128)S(1)} collective-permute-done((f32[64,384]{1,0:T(8,128)S(1)}, f32[64,384]{1,0:T(8,128)S(1)}, u32[]{:S(2)}, u32[]{:S(2)}) %collective-permute-start.12) | collective-permute-done | bytes 98336 | tf_op jit(solution)/shard_map/ppermute | solution.py:372
  41.3 0.8 %weights.1 = (f32[128,128]{1,0:T(8,128)}, f32[256,128]{1,0:T(8,128)}) custom-call(f32[64,384]{1,0:T(8,128)S(1)} %add_add_fusion.mine, f32[64,384]{1,0:T(8,128)S(1)} %collective-permute-done.12.other), custom_call_target="tpu_custom_call" | custom-call | tf_op jit(solution)/shard_map/weights/pallas_call | solution.py:414
  42.1 0.0 all-to-all-done.1
  42.1 0.7 %emit.1 = bf16[1280,128]{1,0:T(8,128)(2,1)} custom-call(bf16[1280,128]{1,0:T(8,128)(2,1)S(1)} %bitcast.6), custom_call_target="tpu_custom_call" | custom-call | tf_op jit(solution)/shard_map/emit/pallas_call | solution.py:416
  (7 shorter events, 0.1 us)
Async XLA Ops:
  0.6 8.8 %collective-permute-start = (bf16[512,128]{1,0:T(8,128)(2,1)}, bf16[512,128]{1,0:T(8,128)(2,1)S(1)}, u32[]{:S(2)}, u32[]{:S(2)}) collective-permute-start(bf16[512,128]{1,0:T(8,128)(2,1)} %lat_hbm.3), channel_id=1, source_target_pairs={{0,2},{1,3},{2,0},{3,1},{4,6},{5,7},{6,4},{7,5},{8,10},{9,11},{10,... | collective-permute-start | bytes 393224 | tf_op jit(solution)/shard_map/ppermute | solution.py:375
  3.7 15.8 %all-to-all-start = ((bf16[8,160,128]{2,1,0:T(8,128)(2,1)}), bf16[8,160,128]{2,1,0:T(8,128)(2,1)S(1)}, u32[]{:S(2)}, u32[]{:S(2)}) async-start(bf16[8,160,128]{2,1,0:T(8,128)(2,1)} %bitcast.7), calls=%async_computation | async-start | bytes 655360 | tf_op jit(solution)/shard_map/all_to_all | solution.py:366
  9.5 1.6 %collective-permute-start.1 = (bf16[512,128]{1,0:T(8,128)(2,1)}, bf16[512,128]{1,0:T(8,128)(2,1)S(1)}, u32[]{:S(2)}, u32[]{:S(2)}) collective-permute-start(bf16[512,128]{1,0:T(8,128)(2,1)} %lat_hbm.3), channel_id=1, source_target_pairs={{0,1},{1,0},{2,3},{3,2},{4,5},{5,4},{6,7},{7,6},{8,9},{9,8},{10,11... | collective-permute-start | bytes 393224 | tf_op jit(solution)/shard_map/ppermute | solution.py:372
  9.6 1.5 %collective-permute-start.2 = (bf16[512,128]{1,0:T(8,128)(2,1)S(1)}, bf16[512,128]{1,0:T(8,128)(2,1)S(1)}, u32[]{:S(2)}, u32[]{:S(2)}) collective-permute-start(bf16[512,128]{1,0:T(8,128)(2,1)S(1)} %collective-permute-done.rest_1_), channel_id=1, source_target_pairs={{0,1},{1,0},{2,3},{3,2},{4,5},{5,4},{6,7},{7,6},{8,9},{9,8},{10,11... | collective-permute-start | bytes 393224 | tf_op jit(solution)/shard_map/ppermute | solution.py:372
  22.6 1.3 %collective-permute-start.3 = (bf16[64,384]{1,0:T(8,128)(2,1)S(1)}, bf16[64,384]{1,0:T(8,128)(2,1)S(1)}, u32[]{:S(2)}, u32[]{:S(2)}) collective-permute-start(bf16[64,384]{1,0:T(8,128)(2,1)S(1)} %get-tuple-element.29), channel_id=1, source_target_pairs={{0,1},{1,0},{2,3},{3,2},{4,5},{5,4},{6,7},{7,6},{8,9},{9,8},{10,11... | collective-permute-start | bytes 147464 | tf_op jit(solution)/shard_map/ppermute | solution.py:372
  22.7 9.3 %collective-permute-start.10 = (bf16[64,2048]{1,0:T(8,128)(2,1)S(1)}, bf16[64,2048]{1,0:T(8,128)(2,1)S(1)}, u32[]{:S(2)}, u32[]{:S(2)}) collective-permute-start(bf16[64,2048]{1,0:T(8,128)(2,1)S(1)} %get-tuple-element.31), channel_id=1, source_target_pairs={{0,1},{1,0},{2,3},{3,2},{4,5},{5,4},{6,7},{7,6},{8,9},{9,8},{10,11... | collective-permute-start | bytes 786440 | tf_op jit(solution)/shard_map/ppermute | solution.py:372
  23.9 8.7 %collective-permute-start.6 = (bf16[64,384]{1,0:T(8,128)(2,1)S(1)}, bf16[64,384]{1,0:T(8,128)(2,1)S(1)}, u32[]{:S(2)}, u32[]{:S(2)}) collective-permute-start(bf16[64,384]{1,0:T(8,128)(2,1)S(1)} %add_convert_fusion.1), channel_id=1, source_target_pairs={{0,24},{1,25},{2,26},{3,27},{4,28},{5,29},{6,30},{7,31},{8,16},{9,... | collective-permute-start | bytes 147464 | tf_op jit(solution)/shard_map/ppermute | solution.py:380
  25.1 7.5 %collective-permute-start.5 = (bf16[64,384]{1,0:T(8,128)(2,1)S(1)}, bf16[64,384]{1,0:T(8,128)(2,1)S(1)}, u32[]{:S(2)}, u32[]{:S(2)}) collective-permute-start(bf16[64,384]{1,0:T(8,128)(2,1)S(1)} %add_convert_fusion.1), channel_id=1, source_target_pairs={{0,16},{1,17},{2,18},{3,19},{4,20},{5,21},{6,22},{7,23},{8,24},{9,... | collective-permute-start | bytes 147464 | tf_op jit(solution)/shard_map/ppermute | solution.py:380
  26.4 6.2 %collective-permute-start.4 = (bf16[64,384]{1,0:T(8,128)(2,1)S(1)}, bf16[64,384]{1,0:T(8,128)(2,1)S(1)}, u32[]{:S(2)}, u32[]{:S(2)}) collective-permute-start(bf16[64,384]{1,0:T(8,128)(2,1)S(1)} %add_convert_fusion.1), channel_id=1, source_target_pairs={{0,8},{1,9},{2,10},{3,11},{4,12},{5,13},{6,14},{7,15},{8,0},{9,1},... | collective-permute-start | bytes 147464 | tf_op jit(solution)/shard_map/ppermute | solution.py:380
  28.4 13.7 %all-to-all-start.1 = ((bf16[8,160,128]{2,1,0:T(8,128)(2,1)}), bf16[8,160,128]{2,1,0:T(8,128)(2,1)S(1)}, u32[]{:S(2)}, u32[]{:S(2)}) async-start(bf16[8,160,128]{2,1,0:T(8,128)(2,1)} %bitcast.3), calls=%async_computation.1 | async-start | bytes 655360 | tf_op jit(solution)/shard_map/all_to_all | solution.py:366
  32.0 6.3 %collective-permute-start.11 = (bf16[128,512]{1,0:T(8,128)(2,1)S(1)}, bf16[128,512]{1,0:T(8,128)(2,1)S(1)}, u32[]{:S(2)}, u32[]{:S(2)}) collective-permute-start(bf16[128,512]{1,0:T(8,128)(2,1)S(1)} %get-tuple-element.34), channel_id=1, source_target_pairs={{0,2},{1,3},{2,0},{3,1},{4,6},{5,7},{6,4},{7,5},{8,10},{9,11},{10,... | collective-permute-start | bytes 393224 | tf_op jit(solution)/shard_map/ppermute | solution.py:375
  32.6 6.5 %collective-permute-start.9 = (bf16[64,384]{1,0:T(8,128)(2,1)S(1)}, bf16[64,384]{1,0:T(8,128)(2,1)S(1)}, u32[]{:S(2)}, u32[]{:S(2)}) collective-permute-start(bf16[64,384]{1,0:T(8,128)(2,1)S(1)} %add_convert_fusion), channel_id=1, source_target_pairs={{0,6},{1,7},{2,4},{3,5},{4,2},{5,3},{6,0},{7,1},{8,14},{9,15},{10,... | collective-permute-start | bytes 147464 | tf_op jit(solution)/shard_map/ppermute | solution.py:380
  35.7 4.2 %collective-permute-start.8 = (bf16[64,384]{1,0:T(8,128)(2,1)S(1)}, bf16[64,384]{1,0:T(8,128)(2,1)S(1)}, u32[]{:S(2)}, u32[]{:S(2)}) collective-permute-start(bf16[64,384]{1,0:T(8,128)(2,1)S(1)} %add_convert_fusion), channel_id=1, source_target_pairs={{0,4},{1,5},{2,6},{3,7},{4,0},{5,1},{6,2},{7,3},{8,12},{9,13},{10,... | collective-permute-start | bytes 147464 | tf_op jit(solution)/shard_map/ppermute | solution.py:380
  35.7 4.2 %collective-permute-start.7 = (bf16[64,384]{1,0:T(8,128)(2,1)S(1)}, bf16[64,384]{1,0:T(8,128)(2,1)S(1)}, u32[]{:S(2)}, u32[]{:S(2)}) collective-permute-start(bf16[64,384]{1,0:T(8,128)(2,1)S(1)} %add_convert_fusion), channel_id=1, source_target_pairs={{0,2},{1,3},{2,0},{3,1},{4,6},{5,7},{6,4},{7,5},{8,10},{9,11},{10,... | collective-permute-start | bytes 147464 | tf_op jit(solution)/shard_map/ppermute | solution.py:380
  39.9 1.4 %collective-permute-start.12 = (f32[64,384]{1,0:T(8,128)S(1)}, f32[64,384]{1,0:T(8,128)S(1)}, u32[]{:S(2)}, u32[]{:S(2)}) collective-permute-start(f32[64,384]{1,0:T(8,128)S(1)} %add_add_fusion.mine), channel_id=1, source_target_pairs={{0,1},{1,0},{2,3},{3,2},{4,5},{5,4},{6,7},{7,6},{8,9},{9,8},{10,11... | collective-permute-start | bytes 294920 | tf_op jit(solution)/shard_map/ppermute | solution.py:372

commit v7 on v6

--- a/solution.py
+++ b/solution.py
@@ -320,7 +320,9 @@
 
 
 def weights_call(z):
-    def kernel(mine, other, grad_msg, grad_node):
+    def kernel(mine, other, updated, grad_msg, grad_node, updated_out, sem):
+        copy = pltpu.make_async_copy(updated, updated_out, sem)
+        copy.start()
         first = (lax.axis_index("space") & 1) == 0
         mine, other = mine[...], other[...]
         total = jnp.concatenate(
@@ -328,33 +330,20 @@
         )
         grad_msg[...] = jnp.transpose(total[:, : z.width])
         grad_node[...] = jnp.transpose(total[:, z.width :])
+        copy.wait()
 
     return pl.pallas_call(
         kernel,
         out_shape=(
             jax.ShapeDtypeStruct((z.width, z.width), F32),
             jax.ShapeDtypeStruct((2 * z.width, z.width), F32),
-        ),
-        in_specs=[VMEM] * 2,
+            jax.ShapeDtypeStruct((z.slots, z.width), BF),
+        ),
+        in_specs=[VMEM] * 3,
+        out_specs=[pl.BlockSpec(), pl.BlockSpec(), ANY],
+        scratch_shapes=[pltpu.SemaphoreType.DMA],
         compiler_params=pltpu.CompilerParams(vmem_limit_bytes=8 << 20),
         name="weights",
-    )
-
-
-def emit_call(z):
-    def kernel(rows, out, sem):
-        copy = pltpu.make_async_copy(rows, out, sem)
-        copy.start()
-        copy.wait()
-
-    return pl.pallas_call(
-        kernel,
-        out_shape=jax.ShapeDtypeStruct((z.slots, z.width), BF),
-        in_specs=[VMEM],
-        out_specs=ANY,
-        scratch_shapes=[pltpu.SemaphoreType.DMA],
-        compiler_params=pltpu.CompilerParams(vmem_limit_bytes=8 << 20),
-        name="emit",
     )
 
 
@@ -411,9 +400,7 @@
         grad = got[0] + got[1]
         if span == 2:
             grad = grad + (got[2] + got[3])
-    grad_msg, grad_node = weights_call(z)(grad, to_core(grad))
-    grad_msg, updated = lax.optimization_barrier((grad_msg, updated))
-    updated = emit_call(z)(updated)
+    grad_msg, grad_node, updated = weights_call(z)(grad, to_core(grad), updated)
     return updated, latent_grad, grad_msg, grad_node
 
 

time: 43.2 us -> 43.5 us (level)
  waiting for transfers between devices: 10.4 us -> 10.9 us
    all_to_all x2, waiting for transfers between devices: 4.51 us -> 6.29 us  [swap(): lax.all_to_all(value.reshape(z.groups, z.capacity, z.width), 'group', spl...]
    ppermute x5, waiting for transfers between devices: 3.06 us -> 1.78 us  [to_core(): return lax.ppermute(value, 'space', [(i, i ^ 1) for i in range(z.spaces)])]
    pallas_call x2 -> x1, Pallas kernels: 1.53 us -> 1.41 us  [body(): grad_msg, grad_node, updated = weights_call(z)(grad, to_core(grad), updated)]
  transfers between devices with their start and end apart: 15 -> 15, of which waited for: 6 -> 6; matrix products, arithmetic and copies ran while one was open for 0% -> 0% of each run, Pallas kernels for 13% -> 11%
where the time goes in v7:
time: 43.5 us; the launch traced here: 43.2 us
  starting transfers between devices  22.3 us (51%)
  waiting for transfers between devices  10.9 us (25%)
  Pallas kernels  9.2 us (21%)
  between operations  0.72 us (2%)
    all_to_all x2, starting transfers between devices, swap(): lax.all_to_all(value.reshape(z.groups, z.capacity, z.width), 'group', spl...  9.39 us
    ppermute x6, starting transfers between devices, flip(): lax.ppermute(value, ('group', 'space'), [(i, i ^ mask) for i in range(dev...  8.12 us
    all_to_all x2, waiting for transfers between devices, swap(): lax.all_to_all(value.reshape(z.groups, z.capacity, z.width), 'group', spl...  6.29 us
    pallas_call x1, Pallas kernels, body(): forward_call(z)(params[0], params[1], owners, *params[2:], *lats)  3.89 us
    ppermute x2, starting transfers between devices, along(): lax.ppermute(value, 'space', [(i, (i + 2 * step) % z.spaces) for i in ran...  3.61 us
    pallas_call x1, Pallas kernels, body(): backward_call(z)(*params, returned, slot, factor, agg, pre_slope, *lats)  3.09 us
    ppermute x2, waiting for transfers between devices, along(): lax.ppermute(value, 'space', [(i, (i + 2 * step) % z.spaces) for i in ran...  2.02 us
    ppermute x5, waiting for transfers between devices, to_core(): return lax.ppermute(value, 'space', [(i, i ^ 1) for i in range(z.spaces)])  1.78 us
  transfers between devices with their start and end apart: 15, of which 6 were waited for; matrix products, arithmetic and copies ran while one was open for 0% of the time, Pallas kernels for 11%

profile of v7, /device:TPU:0, one launch (start us, length us, event | category | flops | bytes accessed | tf_op | source)
XLA Modules:
  0.0 43.2 jit_solution(9161862163827134547)
XLA Ops:
  0.6 3.0 %collective-permute-start = (bf16[512,128]{1,0:T(8,128)(2,1)}, bf16[512,128]{1,0:T(8,128)(2,1)S(1)}, u32[]{:S(2)}, u32[]{:S(2)}) collective-permute-start(bf16[512,128]{1,0:T(8,128)(2,1)} %lat_hbm.3), channel_id=1, source_target_pairs={{0,2},{1,3},{2,0},{3,1},{4,6},{5,7},{6,4},{7,5},{8,10},{9,11},{10,... | collective-permute-start | bytes 393224 | tf_op jit(solution)/shard_map/ppermute | solution.py:364
  3.7 5.8 %all-to-all-start = ((bf16[8,160,128]{2,1,0:T(8,128)(2,1)}), bf16[8,160,128]{2,1,0:T(8,128)(2,1)S(1)}, u32[]{:S(2)}, u32[]{:S(2)}) async-start(bf16[8,160,128]{2,1,0:T(8,128)(2,1)} %bitcast.7), calls=%async_computation | async-start | bytes 655360 | tf_op jit(solution)/shard_map/all_to_all | solution.py:355
  9.5 0.0 collective-permute-done.rest_1_
  9.5 0.1 collective-permute-start.1
  9.6 0.5 %collective-permute-start.2 = (bf16[512,128]{1,0:T(8,128)(2,1)S(1)}, bf16[512,128]{1,0:T(8,128)(2,1)S(1)}, u32[]{:S(2)}, u32[]{:S(2)}) collective-permute-start(bf16[512,128]{1,0:T(8,128)(2,1)S(1)} %collective-permute-done.rest_1_), channel_id=1, source_target_pairs={{0,1},{1,0},{2,3},{3,2},{4,5},{5,4},{6,7},{7,6},{8,9},{9,8},{10,11... | collective-permute-start | bytes 393224 | tf_op jit(solution)/shard_map/ppermute | solution.py:361
  10.1 1.0 %collective-permute-done.1.rest_0_ = bf16[512,128]{1,0:T(8,128)(2,1)S(1)} collective-permute-done((bf16[512,128]{1,0:T(8,128)(2,1)}, bf16[512,128]{1,0:T(8,128)(2,1)S(1)}, u32[]{:S(2)}, u32[]{:S(2)}) %collective-permute-start.1) | collective-permute-done | bytes 131104 | tf_op jit(solution)/shard_map/ppermute | solution.py:361
  11.1 0.0 collective-permute-done.2.rest_2_
  11.1 3.9 %forward.1 = (bf16[1280,128]{1,0:T(8,128)(2,1)}, f32[1,512]{1,0:T(1,128)S(1)}, f32[128,512]{1,0:T(8,128)S(1)}, bf16[512,128]{1,0:T(8,128)(2,1)S(1)}, f32[4,128,512]{2,1,0:T(8,128)S(1)}) custom-call(s32[64]{0:T(128)} %recv_hbm.3, s32[64]{0:T(128)} %send_hbm.3, s32[1,512]{1,0:T(1,128)} %bitcast.8, bf16[64,128,128]{2,1,0:T(8,128)(2,1)} %kern_hbm.3, ...), custom_call_target="tpu_custom_call" | custom-call | flops 4400000000 | bytes 1000 | tf_op jit(solution)/shard_map/forward/pallas_call | solution.py:379
  15.0 4.5 %all-to-all-done = bf16[8,160,128]{2,1,0:T(8,128)(2,1)S(1)} async-done(((bf16[8,160,128]{2,1,0:T(8,128)(2,1)}), bf16[8,160,128]{2,1,0:T(8,128)(2,1)S(1)}, u32[]{:S(2)}, u32[]{:S(2)}) %all-to-all-start) | async-done | bytes 327712 | tf_op jit(solution)/shard_map/all_to_all | solution.py:355
  19.5 3.1 %backward.1 = (bf16[64,2048]{1,0:T(8,128)(2,1)S(1)}, f32[2,128,512]{2,1,0:T(8,128)S(1)}, bf16[64,384]{1,0:T(8,128)(2,1)S(1)}, f32[64,384]{1,0:T(8,128)S(1)}, f32[128,512]{1,0:T(8,128)S(1)}) custom-call(s32[64]{0:T(128)} %recv_hbm.3, s32[64]{0:T(128)} %send_hbm.3, bf16[64,128,128]{2,1,0:T(8,128)(2,1)} %kern_hbm.3, bf16[128,128]{1,0:T(8,128)(2,1)} %w_msg_hbm.3, ...), custom_call_target="tpu_custom_call" | custom-call | flops 1000000 | bytes 1000 | tf_op jit(solution)/shard_map/backward/pallas_call | solution.py:383
  22.6 0.1 collective-permute-start.3
  22.7 0.5 %collective-permute-start.10 = (bf16[64,2048]{1,0:T(8,128)(2,1)S(1)}, bf16[64,2048]{1,0:T(8,128)(2,1)S(1)}, u32[]{:S(2)}, u32[]{:S(2)}) collective-permute-start(bf16[64,2048]{1,0:T(8,128)(2,1)S(1)} %get-tuple-element.30), channel_id=1, source_target_pairs={{0,1},{1,0},{2,3},{3,2},{4,5},{5,4},{6,7},{7,6},{8,9},{9,8},{10,11... | collective-permute-start | bytes 786440 | tf_op jit(solution)/shard_map/ppermute | solution.py:361
  23.2 0.7 %collective-permute-done.3 = bf16[64,384]{1,0:T(8,128)(2,1)S(1)} collective-permute-done((bf16[64,384]{1,0:T(8,128)(2,1)S(1)}, bf16[64,384]{1,0:T(8,128)(2,1)S(1)}, u32[]{:S(2)}, u32[]{:S(2)}) %collective-permute-start.3) | collective-permute-done | bytes 49184 | tf_op jit(solution)/shard_map/ppermute | solution.py:361
  23.9 1.2 %collective-permute-start.6 = (bf16[64,384]{1,0:T(8,128)(2,1)S(1)}, bf16[64,384]{1,0:T(8,128)(2,1)S(1)}, u32[]{:S(2)}, u32[]{:S(2)}) collective-permute-start(bf16[64,384]{1,0:T(8,128)(2,1)S(1)} %add_convert_fusion.1), channel_id=1, source_target_pairs={{0,24},{1,25},{2,26},{3,27},{4,28},{5,29},{6,30},{7,31},{8,16},{9,... | collective-permute-start | bytes 147464 | tf_op jit(solution)/shard_map/ppermute | solution.py:369
  25.1 1.3 %collective-permute-start.5 = (bf16[64,384]{1,0:T(8,128)(2,1)S(1)}, bf16[64,384]{1,0:T(8,128)(2,1)S(1)}, u32[]{:S(2)}, u32[]{:S(2)}) collective-permute-start(bf16[64,384]{1,0:T(8,128)(2,1)S(1)} %add_convert_fusion.1), channel_id=1, source_target_pairs={{0,16},{1,17},{2,18},{3,19},{4,20},{5,21},{6,22},{7,23},{8,24},{9,... | collective-permute-start | bytes 147464 | tf_op jit(solution)/shard_map/ppermute | solution.py:369
  26.4 2.0 %collective-permute-start.4 = (bf16[64,384]{1,0:T(8,128)(2,1)S(1)}, bf16[64,384]{1,0:T(8,128)(2,1)S(1)}, u32[]{:S(2)}, u32[]{:S(2)}) collective-permute-start(bf16[64,384]{1,0:T(8,128)(2,1)S(1)} %add_convert_fusion.1), channel_id=1, source_target_pairs={{0,8},{1,9},{2,10},{3,11},{4,12},{5,13},{6,14},{7,15},{8,0},{9,1},... | collective-permute-start | bytes 147464 | tf_op jit(solution)/shard_map/ppermute | solution.py:369
  28.4 3.6 %all-to-all-start.1 = ((bf16[8,160,128]{2,1,0:T(8,128)(2,1)}), bf16[8,160,128]{2,1,0:T(8,128)(2,1)S(1)}, u32[]{:S(2)}, u32[]{:S(2)}) async-start(bf16[8,160,128]{2,1,0:T(8,128)(2,1)} %bitcast.3), calls=%async_computation.1 | async-start | bytes 655360 | tf_op jit(solution)/shard_map/all_to_all | solution.py:355
  32.0 0.0 collective-permute-done.10.payload
  32.0 0.6 %collective-permute-start.11 = (bf16[128,512]{1,0:T(8,128)(2,1)S(1)}, bf16[128,512]{1,0:T(8,128)(2,1)S(1)}, u32[]{:S(2)}, u32[]{:S(2)}) collective-permute-start(bf16[128,512]{1,0:T(8,128)(2,1)S(1)} %get-tuple-element.33), channel_id=1, source_target_pairs={{0,2},{1,3},{2,0},{3,1},{4,6},{5,7},{6,4},{7,5},{8,10},{9,11},{10,... | collective-permute-start | bytes 393224 | tf_op jit(solution)/shard_map/ppermute | solution.py:364
  32.6 0.0 collective-permute-done.6
  32.6 0.0 collective-permute-done.5
  32.6 3.0 %collective-permute-start.9 = (bf16[64,384]{1,0:T(8,128)(2,1)S(1)}, bf16[64,384]{1,0:T(8,128)(2,1)S(1)}, u32[]{:S(2)}, u32[]{:S(2)}) collective-permute-start(bf16[64,384]{1,0:T(8,128)(2,1)S(1)} %add_convert_fusion), channel_id=1, source_target_pairs={{0,6},{1,7},{2,4},{3,5},{4,2},{5,3},{6,0},{7,1},{8,14},{9,15},{10,... | collective-permute-start | bytes 147464 | tf_op jit(solution)/shard_map/ppermute | solution.py:369
  35.7 0.0 collective-permute-start.8
  35.7 0.6 %collective-permute-start.7 = (bf16[64,384]{1,0:T(8,128)(2,1)S(1)}, bf16[64,384]{1,0:T(8,128)(2,1)S(1)}, u32[]{:S(2)}, u32[]{:S(2)}) collective-permute-start(bf16[64,384]{1,0:T(8,128)(2,1)S(1)} %add_convert_fusion), channel_id=1, source_target_pairs={{0,2},{1,3},{2,0},{3,1},{4,6},{5,7},{6,4},{7,5},{8,10},{9,11},{10,... | collective-permute-start | bytes 147464 | tf_op jit(solution)/shard_map/ppermute | solution.py:369
  36.3 2.0 %collective-permute-done.11.rest_0_ = bf16[128,512]{1,0:T(8,128)(2,1)S(1)} collective-permute-done((bf16[128,512]{1,0:T(8,128)(2,1)S(1)}, bf16[128,512]{1,0:T(8,128)(2,1)S(1)}, u32[]{:S(2)}, u32[]{:S(2)}) %collective-permute-start.11) | collective-permute-done | bytes 131104 | tf_op jit(solution)/shard_map/ppermute | solution.py:364
  38.3 0.8 %finish.1 = bf16[512,128]{1,0:T(8,128)(2,1)} custom-call(f32[128,512]{1,0:T(8,128)S(1)} %get-tuple-element.29.direct, f32[128,512]{1,0:T(8,128)S(1)} %get-tuple-element.32.own, bf16[128,512]{1,0:T(8,128)(2,1)S(1)} %collective-permute-done.11.rest_0_), custom_call_target="tpu_custom_call" | custom-call | tf_op jit(solution)/shard_map/finish/pallas_call | solution.py:390
  39.1 0.8 %collective-permute-done.8 = bf16[64,384]{1,0:T(8,128)(2,1)S(1)} collective-permute-done((bf16[64,384]{1,0:T(8,128)(2,1)S(1)}, bf16[64,384]{1,0:T(8,128)(2,1)S(1)}, u32[]{:S(2)}, u32[]{:S(2)}) %collective-permute-start.8) | collective-permute-done | bytes 49184 | tf_op jit(solution)/shard_map/ppermute | solution.py:369
  39.9 0.0 collective-permute-done.7
  39.9 0.1 collective-permute-start.12
  40.0 1.8 %all-to-all-done.1 = bf16[8,160,128]{2,1,0:T(8,128)(2,1)S(1)} async-done(((bf16[8,160,128]{2,1,0:T(8,128)(2,1)}), bf16[8,160,128]{2,1,0:T(8,128)(2,1)S(1)}, u32[]{:S(2)}, u32[]{:S(2)}) %all-to-all-start.1) | async-done | bytes 327712 | tf_op jit(solution)/shard_map/all_to_all | solution.py:355
  41.8 0.0 collective-permute-done.12.other
  41.8 1.4 %weights.1 = (f32[128,128]{1,0:T(8,128)}, f32[256,128]{1,0:T(8,128)}, bf16[1280,128]{1,0:T(8,128)(2,1)}) custom-call(f32[64,384]{1,0:T(8,128)S(1)} %add_add_fusion.mine, f32[64,384]{1,0:T(8,128)S(1)} %collective-permute-done.12.other, bf16[1280,128]{1,0:T(8,128)(2,1)S(1)} %bitcast.6), custom_call_target="tpu_custom_call" | custom-call | tf_op jit(solution)/shard_map/weights/pallas_call | solution.py:403
  (6 shorter events, 0.1 us)
Async XLA Ops:
  0.6 8.8 %collective-permute-start = (bf16[512,128]{1,0:T(8,128)(2,1)}, bf16[512,128]{1,0:T(8,128)(2,1)S(1)}, u32[]{:S(2)}, u32[]{:S(2)}) collective-permute-start(bf16[512,128]{1,0:T(8,128)(2,1)} %lat_hbm.3), channel_id=1, source_target_pairs={{0,2},{1,3},{2,0},{3,1},{4,6},{5,7},{6,4},{7,5},{8,10},{9,11},{10,... | collective-permute-start | bytes 393224 | tf_op jit(solution)/shard_map/ppermute | solution.py:364
  3.7 15.8 %all-to-all-start = ((bf16[8,160,128]{2,1,0:T(8,128)(2,1)}), bf16[8,160,128]{2,1,0:T(8,128)(2,1)S(1)}, u32[]{:S(2)}, u32[]{:S(2)}) async-start(bf16[8,160,128]{2,1,0:T(8,128)(2,1)} %bitcast.7), calls=%async_computation | async-start | bytes 655360 | tf_op jit(solution)/shard_map/all_to_all | solution.py:355
  9.5 1.6 %collective-permute-start.1 = (bf16[512,128]{1,0:T(8,128)(2,1)}, bf16[512,128]{1,0:T(8,128)(2,1)S(1)}, u32[]{:S(2)}, u32[]{:S(2)}) collective-permute-start(bf16[512,128]{1,0:T(8,128)(2,1)} %lat_hbm.3), channel_id=1, source_target_pairs={{0,1},{1,0},{2,3},{3,2},{4,5},{5,4},{6,7},{7,6},{8,9},{9,8},{10,11... | collective-permute-start | bytes 393224 | tf_op jit(solution)/shard_map/ppermute | solution.py:361
  9.6 1.5 %collective-permute-start.2 = (bf16[512,128]{1,0:T(8,128)(2,1)S(1)}, bf16[512,128]{1,0:T(8,128)(2,1)S(1)}, u32[]{:S(2)}, u32[]{:S(2)}) collective-permute-start(bf16[512,128]{1,0:T(8,128)(2,1)S(1)} %collective-permute-done.rest_1_), channel_id=1, source_target_pairs={{0,1},{1,0},{2,3},{3,2},{4,5},{5,4},{6,7},{7,6},{8,9},{9,8},{10,11... | collective-permute-start | bytes 393224 | tf_op jit(solution)/shard_map/ppermute | solution.py:361
  22.6 1.3 %collective-permute-start.3 = (bf16[64,384]{1,0:T(8,128)(2,1)S(1)}, bf16[64,384]{1,0:T(8,128)(2,1)S(1)}, u32[]{:S(2)}, u32[]{:S(2)}) collective-permute-start(bf16[64,384]{1,0:T(8,128)(2,1)S(1)} %get-tuple-element.28), channel_id=1, source_target_pairs={{0,1},{1,0},{2,3},{3,2},{4,5},{5,4},{6,7},{7,6},{8,9},{9,8},{10,11... | collective-permute-start | bytes 147464 | tf_op jit(solution)/shard_map/ppermute | solution.py:361
  22.7 9.3 %collective-permute-start.10 = (bf16[64,2048]{1,0:T(8,128)(2,1)S(1)}, bf16[64,2048]{1,0:T(8,128)(2,1)S(1)}, u32[]{:S(2)}, u32[]{:S(2)}) collective-permute-start(bf16[64,2048]{1,0:T(8,128)(2,1)S(1)} %get-tuple-element.30), channel_id=1, source_target_pairs={{0,1},{1,0},{2,3},{3,2},{4,5},{5,4},{6,7},{7,6},{8,9},{9,8},{10,11... | collective-permute-start | bytes 786440 | tf_op jit(solution)/shard_map/ppermute | solution.py:361
  23.9 8.7 %collective-permute-start.6 = (bf16[64,384]{1,0:T(8,128)(2,1)S(1)}, bf16[64,384]{1,0:T(8,128)(2,1)S(1)}, u32[]{:S(2)}, u32[]{:S(2)}) collective-permute-start(bf16[64,384]{1,0:T(8,128)(2,1)S(1)} %add_convert_fusion.1), channel_id=1, source_target_pairs={{0,24},{1,25},{2,26},{3,27},{4,28},{5,29},{6,30},{7,31},{8,16},{9,... | collective-permute-start | bytes 147464 | tf_op jit(solution)/shard_map/ppermute | solution.py:369
  25.1 7.5 %collective-permute-start.5 = (bf16[64,384]{1,0:T(8,128)(2,1)S(1)}, bf16[64,384]{1,0:T(8,128)(2,1)S(1)}, u32[]{:S(2)}, u32[]{:S(2)}) collective-permute-start(bf16[64,384]{1,0:T(8,128)(2,1)S(1)} %add_convert_fusion.1), channel_id=1, source_target_pairs={{0,16},{1,17},{2,18},{3,19},{4,20},{5,21},{6,22},{7,23},{8,24},{9,... | collective-permute-start | bytes 147464 | tf_op jit(solution)/shard_map/ppermute | solution.py:369
  26.4 6.2 %collective-permute-start.4 = (bf16[64,384]{1,0:T(8,128)(2,1)S(1)}, bf16[64,384]{1,0:T(8,128)(2,1)S(1)}, u32[]{:S(2)}, u32[]{:S(2)}) collective-permute-start(bf16[64,384]{1,0:T(8,128)(2,1)S(1)} %add_convert_fusion.1), channel_id=1, source_target_pairs={{0,8},{1,9},{2,10},{3,11},{4,12},{5,13},{6,14},{7,15},{8,0},{9,1},... | collective-permute-start | bytes 147464 | tf_op jit(solution)/shard_map/ppermute | solution.py:369
  28.4 13.4 %all-to-all-start.1 = ((bf16[8,160,128]{2,1,0:T(8,128)(2,1)}), bf16[8,160,128]{2,1,0:T(8,128)(2,1)S(1)}, u32[]{:S(2)}, u32[]{:S(2)}) async-start(bf16[8,160,128]{2,1,0:T(8,128)(2,1)} %bitcast.3), calls=%async_computation.1 | async-start | bytes 655360 | tf_op jit(solution)/shard_map/all_to_all | solution.py:355
  32.0 6.3 %collective-permute-start.11 = (bf16[128,512]{1,0:T(8,128)(2,1)S(1)}, bf16[128,512]{1,0:T(8,128)(2,1)S(1)}, u32[]{:S(2)}, u32[]{:S(2)}) collective-permute-start(bf16[128,512]{1,0:T(8,128)(2,1)S(1)} %get-tuple-element.33), channel_id=1, source_target_pairs={{0,2},{1,3},{2,0},{3,1},{4,6},{5,7},{6,4},{7,5},{8,10},{9,11},{10,... | collective-permute-start | bytes 393224 | tf_op jit(solution)/shard_map/ppermute | solution.py:364
  32.6 6.5 %collective-permute-start.9 = (bf16[64,384]{1,0:T(8,128)(2,1)S(1)}, bf16[64,384]{1,0:T(8,128)(2,1)S(1)}, u32[]{:S(2)}, u32[]{:S(2)}) collective-permute-start(bf16[64,384]{1,0:T(8,128)(2,1)S(1)} %add_convert_fusion), channel_id=1, source_target_pairs={{0,6},{1,7},{2,4},{3,5},{4,2},{5,3},{6,0},{7,1},{8,14},{9,15},{10,... | collective-permute-start | bytes 147464 | tf_op jit(solution)/shard_map/ppermute | solution.py:369
  35.7 4.2 %collective-permute-start.8 = (bf16[64,384]{1,0:T(8,128)(2,1)S(1)}, bf16[64,384]{1,0:T(8,128)(2,1)S(1)}, u32[]{:S(2)}, u32[]{:S(2)}) collective-permute-start(bf16[64,384]{1,0:T(8,128)(2,1)S(1)} %add_convert_fusion), channel_id=1, source_target_pairs={{0,4},{1,5},{2,6},{3,7},{4,0},{5,1},{6,2},{7,3},{8,12},{9,13},{10,... | collective-permute-start | bytes 147464 | tf_op jit(solution)/shard_map/ppermute | solution.py:369
  35.7 4.2 %collective-permute-start.7 = (bf16[64,384]{1,0:T(8,128)(2,1)S(1)}, bf16[64,384]{1,0:T(8,128)(2,1)S(1)}, u32[]{:S(2)}, u32[]{:S(2)}) collective-permute-start(bf16[64,384]{1,0:T(8,128)(2,1)S(1)} %add_convert_fusion), channel_id=1, source_target_pairs={{0,2},{1,3},{2,0},{3,1},{4,6},{5,7},{6,4},{7,5},{8,10},{9,11},{10,... | collective-permute-start | bytes 147464 | tf_op jit(solution)/shard_map/ppermute | solution.py:369
  39.9 1.9 %collective-permute-start.12 = (f32[64,384]{1,0:T(8,128)S(1)}, f32[64,384]{1,0:T(8,128)S(1)}, u32[]{:S(2)}, u32[]{:S(2)}) collective-permute-start(f32[64,384]{1,0:T(8,128)S(1)} %add_add_fusion.mine), channel_id=1, source_target_pairs={{0,1},{1,0},{2,3},{3,2},{4,5},{5,4},{6,7},{7,6},{8,9},{9,8},{10,11... | collective-permute-start | bytes 294920 | tf_op jit(solution)/shard_map/ppermute | solution.py:361
